TPU v7x, 32 devices: a whole 2x2x4 slice. The times are simulated.
32 devices in a mesh: rows: 16 (over z, x, core), seq: 2 (over y).
Axes of the slice: x: 2, y: 2, z: 4, core: 2. Of those that a mesh axis runs over, the one named last changes fastest.
Arguments:
- encoder_input: bfloat16 [32, 512, 768], P('rows', 'seq'), may hold values from -23 to 23
- decoder_input: bfloat16 [32, 128, 768], P('rows', 'seq'), may hold values from -23 to 23
- segment_lengths: int32 [32, 8], P('rows'), may hold values from 0 to 512, as said below
- target_lengths: int32 [32], P('rows'), may hold values from 32 to 128, as said below
- bucket_table: int32 [1023], replicated, may hold values from 0 to 31
- encoder_attention_gain: bfloat16 [768], P(('rows', 'seq')), may hold values from 0.5 to 1.5
- encoder_query: bfloat16 [768, 768], P(('rows', 'seq')), may hold values from -0.109375 to 0.109375
- encoder_key: bfloat16 [768, 768], P(('rows', 'seq')), may hold values from -0.109375 to 0.109375
- encoder_value: bfloat16 [768, 768], P(('rows', 'seq')), may hold values from -0.21875 to 0.21875
- encoder_outward: bfloat16 [768, 768], P(('rows', 'seq')), may hold values from -0.875 to 0.875
- encoder_position_bias: float32 [32, 12], replicated, may hold values from -4 to 4
- encoder_feedforward_gain: bfloat16 [768], P(('rows', 'seq')), may hold values from 0.5 to 1.5
- encoder_widen: bfloat16 [768, 3072], P(('rows', 'seq')), may hold values from -0.21875 to 0.21875
- encoder_narrow: bfloat16 [3072, 768], P(('rows', 'seq')), may hold values from -0.15625 to 0.15625
- encoder_final_gain: bfloat16 [768], P(('rows', 'seq')), may hold values from 0.5 to 1.5
- decoder_self_gain: bfloat16 [768], P(('rows', 'seq')), may hold values from 0.5 to 1.5
- decoder_query: bfloat16 [768, 768], P(('rows', 'seq')), may hold values from -0.109375 to 0.109375
- decoder_key: bfloat16 [768, 768], P(('rows', 'seq')), may hold values from -0.109375 to 0.109375
- decoder_value: bfloat16 [768, 768], P(('rows', 'seq')), may hold values from -0.21875 to 0.21875
- decoder_outward: bfloat16 [768, 768], P(('rows', 'seq')), may hold values from -0.875 to 0.875
- decoder_position_bias: float32 [32, 12], replicated, may hold values from -4 to 4
- decoder_cross_gain: bfloat16 [768], P(('rows', 'seq')), may hold values from 0.5 to 1.5
- cross_query: bfloat16 [768, 768], P(('rows', 'seq')), may hold values from -0.109375 to 0.109375
- cross_key: bfloat16 [768, 768], P(('rows', 'seq')), may hold values from -0.109375 to 0.109375
- cross_value: bfloat16 [768, 768], P(('rows', 'seq')), may hold values from -0.21875 to 0.21875
- cross_outward: bfloat16 [768, 768], P(('rows', 'seq')), may hold values from -0.875 to 0.875
- decoder_feedforward_gain: bfloat16 [768], P(('rows', 'seq')), may hold values from 0.5 to 1.5
- decoder_widen: bfloat16 [768, 3072], P(('rows', 'seq')), may hold values from -0.21875 to 0.21875
- decoder_narrow: bfloat16 [3072, 768], P(('rows', 'seq')), may hold values from -0.15625 to 0.15625
- encoder_cotangent: bfloat16 [32, 512, 768], P('rows', 'seq'), may hold values from -6 to 6
- decoder_cotangent: bfloat16 [32, 128, 768], P('rows', 'seq'), may hold values from -6 to 6
Outputs:
- encoder_output: float32 [32, 512, 768], P('rows', 'seq')
- decoder_output: float32 [32, 128, 768], P('rows', 'seq')
- encoder_input_grad: float32 [32, 512, 768], P('rows', 'seq')
- decoder_input_grad: float32 [32, 128, 768], P('rows', 'seq')
- encoder_attention_gain_grad: float32 [768], P(('rows', 'seq'))
- encoder_query_grad: float32 [768, 768], P(('rows', 'seq'))
- encoder_key_grad: float32 [768, 768], P(('rows', 'seq'))
- encoder_value_grad: float32 [768, 768], P(('rows', 'seq'))
- encoder_outward_grad: float32 [768, 768], P(('rows', 'seq'))
- encoder_position_bias_grad: float32 [32, 12], replicated
- encoder_feedforward_gain_grad: float32 [768], P(('rows', 'seq'))
- encoder_widen_grad: float32 [768, 3072], P(('rows', 'seq'))
- encoder_narrow_grad: float32 [3072, 768], P(('rows', 'seq'))
- encoder_final_gain_grad: float32 [768], P(('rows', 'seq'))
- decoder_self_gain_grad: float32 [768], P(('rows', 'seq'))
- decoder_query_grad: float32 [768, 768], P(('rows', 'seq'))
- decoder_key_grad: float32 [768, 768], P(('rows', 'seq'))
- decoder_value_grad: float32 [768, 768], P(('rows', 'seq'))
- decoder_outward_grad: float32 [768, 768], P(('rows', 'seq'))
- decoder_position_bias_grad: float32 [32, 12], replicated
- decoder_cross_gain_grad: float32 [768], P(('rows', 'seq'))
- cross_query_grad: float32 [768, 768], P(('rows', 'seq'))
- cross_key_grad: float32 [768, 768], P(('rows', 'seq'))
- cross_value_grad: float32 [768, 768], P(('rows', 'seq'))
- cross_outward_grad: float32 [768, 768], P(('rows', 'seq'))
- decoder_feedforward_gain_grad: float32 [768], P(('rows', 'seq'))
- decoder_widen_grad: float32 [768, 3072], P(('rows', 'seq'))
- decoder_narrow_grad: float32 [3072, 768], P(('rows', 'seq'))
- norm_statistics: float32 [4], replicated
Inputs may be any that keep to these rules, and one draw needn't show every extreme that they name: `segment_lengths`: in each row either entry 0 alone is nonzero, above 256, or all 8 entries lie in 16 to 64; among the 2 rows of each index of rows one is a single input of 512 tokens. `target_lengths`: among the 2 rows of each index of rows one has length 128.
All inputs are finite; a program needn't handle non-finite values.
Results may differ from a plain program's by a relative error of at most 0.025.
The roundings to bfloat16 on the way count: a program that leaves them out, or rounds other values in their place, can miss the bound.
Values may be sent and summed in bfloat16 or wider, within the bound.
A program may use at most 384 MiB of HBM per device.

v0:
```python
import jax
import jax.numpy as jnp
from jax import lax
from jax.sharding import PartitionSpec as P

HEADS = 12
BUCKETS = 32


EPSILON = 1e-06
NEGATIVE = -1e30
HIGHEST_PRECISION = lax.Precision.HIGHEST


def as_sent(shard):

    def short(part):
        return part.astype(jnp.bfloat16) if part.dtype == jnp.float32 else part

    return jax.tree.map(short, shard)


def rms_scale(values, gain_vec):
    return (
        values * lax.rsqrt(jnp.mean(values * values, axis=-1, keepdims=True) + EPSILON) * gain_vec
    )


def gelu_float(values):
    return jax.nn.gelu(values, approximate=True)


def position_bias(table_in, buckets, query_pos, key_pos, span):
    distance_index = key_pos[None, :] - query_pos[:, None] + (span - 1)
    bucket_index = jnp.take(buckets, distance_index, axis=0)
    bucket_ids = jnp.arange(BUCKETS, dtype=jnp.int32)
    selector = (bucket_index[:, :, None] == bucket_ids[None, None, :]).astype(jnp.float32)
    return jnp.einsum("qkb,bh->hqk", selector, table_in, precision=HIGHEST_PRECISION)


def segment_number(segment_ends, positions):
    return jnp.sum((segment_ends[:, None, :] <= positions[None, :, None]).astype(jnp.int32), axis=2)


def project(normed, weight):
    return jnp.einsum("rsd,de->rse", normed, weight, preferred_element_type=jnp.float32)


def project_back(grads, weight):
    return jnp.einsum("rse,de->rsd", grads, weight, preferred_element_type=jnp.float32)


def weight_grad(inputs, grads):
    return jnp.einsum("rsd,rse->de", inputs, grads, preferred_element_type=jnp.float32)


def split_heads(values):
    return values.reshape(values.shape[0], HEADS, values.shape[1] // HEADS)


def scores_of(queries, keys_all, rel_bias, key_mask):
    scores = jnp.einsum("qhe,khe->hqk", queries, keys_all, preferred_element_type=jnp.float32)
    if rel_bias is not None:
        scores = scores + rel_bias
    return jnp.where(key_mask[None], scores, NEGATIVE)


def core_forward(queries, keys_all, values_all, rel_bias, key_mask):
    scores = scores_of(queries, keys_all, rel_bias, key_mask)
    row_maximum = jnp.max(scores, axis=-1, keepdims=True)
    exponent = jnp.exp(scores - row_maximum)
    totals = jnp.sum(exponent, axis=-1, keepdims=True)
    softmax_probs = (exponent / totals).astype(jnp.bfloat16)
    attended = jnp.einsum(
        "hqk,khe->qhe", softmax_probs, values_all, preferred_element_type=jnp.float32
    )
    return (attended.astype(jnp.bfloat16), (row_maximum + jnp.log(totals))[:, :, 0])


def core_backward(queries, keys_all, values_all, rel_bias, key_mask, log_total, attended_grad):
    scores = scores_of(queries, keys_all, rel_bias, key_mask)
    softmax_probs = jnp.exp(scores - log_total[:, :, None])
    probs_low = softmax_probs.astype(jnp.bfloat16)
    value_grad = jnp.einsum(
        "hqk,qhe->khe", probs_low, attended_grad, preferred_element_type=jnp.float32
    )
    probs_grad = jnp.einsum(
        "qhe,khe->hqk", attended_grad, values_all, preferred_element_type=jnp.float32
    )
    score_grad = softmax_probs * (
        probs_grad - jnp.sum(probs_grad * softmax_probs, axis=-1, keepdims=True)
    )
    score_low = score_grad.astype(jnp.bfloat16)
    query_grad = jnp.einsum("hqk,khe->qhe", score_low, keys_all, preferred_element_type=jnp.float32)
    key_grad = jnp.einsum("hqk,qhe->khe", score_low, queries, preferred_element_type=jnp.float32)
    return (query_grad, key_grad, value_grad, score_low)


def attend_rows(queries, keys_all, values_all, rel_bias, key_masks):
    rows_here, query_len, feature_count = queries.shape

    def one_row(row_items):
        return core_forward(
            split_heads(row_items[0]),
            split_heads(row_items[1]),
            split_heads(row_items[2]),
            rel_bias,
            row_items[3],
        )

    attended, log_total = lax.map(one_row, (queries, keys_all, values_all, key_masks))
    return (attended.reshape(rows_here, query_len, feature_count), log_total)


def attend_rows_back(queries, keys_all, values_all, rel_bias, key_masks, log_total, attended_low):
    rows_here, query_len, feature_count = queries.shape
    key_len = keys_all.shape[1]

    def one_row(bias_total, row_items):
        query_grad, key_grad, value_grad, score_low = core_backward(
            split_heads(row_items[0]),
            split_heads(row_items[1]),
            split_heads(row_items[2]),
            rel_bias,
            row_items[3],
            row_items[4],
            split_heads(row_items[5]),
        )
        if rel_bias is not None:
            bias_total = bias_total + score_low.astype(jnp.float32)
        return (
            bias_total,
            (
                query_grad.reshape(query_len, feature_count),
                key_grad.reshape(key_len, feature_count),
                value_grad.reshape(key_len, feature_count),
            ),
        )

    if rel_bias is not None:
        bias_begin = jnp.zeros((HEADS, query_len, key_len), jnp.float32)
    else:
        bias_begin = jnp.zeros((), jnp.float32)
    bias_total, grads = lax.scan(
        one_row, bias_begin, (queries, keys_all, values_all, key_masks, log_total, attended_low)
    )
    return (grads[0], grads[1], grads[2], bias_total)


def attention_back_local(
    queries, keys_all, values_all, rel_bias, key_masks, log_total, attended, outward, upstream
):
    branch_low = upstream.astype(jnp.bfloat16)
    outward_grad = weight_grad(attended, branch_low)
    attended_low = project_back(branch_low, outward).astype(jnp.bfloat16)
    query_grad, key_grad, value_grad, bias_total = attend_rows_back(
        queries, keys_all, values_all, rel_bias, key_masks, log_total, attended_low
    )
    return (outward_grad, query_grad.astype(jnp.bfloat16), key_grad, value_grad, bias_total)


def norm_back(values, gain_vec, upstream):
    unused_value, pullback = jax.vjp(rms_scale, values, gain_vec)
    return pullback(upstream)


def feedforward_back(normed, pre_values, active, widen, narrow, upstream):
    branch_low = upstream.astype(jnp.bfloat16)
    narrow_grad = weight_grad(active, branch_low)
    active_grad = project_back(branch_low, narrow)
    unused_value, gelu_pull = jax.vjp(gelu_float, pre_values)
    pre_low = gelu_pull(active_grad)[0].astype(jnp.bfloat16)
    widen_grad = weight_grad(normed, pre_low)
    normed_grad = project_back(pre_low, widen)
    return (normed_grad, widen_grad, narrow_grad)


def gather_weights(shards):
    return jax.tree.map(
        lambda part, own: part.astype(own.dtype),
        lax.all_gather(as_sent(shards), ("rows", "seq"), axis=0, tiled=True),
        shards,
    )


def gather_again(shards):
    return jax.tree.map(
        lambda part, own: part.astype(own.dtype),
        lax.all_gather(as_sent(shards), ("rows", "seq"), axis=0, tiled=True),
        shards,
    )


def reduce_weights(grads):
    return lax.psum_scatter(grads, ("rows", "seq"), scatter_dimension=0, tiled=True)


def body(
    encoder_input,
    decoder_input,
    segment_lengths,
    target_lengths,
    bucket_table,
    encoder_attention_gain,
    encoder_query,
    encoder_key,
    encoder_value,
    encoder_outward,
    encoder_position_bias,
    encoder_feedforward_gain,
    encoder_widen,
    encoder_narrow,
    encoder_final_gain,
    decoder_self_gain,
    decoder_query,
    decoder_key,
    decoder_value,
    decoder_outward,
    decoder_position_bias,
    decoder_cross_gain,
    cross_query,
    cross_key,
    cross_value,
    cross_outward,
    decoder_feedforward_gain,
    decoder_widen,
    decoder_narrow,
    encoder_cotangent,
    decoder_cotangent,
):
    seq_index = lax.axis_index("seq")
    seq_count = lax.axis_size("seq")
    rows_here, encoder_local, feature_count = encoder_input.shape
    decoder_local = decoder_input.shape[1]
    encoder_span = encoder_local * seq_count
    encoder_query_pos = seq_index * encoder_local + jnp.arange(encoder_local, dtype=jnp.int32)
    encoder_key_pos = jnp.arange(encoder_span, dtype=jnp.int32)
    target_query_pos = seq_index * decoder_local + jnp.arange(decoder_local, dtype=jnp.int32)
    target_key_pos = jnp.arange(decoder_local * seq_count, dtype=jnp.int32)
    segment_ends = jnp.cumsum(segment_lengths, axis=1)
    encoder_query_segment = segment_number(segment_ends, encoder_query_pos)
    encoder_key_segment = segment_number(segment_ends, encoder_key_pos)
    encoder_masks = encoder_query_segment[:, :, None] == encoder_key_segment[:, None, :]
    encoder_valid_query = encoder_query_pos[None, :] < segment_ends[:, -1:]
    encoder_valid_key = encoder_key_pos[None, :] < segment_ends[:, -1:]
    target_valid_query = target_query_pos[None, :] < target_lengths[:, None]
    target_valid_key = target_key_pos[None, :] < target_lengths[:, None]
    causal = target_key_pos[None, :] <= target_query_pos[:, None]
    target_masks = causal[None] & (target_valid_query[:, :, None] == target_valid_key[:, None, :])
    cross_masks = jnp.logical_not(target_valid_query)[:, :, None] | encoder_valid_key[:, None, :]
    encoder_attention_shards = (
        encoder_attention_gain,
        encoder_query,
        encoder_key,
        encoder_value,
        encoder_outward,
    )
    encoder_attention_full = gather_weights(encoder_attention_shards)
    encoder_residual = encoder_input.astype(jnp.float32)
    first_gain = encoder_attention_full[0].astype(jnp.float32)
    first_normed = rms_scale(encoder_residual, first_gain).astype(jnp.bfloat16)
    encoder_queries = project(first_normed, encoder_attention_full[1]).astype(jnp.bfloat16)
    encoder_keys_own = project(first_normed, encoder_attention_full[2]).astype(jnp.bfloat16)
    encoder_values_own = project(first_normed, encoder_attention_full[3]).astype(jnp.bfloat16)
    encoder_keys, encoder_values = (
        lax.all_gather(encoder_keys_own, "seq", axis=1, tiled=True),
        lax.all_gather(encoder_values_own, "seq", axis=1, tiled=True),
    )
    encoder_bias, encoder_bias_back = jax.vjp(
        lambda table_in: position_bias(
            table_in, bucket_table, encoder_query_pos, encoder_key_pos, encoder_span
        ),
        encoder_position_bias,
    )
    encoder_attended, encoder_log_total = attend_rows(
        encoder_queries, encoder_keys, encoder_values, encoder_bias, encoder_masks
    )
    encoder_middle = encoder_residual + project(encoder_attended, encoder_attention_full[4])
    encoder_feedforward_shards = (
        encoder_feedforward_gain,
        encoder_widen,
        encoder_narrow,
        encoder_final_gain,
    )
    encoder_feedforward_full = gather_weights(encoder_feedforward_shards)
    second_gain = encoder_feedforward_full[0].astype(jnp.float32)
    second_normed = rms_scale(encoder_middle, second_gain).astype(jnp.bfloat16)
    encoder_pre = project(second_normed, encoder_feedforward_full[1])
    encoder_active = gelu_float(encoder_pre).astype(jnp.bfloat16)
    encoder_branch = project(encoder_active, encoder_feedforward_full[2])
    encoder_output = encoder_middle + encoder_branch
    final_gain = encoder_feedforward_full[3].astype(jnp.float32)
    memory_normed = rms_scale(encoder_output, final_gain).astype(jnp.bfloat16)
    decoder_attention_shards = (
        decoder_self_gain,
        decoder_query,
        decoder_key,
        decoder_value,
        decoder_outward,
        decoder_cross_gain,
        cross_query,
        cross_key,
        cross_value,
        cross_outward,
    )
    decoder_attention_full = gather_weights(decoder_attention_shards)
    target_residual = decoder_input.astype(jnp.float32)
    self_gain = decoder_attention_full[0].astype(jnp.float32)
    self_normed = rms_scale(target_residual, self_gain).astype(jnp.bfloat16)
    self_queries = project(self_normed, decoder_attention_full[1]).astype(jnp.bfloat16)
    self_keys_own = project(self_normed, decoder_attention_full[2]).astype(jnp.bfloat16)
    self_values_own = project(self_normed, decoder_attention_full[3]).astype(jnp.bfloat16)
    self_keys, self_values = (
        lax.all_gather(self_keys_own, "seq", axis=1, tiled=True),
        lax.all_gather(self_values_own, "seq", axis=1, tiled=True),
    )
    target_bias, target_bias_back = jax.vjp(
        lambda table_in: position_bias(
            table_in, bucket_table, target_query_pos, target_key_pos, encoder_span
        ),
        decoder_position_bias,
    )
    self_attended, self_log_total = attend_rows(
        self_queries, self_keys, self_values, target_bias, target_masks
    )
    target_middle = target_residual + project(self_attended, decoder_attention_full[4])
    cross_gain = decoder_attention_full[5].astype(jnp.float32)
    cross_normed = rms_scale(target_middle, cross_gain).astype(jnp.bfloat16)
    cross_queries = project(cross_normed, decoder_attention_full[6]).astype(jnp.bfloat16)
    cross_keys_own = project(memory_normed, decoder_attention_full[7]).astype(jnp.bfloat16)
    cross_values_own = project(memory_normed, decoder_attention_full[8]).astype(jnp.bfloat16)
    cross_keys_all, cross_values_all = (
        lax.all_gather(cross_keys_own, "seq", axis=1, tiled=True),
        lax.all_gather(cross_values_own, "seq", axis=1, tiled=True),
    )
    cross_attended, cross_log_total = attend_rows(
        cross_queries, cross_keys_all, cross_values_all, None, cross_masks
    )
    target_crossed = target_middle + project(cross_attended, decoder_attention_full[9])
    decoder_feedforward_shards = (decoder_feedforward_gain, decoder_widen, decoder_narrow)
    decoder_feedforward_full = gather_weights(decoder_feedforward_shards)
    third_gain = decoder_feedforward_full[0].astype(jnp.float32)
    third_normed = rms_scale(target_crossed, third_gain).astype(jnp.bfloat16)
    decoder_pre = project(third_normed, decoder_feedforward_full[1])
    decoder_active = gelu_float(decoder_pre).astype(jnp.bfloat16)
    decoder_branch = project(decoder_active, decoder_feedforward_full[2])
    decoder_output = target_crossed + decoder_branch
    decoder_feedforward_back = gather_again(decoder_feedforward_shards)
    output_grad = decoder_cotangent.astype(jnp.float32)
    normed_grad, decoder_widen_grad, decoder_narrow_grad = feedforward_back(
        third_normed,
        decoder_pre,
        decoder_active,
        decoder_feedforward_back[1],
        decoder_feedforward_back[2],
        output_grad,
    )
    crossed_part, third_gain_grad = norm_back(target_crossed, third_gain, normed_grad)
    crossed_grad = output_grad + crossed_part
    decoder_feedforward_grads = reduce_weights(
        (third_gain_grad, decoder_widen_grad, decoder_narrow_grad)
    )
    decoder_attention_back = gather_again(decoder_attention_shards)
    cross_outward_grad, cross_query_low, cross_key_full, cross_value_full, unused_total = (
        attention_back_local(
            cross_queries,
            cross_keys_all,
            cross_values_all,
            None,
            cross_masks,
            cross_log_total,
            cross_attended,
            decoder_attention_back[9],
            crossed_grad,
        )
    )
    cross_key_own, cross_value_own = (
        lax.psum_scatter(
            cross_key_full.astype(jnp.bfloat16), "seq", scatter_dimension=1, tiled=True
        ).astype(jnp.float32),
        lax.psum_scatter(
            cross_value_full.astype(jnp.bfloat16), "seq", scatter_dimension=1, tiled=True
        ).astype(jnp.float32),
    )
    cross_key_low = cross_key_own.astype(jnp.bfloat16)
    cross_value_low = cross_value_own.astype(jnp.bfloat16)
    cross_query_grad = weight_grad(cross_normed, cross_query_low)
    cross_key_grad = weight_grad(memory_normed, cross_key_low)
    cross_value_grad = weight_grad(memory_normed, cross_value_low)
    cross_normed_grad = project_back(cross_query_low, decoder_attention_back[6])
    memory_grad = project_back(cross_key_low, decoder_attention_back[7]) + project_back(
        cross_value_low, decoder_attention_back[8]
    )
    middle_part, cross_gain_grad = norm_back(target_middle, cross_gain, cross_normed_grad)
    middle_grad = crossed_grad + middle_part
    self_outward_grad, self_query_low, self_key_full, self_value_full, target_bias_total = (
        attention_back_local(
            self_queries,
            self_keys,
            self_values,
            target_bias,
            target_masks,
            self_log_total,
            self_attended,
            decoder_attention_back[4],
            middle_grad,
        )
    )
    self_key_own, self_value_own = (
        lax.psum_scatter(
            self_key_full.astype(jnp.bfloat16), "seq", scatter_dimension=1, tiled=True
        ).astype(jnp.float32),
        lax.psum_scatter(
            self_value_full.astype(jnp.bfloat16), "seq", scatter_dimension=1, tiled=True
        ).astype(jnp.float32),
    )
    self_key_low = self_key_own.astype(jnp.bfloat16)
    self_value_low = self_value_own.astype(jnp.bfloat16)
    self_query_grad = weight_grad(self_normed, self_query_low)
    self_key_grad = weight_grad(self_normed, self_key_low)
    self_value_grad = weight_grad(self_normed, self_value_low)
    self_normed_grad = (
        project_back(self_query_low, decoder_attention_back[1])
        + project_back(self_key_low, decoder_attention_back[2])
        + project_back(self_value_low, decoder_attention_back[3])
    )
    target_part, self_gain_grad = norm_back(target_residual, self_gain, self_normed_grad)
    decoder_input_grad = middle_grad + target_part
    target_table_grad = target_bias_back(target_bias_total)[0]
    decoder_attention_grads = reduce_weights(
        (
            self_gain_grad,
            self_query_grad,
            self_key_grad,
            self_value_grad,
            self_outward_grad,
            cross_gain_grad,
            cross_query_grad,
            cross_key_grad,
            cross_value_grad,
            cross_outward_grad,
        )
    )
    encoder_feedforward_back = gather_again(encoder_feedforward_shards)
    memory_part, final_gain_grad = norm_back(encoder_output, final_gain, memory_grad)
    encoder_output_grad = encoder_cotangent.astype(jnp.float32) + memory_part
    encoder_normed_grad, encoder_widen_grad, encoder_narrow_grad = feedforward_back(
        second_normed,
        encoder_pre,
        encoder_active,
        encoder_feedforward_back[1],
        encoder_feedforward_back[2],
        encoder_output_grad,
    )
    encoder_middle_part, second_gain_grad = norm_back(
        encoder_middle, second_gain, encoder_normed_grad
    )
    encoder_middle_grad = encoder_output_grad + encoder_middle_part
    encoder_feedforward_grads = reduce_weights(
        (second_gain_grad, encoder_widen_grad, encoder_narrow_grad, final_gain_grad)
    )
    encoder_attention_back = gather_again(encoder_attention_shards)
    (
        encoder_outward_grad,
        encoder_query_low,
        encoder_key_full,
        encoder_value_full,
        encoder_bias_total,
    ) = attention_back_local(
        encoder_queries,
        encoder_keys,
        encoder_values,
        encoder_bias,
        encoder_masks,
        encoder_log_total,
        encoder_attended,
        encoder_attention_back[4],
        encoder_middle_grad,
    )
    encoder_key_own, encoder_value_own = (
        lax.psum_scatter(
            encoder_key_full.astype(jnp.bfloat16), "seq", scatter_dimension=1, tiled=True
        ).astype(jnp.float32),
        lax.psum_scatter(
            encoder_value_full.astype(jnp.bfloat16), "seq", scatter_dimension=1, tiled=True
        ).astype(jnp.float32),
    )
    encoder_key_low = encoder_key_own.astype(jnp.bfloat16)
    encoder_value_low = encoder_value_own.astype(jnp.bfloat16)
    encoder_query_grad = weight_grad(first_normed, encoder_query_low)
    encoder_key_grad = weight_grad(first_normed, encoder_key_low)
    encoder_value_grad = weight_grad(first_normed, encoder_value_low)
    first_normed_grad = (
        project_back(encoder_query_low, encoder_attention_back[1])
        + project_back(encoder_key_low, encoder_attention_back[2])
        + project_back(encoder_value_low, encoder_attention_back[3])
    )
    encoder_part, first_gain_grad = norm_back(encoder_residual, first_gain, first_normed_grad)
    encoder_input_grad = encoder_middle_grad + encoder_part
    encoder_table_grad = encoder_bias_back(encoder_bias_total)[0]
    encoder_attention_grads = reduce_weights(
        (
            first_gain_grad,
            encoder_query_grad,
            encoder_key_grad,
            encoder_value_grad,
            encoder_outward_grad,
        )
    )
    encoder_valid = encoder_valid_query[:, :, None]
    target_valid = target_valid_query[:, :, None]
    partial_sums = jnp.stack(
        [
            jnp.sum(jnp.where(encoder_valid, encoder_output * encoder_output, 0.0)),
            jnp.sum(jnp.where(encoder_valid, encoder_branch * encoder_branch, 0.0)),
            jnp.sum(jnp.where(target_valid, decoder_output * decoder_output, 0.0)),
            jnp.sum(jnp.where(target_valid, decoder_branch * decoder_branch, 0.0)),
            jnp.sum(encoder_valid_query.astype(jnp.float32)),
            jnp.sum(target_valid_query.astype(jnp.float32)),
        ]
    )
    encoder_table_total, target_table_total, summed = lax.psum(
        (encoder_table_grad, target_table_grad, partial_sums), ("rows", "seq")
    )
    divisors = jnp.stack([summed[4], summed[4], summed[5], summed[5]]) * feature_count
    statistics = jnp.sqrt(summed[:4] / divisors)
    return (
        encoder_output,
        decoder_output,
        encoder_input_grad,
        decoder_input_grad,
        encoder_attention_grads[0],
        encoder_attention_grads[1],
        encoder_attention_grads[2],
        encoder_attention_grads[3],
        encoder_attention_grads[4],
        encoder_table_total,
        encoder_feedforward_grads[0],
        encoder_feedforward_grads[1],
        encoder_feedforward_grads[2],
        encoder_feedforward_grads[3],
        decoder_attention_grads[0],
        decoder_attention_grads[1],
        decoder_attention_grads[2],
        decoder_attention_grads[3],
        decoder_attention_grads[4],
        target_table_total,
        decoder_attention_grads[5],
        decoder_attention_grads[6],
        decoder_attention_grads[7],
        decoder_attention_grads[8],
        decoder_attention_grads[9],
        decoder_feedforward_grads[0],
        decoder_feedforward_grads[1],
        decoder_feedforward_grads[2],
        statistics,
    )


def solution(mesh):
    in_specs = (
        P("rows", "seq", None),
        P("rows", "seq", None),
        P("rows", None),
        P("rows"),
        P(),
        P(("rows", "seq")),
        P(("rows", "seq"), None),
        P(("rows", "seq"), None),
        P(("rows", "seq"), None),
        P(("rows", "seq"), None),
        P(),
        P(("rows", "seq")),
        P(("rows", "seq"), None),
        P(("rows", "seq"), None),
        P(("rows", "seq")),
        P(("rows", "seq")),
        P(("rows", "seq"), None),
        P(("rows", "seq"), None),
        P(("rows", "seq"), None),
        P(("rows", "seq"), None),
        P(),
        P(("rows", "seq")),
        P(("rows", "seq"), None),
        P(("rows", "seq"), None),
        P(("rows", "seq"), None),
        P(("rows", "seq"), None),
        P(("rows", "seq")),
        P(("rows", "seq"), None),
        P(("rows", "seq"), None),
        P("rows", "seq", None),
        P("rows", "seq", None),
    )
    out_specs = (
        P("rows", "seq", None),
        P("rows", "seq", None),
        P("rows", "seq", None),
        P("rows", "seq", None),
        P(("rows", "seq")),
        P(("rows", "seq"), None),
        P(("rows", "seq"), None),
        P(("rows", "seq"), None),
        P(("rows", "seq"), None),
        P(),
        P(("rows", "seq")),
        P(("rows", "seq"), None),
        P(("rows", "seq"), None),
        P(("rows", "seq")),
        P(("rows", "seq")),
        P(("rows", "seq"), None),
        P(("rows", "seq"), None),
        P(("rows", "seq"), None),
        P(("rows", "seq"), None),
        P(),
        P(("rows", "seq")),
        P(("rows", "seq"), None),
        P(("rows", "seq"), None),
        P(("rows", "seq"), None),
        P(("rows", "seq"), None),
        P(("rows", "seq")),
        P(("rows", "seq"), None),
        P(("rows", "seq"), None),
        P(),
    )
    return jax.shard_map(body, mesh=mesh, in_specs=in_specs, out_specs=out_specs, check_vma=False)
```

profile of v0, /device:TPU:0, one launch (start us, length us, event | category | flops | bytes accessed | tf_op | source)
XLA Modules:
  0.0 3121.4 jit_solution(6884929663886264619)
XLA Ops:
  14.5 42.2 %all-reduce.15 = (bf16[768]{0:T(1024)(128)(2,1)S(1)}, bf16[768]{0:T(1024)(128)(2,1)}, bf16[768]{0:T(1024)(128)(2,1)}, bf16[768]{0:T(1024)(128)(2,1)}, bf16[768]{0:T(1024)(128)(2,1)}, /*index=5*/bf16[768]{0:T(1024)(128)(2,1)}) all-reduce(bf16[768]{0:T(1024)(128)(2,1)S(1)} %dynamic-update-slice, ...), channel_id=1, replica_groups=mesh['rows'=16,'seq'=2] {'rows','seq'}, use_global_device_ids=true, to_apply=%add | all-reduce | flops 4608 | bytes 18432
  58.7 9.1 all-gather.21.cloned.1.call-done
  71.2 52.7 %all-gather.27.cloned.1.call-done = bf16[768,768]{1,0:T(8,128)(2,1)} async-done(((bf16[24,768]{1,0:T(8,128)(2,1)}), bf16[768,768]{1,0:T(8,128)(2,1)}) %all-gather.27.cloned.1.call-update) | async-done | bytes 1179664 | tf_op jit(solution)/shard_map/all_gather | solution.py:181
  136.3 521.4 %gather_fusion = s32[131072]{0:T(1024)S(1)} fusion(s32[1023]{0:T(1024)S(1)} %copy-done.2, s32[131072]{0:T(1024)S(1)} %broadcast_clamp_fusion), kind=kCustom, calls=%fused_computation | custom fusion | bytes 1572864 | tf_op jit(solution)/shard_map/jvp(jit(_take))/gather | solution.py:35
  658.9 5.8 fusion.53
  664.8 6.2 copy.261
  678.7 21.0 while.84
  680.1 4.1 fusion.326
  690.4 4.3 fusion.326
  699.7 4.9 multiply_reduce_fusion.7
  704.8 8.1 fusion.51
  712.9 8.1 multiply_reduce_fusion.8
  731.6 32.9 %gather_fusion.1 = s32[8192]{0:T(1024)S(1)} fusion(s32[1023]{0:T(1024)S(1)} %copy-done.2, s32[8192]{0:T(1024)S(1)} %fusion.165), kind=kCustom, calls=%fused_computation.1 | custom fusion | bytes 98304 | tf_op jit(solution)/shard_map/jvp(jit(_take))/gather | solution.py:35
  768.7 8.0 all_gather.112
  778.7 7.1 all_gather.115
  788.4 5.0 while.85
  795.5 21.5 all-gather.49.cloned.1.call-done
  818.7 25.9 all-gather.47.cloned.1.call-done
  847.2 26.0 all-gather.53.cloned.1.call-done
  876.5 10.1 while.86
  886.7 43.5 %all-gather.55.cloned.1.call-done = bf16[768,768]{1,0:T(8,128)(2,1)} async-done(((bf16[24,768]{1,0:T(8,128)(2,1)}), bf16[768,768]{1,0:T(8,128)(2,1)}) %all-gather.55.cloned.1.call-update) | async-done | bytes 1179664 | tf_op jit(solution)/shard_map/all_gather | solution.py:181
  932.1 63.6 %all-gather.57.cloned.1.call-done = bf16[768,3072]{1,0:T(8,128)(2,1)} async-done(((bf16[24,3072]{1,0:T(8,128)(2,1)}), bf16[768,3072]{1,0:T(8,128)(2,1)}) %all-gather.57.cloned.1.call-update) | async-done | bytes 4718608 | tf_op jit(solution)/shard_map/all_gather | solution.py:181
  998.9 62.1 %all-gather.59.cloned.1.call-done = bf16[3072,768]{1,0:T(8,128)(2,1)} async-done(((bf16[96,768]{1,0:T(8,128)(2,1)}), bf16[3072,768]{1,0:T(8,128)(2,1)}) %all-gather.59.cloned.1.call-update) | async-done | bytes 4718608 | tf_op jit(solution)/shard_map/all_gather | solution.py:181
  1061.0 4.5 fusion.66
  1075.3 26.8 while.87
  1111.3 35.7 %while.89 = (s32[]{:T(128)}, f32[12,64,128]{2,1,0:T(8,128)S(1)}, bf16[2,64,768]{1,2,0:T(8,128)(2,1)}, bf16[2,128,768]{2,0,1:T(2,128)(2,1)}, bf16[2,128,768]{2,0,...) while((s32[]{:T(128)}, f32[12,64,128]{2,1,0:T(8,128)S(1)}, ...), condition=%wide.region_38.39_spmd.clone, body=%wide.region_36.38_spmd.clone.sunk | while | flops 64093440 | bytes 12230367 | solution.py:144
  1115.6 7.3 dynamic_update_slice.96
  1124.5 3.8 dynamic_update_slice.97
  1133.4 7.3 dynamic_update_slice.96
  1142.4 3.8 dynamic_update_slice.97
  1150.8 4.8 reduce-scatter.23.cloned.1.call-done
  1155.6 4.1 multiply_reduce_fusion.3
  1160.3 9.2 fusion.36
  1177.9 63.4 %while.88 = (s32[]{:T(128)}, f32[12,256,512]{2,1,0:T(8,128)}, bf16[2,256,768]{1,2,0:T(8,128)(2,1)}, bf16[2,512,768]{1,2,0:T(8,128)(2,1)}, bf16[2,512,768]{1,2,0:...) while((s32[]{:T(128)}, f32[12,256,512]{2,1,0:T(8,128)}, ...), condition=%wide.region_31.32_spmd.clone, body=%wide.region_29.31_spmd.clone.sunk | while | flops 1025504256 | bytes 141619744 | solution.py:144
  1181.2 5.7 subtract_exponential_fusion.8
  1188.3 7.1 multiply_reduce_fusion.19
  1195.4 7.7 select_add_fusion.4
  1211.9 5.5 subtract_exponential_fusion.8
  1218.7 7.1 multiply_reduce_fusion.19
  1225.9 10.0 select_add_fusion.4
  1281.1 14.6 reduce-scatter.27.cloned.1.call-done
  1295.7 3.7 convolution_bitcast_fusion.13
  1300.7 5.2 convolution_bitcast_fusion.1
  1307.3 6.2 convolution_bitcast_fusion
  1314.8 7.1 convolution_bitcast_fusion.3
  1323.1 9.7 convolution_bitcast_fusion.2
  1340.1 4.0 stack.31
  1346.2 13.2 fusion.127
  1363.4 40.3 %all-reduce.14 = (f32[768]{0:T(1024)S(1)}, f32[32,12]{0,1:T(8,128)}, f32[768]{0:T(1024)S(1)}, f32[768]{0:T(1024)S(1)}, f32[768]{0:T(1024)S(1)}, /*index=5*/f32[3...) all-reduce(f32[768]{0:T(1024)S(1)} %get-tuple-element.664, ...), channel_id=8, replica_groups=mesh['rows'=16,'seq'=2] {'rows','seq'}, use_global_device_ids=true, to_apply=%region_43.44.clone | all-reduce | flops 5382 | bytes 43056
  1412.6 92.5 %reduce-scatter.41.cloned.1.call-done = f32[24,768]{1,0:T(8,128)} async-done(((f32[768,768]{1,0:T(8,128)}), f32[24,768]{1,0:T(8,128)}) %reduce-scatter.41.cloned.1.call-update) | async-done | bytes 73744 | tf_op jit(solution)/shard_map/reduce_scatter | solution.py:195
  1505.2 104.7 %reduce-scatter.55.cloned.1.call-done = f32[24,768]{1,0:T(8,128)} async-done(((f32[768,768]{1,0:T(8,128)}), f32[24,768]{1,0:T(8,128)}) %reduce-scatter.55.cloned.1.call-update) | async-done | bytes 73744 | tf_op jit(solution)/shard_map/reduce_scatter | solution.py:195
  1609.9 104.0 %reduce-scatter.49.cloned.1.call-done = f32[24,768]{1,0:T(8,128)} async-done(((f32[768,768]{1,0:T(8,128)}), f32[24,768]{1,0:T(8,128)}) %reduce-scatter.49.cloned.1.call-update) | async-done | bytes 73744 | tf_op jit(solution)/shard_map/reduce_scatter | solution.py:195
  1713.9 104.6 %reduce-scatter.43.cloned.1.call-done = f32[24,768]{1,0:T(8,128)} async-done(((f32[768,768]{1,0:T(8,128)}), f32[24,768]{1,0:T(8,128)}) %reduce-scatter.43.cloned.1.call-update) | async-done | bytes 73744 | tf_op jit(solution)/shard_map/reduce_scatter | solution.py:195
  1818.5 104.0 %reduce-scatter.45.cloned.1.call-done = f32[24,768]{1,0:T(8,128)} async-done(((f32[768,768]{1,0:T(8,128)}), f32[24,768]{1,0:T(8,128)}) %reduce-scatter.45.cloned.1.call-update) | async-done | bytes 73744 | tf_op jit(solution)/shard_map/reduce_scatter | solution.py:195
  1922.4 104.7 %reduce-scatter.51.cloned.1.call-done = f32[24,768]{1,0:T(8,128)} async-done(((f32[768,768]{1,0:T(8,128)}), f32[24,768]{1,0:T(8,128)}) %reduce-scatter.51.cloned.1.call-update) | async-done | bytes 73744 | tf_op jit(solution)/shard_map/reduce_scatter | solution.py:195
  2027.2 103.8 %reduce-scatter.53.cloned.1.call-done = f32[24,768]{1,0:T(8,128)} async-done(((f32[768,768]{1,0:T(8,128)}), f32[24,768]{1,0:T(8,128)}) %reduce-scatter.53.cloned.1.call-update) | async-done | bytes 73744 | tf_op jit(solution)/shard_map/reduce_scatter | solution.py:195
  2130.9 104.8 %reduce-scatter.35.cloned.1.call-done = f32[24,768]{1,0:T(8,128)} async-done(((f32[768,768]{1,0:T(8,128)}), f32[24,768]{1,0:T(8,128)}) %reduce-scatter.35.cloned.1.call-update) | async-done | bytes 73744 | tf_op jit(solution)/shard_map/reduce_scatter | solution.py:195
  2235.7 103.9 %reduce-scatter.29.cloned.1.call-done = f32[24,768]{1,0:T(8,128)} async-done(((f32[768,768]{1,0:T(8,128)}), f32[24,768]{1,0:T(8,128)}) %reduce-scatter.29.cloned.1.call-update) | async-done | bytes 73744 | tf_op jit(solution)/shard_map/reduce_scatter | solution.py:195
  2339.6 104.6 %reduce-scatter.31.cloned.1.call-done = f32[24,768]{1,0:T(8,128)} async-done(((f32[768,768]{1,0:T(8,128)}), f32[24,768]{1,0:T(8,128)}) %reduce-scatter.31.cloned.1.call-update) | async-done | bytes 73744 | tf_op jit(solution)/shard_map/reduce_scatter | solution.py:195
  2444.2 103.8 %reduce-scatter.33.cloned.1.call-done = f32[24,768]{1,0:T(8,128)} async-done(((f32[768,768]{1,0:T(8,128)}), f32[24,768]{1,0:T(8,128)}) %reduce-scatter.33.cloned.1.call-update) | async-done | bytes 73744 | tf_op jit(solution)/shard_map/reduce_scatter | solution.py:195
  2548.0 142.1 %reduce-scatter.57.cloned.1.call-done = f32[24,3072]{1,0:T(8,128)} async-done(((f32[768,3072]{1,0:T(8,128)}), f32[24,3072]{1,0:T(8,128)}) %reduce-scatter.57.cloned.1.call-update) | async-done | bytes 294928 | tf_op jit(solution)/shard_map/reduce_scatter | solution.py:195
  2690.1 141.0 %reduce-scatter.59.cloned.1.call-done = f32[96,768]{1,0:T(8,128)} async-done(((f32[3072,768]{1,0:T(8,128)}), f32[96,768]{1,0:T(8,128)}) %reduce-scatter.59.cloned.1.call-update) | async-done | bytes 294928 | tf_op jit(solution)/shard_map/reduce_scatter | solution.py:195
  2831.1 142.1 %reduce-scatter.37.cloned.1.call-done = f32[24,3072]{1,0:T(8,128)} async-done(((f32[768,3072]{1,0:T(8,128)}), f32[24,3072]{1,0:T(8,128)}) %reduce-scatter.37.cloned.1.call-update) | async-done | bytes 294928 | tf_op jit(solution)/shard_map/reduce_scatter | solution.py:195
  2973.2 141.1 %reduce-scatter.39.cloned.1.call-done = f32[96,768]{1,0:T(8,128)} async-done(((f32[3072,768]{1,0:T(8,128)}), f32[96,768]{1,0:T(8,128)}) %reduce-scatter.39.cloned.1.call-update) | async-done | bytes 294928 | tf_op jit(solution)/shard_map/reduce_scatter | solution.py:195
  (737 shorter events, 251.4 us)
Async XLA Ops:
  7.2 651.7 %copy-start = (f32[32,12]{0,1:T(8,128)S(1)}, f32[32,12]{0,1:T(8,128)}, u32[]{:S(2)}) copy-start(f32[32,12]{0,1:T(8,128)} %param.53) | copy-start | bytes 4612
  7.2 60.6 %all-gather.21.cloned.1.call-start = ((), (), s32[]{:S(2)}) async-start(), calls=%async_computation.20 | async-start | bytes 1216512 | tf_op jit(solution)/shard_map/all_gather | solution.py:181
  8.0 115.9 %all-gather.27.cloned.1.call-start = ((), (), s32[]{:S(2)}) async-start(), calls=%async_computation.23 | async-start | bytes 1216512 | tf_op jit(solution)/shard_map/all_gather | solution.py:181
  8.7 663.3 %all-gather.25.cloned.1.call-start = ((), (), s32[]{:S(2)}) async-start(), calls=%async_computation.22 | async-start | bytes 1216512 | tf_op jit(solution)/shard_map/all_gather | solution.py:181
  9.4 665.8 %all-gather.23.cloned.1.call-start = ((), (), s32[]{:S(2)}) async-start(), calls=%async_computation.21 | async-start | bytes 2359296 | tf_op jit(solution)/shard_map/all_gather | solution.py:267
  56.8 67.1 %copy-start.99 = (f32[768]{0:T(1024)}, f32[768]{0:T(1024)S(1)}, u32[]{:S(2)}) copy-start(f32[768]{0:T(1024)S(1)} %convert_element_type.214) | copy-start | bytes 9220
  58.7 65.2 %copy-start.110 = (f32[2,256]{1,0:T(2,128)}, f32[2,256]{1,0:T(2,128)S(1)}, u32[]{:S(2)}) copy-start(f32[2,256]{1,0:T(2,128)S(1)} %fusion.171) | copy-start | bytes 6148
  58.7 65.2 %copy-start.8 = (bf16[2,256,768]{2,1,0:T(8,128)(2,1)S(1)}, bf16[2,256,768]{2,1,0:T(8,128)(2,1)}, u32[]{:S(2)}) copy-start(bf16[2,256,768]{2,1,0:T(8,128)(2,1)} %param.43) | copy-start | bytes 2359300
  71.1 605.9 %all-gather.29.cloned.1.call-start = ((), (), s32[]{:S(2)}) async-start(), calls=%async_computation.24 | async-start | bytes 2359296 | tf_op jit(solution)/shard_map/all_gather | solution.py:266
  127.0 572.8 %all-gather.31.cloned.1.call-start = ((), (), s32[]{:S(2)}) async-start(), calls=%async_computation.25 | async-start | bytes 1216512 | tf_op jit(solution)/shard_map/all_gather | solution.py:181
  127.5 577.2 %all-gather.33.cloned.1.call-start = ((), (), s32[]{:S(2)}) async-start(), calls=%async_computation.26 | async-start | bytes 4866048 | tf_op jit(solution)/shard_map/all_gather | solution.py:181
  128.3 584.6 %all-gather.35.cloned.1.call-start = ((), (), s32[]{:S(2)}) async-start(), calls=%async_computation.27 | async-start | bytes 4866048 | tf_op jit(solution)/shard_map/all_gather | solution.py:181
  129.0 593.3 %all-gather.45.cloned.1.call-start = ((), (), s32[]{:S(2)}) async-start(), calls=%async_computation.32 | async-start | bytes 1216512 | tf_op jit(solution)/shard_map/all_gather | solution.py:181
  129.8 595.9 %all-gather.51.cloned.1.call-start = ((), (), s32[]{:S(2)}) async-start(), calls=%async_computation.35 | async-start | bytes 1216512 | tf_op jit(solution)/shard_map/all_gather | solution.py:181
  130.4 636.7 %all-gather.37.cloned.1.call-start = ((), (), s32[]{:S(2)}) async-start(), calls=%async_computation.28 | async-start | bytes 1216512 | tf_op jit(solution)/shard_map/all_gather | solution.py:181
  131.1 645.9 %all-gather.41.cloned.1.call-start = ((), (), s32[]{:S(2)}) async-start(), calls=%async_computation.30 | async-start | bytes 1216512 | tf_op jit(solution)/shard_map/all_gather | solution.py:181
  131.7 654.3 %all-gather.39.cloned.1.call-start = ((), (), s32[]{:S(2)}) async-start(), calls=%async_computation.29 | async-start | bytes 1216512 | tf_op jit(solution)/shard_map/all_gather | solution.py:181
  132.4 661.1 %all-gather.43.cloned.1.call-start = ((), (), s32[]{:S(2)}) async-start(), calls=%async_computation.31 | async-start | bytes 1216512 | tf_op jit(solution)/shard_map/all_gather | solution.py:181
  133.0 684.0 %all-gather.49.cloned.1.call-start = ((), (), s32[]{:S(2)}) async-start(), calls=%async_computation.34 | async-start | bytes 1216512 | tf_op jit(solution)/shard_map/all_gather | solution.py:181
  133.6 711.0 %all-gather.47.cloned.1.call-start = ((), (), s32[]{:S(2)}) async-start(), calls=%async_computation.33 | async-start | bytes 2359296 | tf_op jit(solution)/shard_map/all_gather | solution.py:334
  136.3 521.5 %copy-start.127 = (s32[256]{0:T(256)S(1)}, s32[256]{0:T(256)}, u32[]{:S(2)}) copy-start(s32[256]{0:T(256)} %copy-done.126) | copy-start | bytes 3076
  671.7 41.2 %copy-start.150 = (pred[2,256]{1,0:T(4,128)(4,1)}, pred[2,256]{1,0:T(4,128)(4,1)S(1)}, u32[]{:S(2)}) copy-start(pred[2,256]{1,0:T(4,128)(4,1)S(1)} %get-tuple-element.813) | copy-start | bytes 1540
  671.7 49.3 %copy-start.114 = (f32[768]{0:T(1024)}, f32[768]{0:T(1024)S(1)}, u32[]{:S(2)}) copy-start(f32[768]{0:T(1024)S(1)} %convert_element_type.230) | copy-start | bytes 9220
  725.6 147.6 %all-gather.53.cloned.1.call-start = ((), (), s32[]{:S(2)}) async-start(), calls=%async_computation.36 | async-start | bytes 2359296 | tf_op jit(solution)/shard_map/all_gather | solution.py:333
  728.7 201.5 %all-gather.55.cloned.1.call-start = ((), (), s32[]{:S(2)}) async-start(), calls=%async_computation.37 | async-start | bytes 1216512 | tf_op jit(solution)/shard_map/all_gather | solution.py:181
  729.3 266.4 %all-gather.57.cloned.1.call-start = ((), (), s32[]{:S(2)}) async-start(), calls=%async_computation.38 | async-start | bytes 4866048 | tf_op jit(solution)/shard_map/all_gather | solution.py:181
  730.0 330.9 %all-gather.59.cloned.1.call-start = ((), (), s32[]{:S(2)}) async-start(), calls=%async_computation.39 | async-start | bytes 4866048 | tf_op jit(solution)/shard_map/all_gather | solution.py:181
  730.6 416.5 %reduce-scatter.21.cloned.1.call-start = ((), (), s32[]{:S(2)}) async-start(), calls=%async_computation.40 | async-start | bytes 2359296 | tf_op jit(solution)/shard_map/reduce_scatter | solution.py:378
  731.4 34.8 %copy-start.147 = (pred[2,64]{1,0:T(4,128)(4,1)}, pred[2,64]{1,0:T(4,128)(4,1)S(1)}, u32[]{:S(2)}) copy-start(pred[2,64]{1,0:T(4,128)(4,1)S(1)} %get-tuple-element.811) | copy-start | bytes 388
  731.5 54.5 %copy-start.92 = (f32[768]{0:T(1024)}, f32[768]{0:T(1024)S(1)}, u32[]{:S(2)}) copy-start(f32[768]{0:T(1024)S(1)} %convert_element_type.225) | copy-start | bytes 9220
  731.6 33.6 %copy-start.142 = (bf16[768]{0:T(1024)(128)(2,1)S(1)}, bf16[768]{0:T(1024)(128)(2,1)}, u32[]{:S(2)}) copy-start(bf16[768]{0:T(1024)(128)(2,1)} %get-tuple-element.803) | copy-start | bytes 4612
  765.2 51.8 %copy-start.103 = (f32[768]{0:T(1024)}, f32[768]{0:T(1024)S(1)}, u32[]{:S(2)}) copy-start(f32[768]{0:T(1024)S(1)} %convert_element_type.233) | copy-start | bytes 9220
  765.4 302.4 %copy-start.88 = (f32[768]{0:T(1024)}, f32[768]{0:T(1024)S(1)}, u32[]{:S(2)}) copy-start(f32[768]{0:T(1024)S(1)} %convert_element_type.237) | copy-start | bytes 9220
  795.5 51.7 %copy-start.132 = (f32[2,64]{1,0:T(2,128)}, f32[2,64]{1,0:T(2,128)S(1)}, u32[]{:S(2)}) copy-start(f32[2,64]{1,0:T(2,128)S(1)} %get-tuple-element.849) | copy-start | bytes 1540
  795.5 134.7 %copy-start.26 = (f32[2,64,768]{2,1,0:T(8,128)}, f32[2,64,768]{2,1,0:T(8,128)S(1)}, u32[]{:S(2)}) copy-start(f32[2,64,768]{2,1,0:T(8,128)S(1)} %get-tuple-element.850) | copy-start | bytes 1179652
  795.5 51.7 %copy-start.120 = (f32[2,64]{1,0:T(2,128)}, f32[2,64]{1,0:T(2,128)S(1)}, u32[]{:S(2)}) copy-start(f32[2,64]{1,0:T(2,128)S(1)} %fusion.175) | copy-start | bytes 1540
  886.7 43.5 %copy-start.61 = (bf16[2,64,12,64]{1,3,2,0:T(8,128)(2,1)}, bf16[2,64,12,64]{1,3,2,0:T(8,128)(2,1)S(1)}, u32[]{:S(2)}) copy-start(bf16[2,64,12,64]{1,3,2,0:T(8,128)(2,1)S(1)} %get-tuple-element.339) | copy-start | bytes 589828
  886.7 109.0 %copy-start.37 = (bf16[2,64,768]{2,1,0:T(8,128)(2,1)}, bf16[2,64,768]{2,1,0:T(8,128)(2,1)S(1)}, u32[]{:S(2)}) copy-start(bf16[2,64,768]{2,1,0:T(8,128)(2,1)S(1)} %get-tuple-element.1547) | copy-start | bytes 589828
  932.0 135.8 %copy-start.40 = (f32[2,64,768]{2,1,0:T(8,128)}, f32[2,64,768]{2,1,0:T(8,128)S(1)}, u32[]{:S(2)}) copy-start(f32[2,64,768]{2,1,0:T(8,128)S(1)} %get-tuple-element.852) | copy-start | bytes 1179652
  932.0 135.8 %copy-start.116 = (f32[2,64]{1,0:T(2,128)}, f32[2,64]{1,0:T(2,128)S(1)}, u32[]{:S(2)}) copy-start(f32[2,64]{1,0:T(2,128)S(1)} %fusion.176) | copy-start | bytes 1540
  998.9 69.0 %copy-start.31 = (f32[2,64,3072]{2,1,0:T(8,128)}, f32[2,64,3072]{2,1,0:T(8,128)S(1)}, u32[]{:S(2)}) copy-start(f32[2,64,3072]{2,1,0:T(8,128)S(1)} %fusion.43) | copy-start | bytes 4718596
  1102.1 53.5 %reduce-scatter.23.cloned.1.call-start = ((), (), s32[]{:S(2)}) async-start(), calls=%async_computation.41 | async-start | bytes 2359296 | tf_op jit(solution)/shard_map/reduce_scatter | solution.py:381
  1106.4 149.2 %all-reduce.19.cloned.1.call-start = ((), (), s32[]{:S(2)}) async-start(), calls=%async_computation.60 | async-start | bytes 1572864
  1147.1 130.5 %reduce-scatter.25.cloned.1.call-start = ((), (), s32[]{:S(2)}) async-start(), calls=%async_computation.42 | async-start | bytes 2359296 | tf_op jit(solution)/shard_map/reduce_scatter | solution.py:481
  1241.3 54.4 %reduce-scatter.27.cloned.1.call-start = ((), (), s32[]{:S(2)}) async-start(), calls=%async_computation.43 | async-start | bytes 2359296 | tf_op jit(solution)/shard_map/reduce_scatter | solution.py:484
  1242.1 170.6 %reduce-scatter.47.cloned.1.call-start = ((), (), s32[]{:S(2)}) async-start(), calls=%async_computation.53 | async-start | bytes 2433024 | tf_op jit(solution)/shard_map/reduce_scatter | solution.py:195
  1244.4 260.8 %reduce-scatter.41.cloned.1.call-start = ((), (), s32[]{:S(2)}) async-start(), calls=%async_computation.50 | async-start | bytes 2433024 | tf_op jit(solution)/shard_map/reduce_scatter | solution.py:195
  1247.5 362.4 %reduce-scatter.55.cloned.1.call-start = ((), (), s32[]{:S(2)}) async-start(), calls=%async_computation.57 | async-start | bytes 2433024 | tf_op jit(solution)/shard_map/reduce_scatter | solution.py:195
  1250.6 463.3 %reduce-scatter.49.cloned.1.call-start = ((), (), s32[]{:S(2)}) async-start(), calls=%async_computation.54 | async-start | bytes 2433024 | tf_op jit(solution)/shard_map/reduce_scatter | solution.py:195
  1253.8 564.7 %reduce-scatter.43.cloned.1.call-start = ((), (), s32[]{:S(2)}) async-start(), calls=%async_computation.51 | async-start | bytes 2433024 | tf_op jit(solution)/shard_map/reduce_scatter | solution.py:195
  1258.8 663.7 %reduce-scatter.45.cloned.1.call-start = ((), (), s32[]{:S(2)}) async-start(), calls=%async_computation.52 | async-start | bytes 2433024 | tf_op jit(solution)/shard_map/reduce_scatter | solution.py:195
  1261.9 765.2 %reduce-scatter.51.cloned.1.call-start = ((), (), s32[]{:S(2)}) async-start(), calls=%async_computation.55 | async-start | bytes 2433024 | tf_op jit(solution)/shard_map/reduce_scatter | solution.py:195
  1265.5 865.4 %reduce-scatter.53.cloned.1.call-start = ((), (), s32[]{:S(2)}) async-start(), calls=%async_computation.56 | async-start | bytes 2433024 | tf_op jit(solution)/shard_map/reduce_scatter | solution.py:195
  1268.9 966.8 %reduce-scatter.35.cloned.1.call-start = ((), (), s32[]{:S(2)}) async-start(), calls=%async_computation.47 | async-start | bytes 2433024 | tf_op jit(solution)/shard_map/reduce_scatter | solution.py:195
  1273.7 1065.9 %reduce-scatter.29.cloned.1.call-start = ((), (), s32[]{:S(2)}) async-start(), calls=%async_computation.44 | async-start | bytes 2433024 | tf_op jit(solution)/shard_map/reduce_scatter | solution.py:195
  1277.5 1166.8 %reduce-scatter.31.cloned.1.call-start = ((), (), s32[]{:S(2)}) async-start(), calls=%async_computation.45 | async-start | bytes 2433024 | tf_op jit(solution)/shard_map/reduce_scatter | solution.py:195
  1281.1 1266.9 %reduce-scatter.33.cloned.1.call-start = ((), (), s32[]{:S(2)}) async-start(), calls=%async_computation.46 | async-start | bytes 2433024 | tf_op jit(solution)/shard_map/reduce_scatter | solution.py:195
  1299.4 1390.6 %reduce-scatter.57.cloned.1.call-start = ((), (), s32[]{:S(2)}) async-start(), calls=%async_computation.58 | async-start | bytes 9732096 | tf_op jit(solution)/shard_map/reduce_scatter | solution.py:195
  1305.9 1525.2 %reduce-scatter.59.cloned.1.call-start = ((), (), s32[]{:S(2)}) async-start(), calls=%async_computation.59 | async-start | bytes 9732096 | tf_op jit(solution)/shard_map/reduce_scatter | solution.py:195
  1313.4 1659.7 %reduce-scatter.37.cloned.1.call-start = ((), (), s32[]{:S(2)}) async-start(), calls=%async_computation.48 | async-start | bytes 9732096 | tf_op jit(solution)/shard_map/reduce_scatter | solution.py:195
  1322.0 1792.4 %reduce-scatter.39.cloned.1.call-start = ((), (), s32[]{:S(2)}) async-start(), calls=%async_computation.49 | async-start | bytes 9732096 | tf_op jit(solution)/shard_map/reduce_scatter | solution.py:195
  1361.0 48.6 %copy-start.124 = (f32[2,256]{1,0:T(2,128)S(1)}, f32[2,256]{1,0:T(2,128)}, u32[]{:S(2)}) copy-start(f32[2,256]{1,0:T(2,128)} %copy-done.123) | copy-start | bytes 6148
  1361.0 48.6 %copy-start.25 = (f32[2,256,768]{2,1,0:T(8,128)S(1)}, f32[2,256,768]{2,1,0:T(8,128)}, u32[]{:S(2)}) copy-start(f32[2,256,768]{2,1,0:T(8,128)} %copy-done.23) | copy-start | bytes 4718596
  1409.6 1704.7 %copy-start.1 = (f32[32,12]{0,1:T(8,128)S(1)}, f32[32,12]{0,1:T(8,128)}, u32[]{:S(2)}) copy-start(f32[32,12]{0,1:T(8,128)} %param.53) | copy-start | bytes 4612
  (162 other events, 734.1 us)
Sparse Core Ops, SparseCore 0:
  11.0 56.8 all-gather.20
  70.8 53.0 all-gather.26
  126.8 53.1 all-gather.24
  181.9 26.1 all-gather.22
  210.1 27.1 all-gather.28
  240.1 54.1 all-gather.30
  297.2 62.6 all-gather.32
  362.8 62.4 all-gather.34
  428.2 52.9 all-gather.44
  484.0 53.0 all-gather.50
  540.0 53.1 all-gather.36
  595.9 53.0 all-gather.40
  652.0 53.0 all-gather.38
  707.9 53.1 all-gather.42
  763.8 53.1 all-gather.48
  818.4 26.1 all-gather.46
  846.0 27.2 all-gather.52
  876.0 54.1 all-gather.54
  933.1 62.5 all-gather.56
  998.5 62.4 all-gather.58
  1102.2 24.8 reduce-scatter.20
  1129.5 26.0 reduce-scatter.22
  1158.0 34.4 all-reduce.18
  1241.4 25.8 reduce-scatter.24
  1269.6 26.0 reduce-scatter.26
  1302.3 99.0 reduce-scatter.46
  1407.1 98.0 reduce-scatter.40
  1511.9 97.9 reduce-scatter.54
  1615.7 98.1 reduce-scatter.48
  1720.5 97.9 reduce-scatter.42
  1824.3 98.0 reduce-scatter.44
  1929.2 97.9 reduce-scatter.50
  2032.9 98.0 reduce-scatter.52
  2137.7 98.0 reduce-scatter.34
  2241.6 98.0 reduce-scatter.28
  2346.2 98.0 reduce-scatter.30
  2450.0 98.0 reduce-scatter.32
  2555.5 134.5 reduce-scatter.56
  2696.4 134.6 reduce-scatter.58
  2838.6 134.5 reduce-scatter.36
  2979.7 134.6 reduce-scatter.38
where the time goes:
time: 3130 us; the launch traced here: 3120 us
  waiting for transfers between devices  2040 us (65%)
  local copies, waits for them, and re-layouts  698 us (22%)
  matrix products  228 us (7%)
  blocking collectives  97.6 us (3%)
  other arithmetic  39.7 us (1%)
    reduce_scatter x16, waiting for transfers between devices, reduce_weights(): lax.psum_scatter(grads, ('rows', 'seq'), scatter_dimension=0, tiled=True)  1700 us
    gather x3, local copies, waits for them, and re-layouts, position_bias(): bucket_index = jnp.take(buckets, distance_index, axis=0)  554 us
    all_gather x16, waiting for transfers between devices, gather_weights(): lax.all_gather(as_sent(shards), ('rows', 'seq'), axis=0, tiled=True)  253 us
    unnamed x2, blocking collectives  82.5 us
  transfers between devices with their start and end apart: 41, of which 25 were waited for; matrix products, arithmetic and copies ran while one was open for 29% of the time, Pallas kernels for 0%

commit v1 on v0

v1 whole, which is shorter than its diff:
```python
import functools

import jax
import jax.numpy as jnp
from jax import lax
from jax.experimental import pallas as pl
from jax.experimental.pallas import tpu as pltpu
from jax.sharding import PartitionSpec as P

HEADS = 12
BUCKETS = 32
EPSILON = 1e-06
NEGATIVE = -1e30
HIGHEST_PRECISION = lax.Precision.HIGHEST
BOTH = ("rows", "seq")
CHAIN = 4

SPAN=1024
CONTRACT_LAST=(((1,),(1,)),((),()))
CONTRACT_FIRST=(((0,),(0,)),((),()))

def dotf(a,b,dims):
    return lax.dot_general(a,b,dims,preferred_element_type=jnp.float32)

def allowed_of(mode,qcode,kcode,shape):
    if mode=="segment":
        return qcode==kcode
    if mode=="causal":
        qi=lax.broadcasted_iota(jnp.int32,shape,0); ki=lax.broadcasted_iota(jnp.int32,shape,1)
        return (ki<=qi)&(qcode==kcode)
    return (qcode==0)|(kcode==1)

def probs_of(q,k,table_ref,h,allowed,half):
    s=dotf(q,k,CONTRACT_LAST)
    if table_ref is not None:
        row=jnp.broadcast_to(table_ref[0,h:h+1,:],(s.shape[0],SPAN))
        s=s+pltpu.roll(row,SPAN-half,1,stride=1,stride_axis=0)[:,:s.shape[1]]
    s=jnp.where(allowed,s,NEGATIVE)
    e=jnp.exp(s-jnp.max(s,axis=-1,keepdims=True))
    return e*(1.0/jnp.sum(e,axis=-1,keepdims=True))

def fwd_kernel(mode,half,*refs):
    if mode=="cross":
        q_ref,k_ref,v_ref,qc,kc,o_ref=refs; t_ref=None
    else:
        q_ref,k_ref,v_ref,qc,kc,t_ref,o_ref=refs
    allowed=allowed_of(mode,qc[...],kc[...],(q_ref.shape[0],k_ref.shape[0]))
    for h in range(2):
        sl=slice(64*h,64*h+64)
        p=probs_of(q_ref[:,sl],k_ref[:,sl],t_ref,h,allowed,half)
        o_ref[:,sl]=jnp.dot(p.astype(jnp.bfloat16),v_ref[:,sl],preferred_element_type=jnp.float32).astype(jnp.bfloat16)

def bwd_kernel(mode,half,*refs):
    if mode=="cross":
        q_ref,k_ref,v_ref,g_ref,qc,kc,dq_ref,dk_ref,dv_ref=refs; t_ref=None
    else:
        q_ref,k_ref,v_ref,g_ref,qc,kc,t_ref,dq_ref,dk_ref,dv_ref,dt_ref=refs
    allowed=allowed_of(mode,qc[...],kc[...],(q_ref.shape[0],k_ref.shape[0]))
    for h in range(2):
        sl=slice(64*h,64*h+64)
        q=q_ref[:,sl];k=k_ref[:,sl];v=v_ref[:,sl];g=g_ref[:,sl]
        p=probs_of(q,k,t_ref,h,allowed,half)
        dv_ref[:,sl]=dotf(p.astype(jnp.bfloat16),g,CONTRACT_FIRST).astype(jnp.bfloat16)
        dp=dotf(g,v,CONTRACT_LAST)
        ds=p*(dp-jnp.sum(dp*p,axis=-1,keepdims=True))
        dsb=ds.astype(jnp.bfloat16)
        dq_ref[:,sl]=jnp.dot(dsb,k,preferred_element_type=jnp.float32).astype(jnp.bfloat16)
        dk_ref[:,sl]=dotf(dsb,q,CONTRACT_FIRST).astype(jnp.bfloat16)
        if t_ref is not None:
            sq=ds.shape[0]
            flip=(lax.broadcasted_iota(jnp.int32,(sq,sq),0)+lax.broadcasted_iota(jnp.int32,(sq,sq),1)==sq-1).astype(jnp.bfloat16)
            flipped=jnp.dot(flip,dsb,preferred_element_type=jnp.float32)
            wide=jnp.concatenate([flipped,jnp.zeros((sq,SPAN-ds.shape[1]),jnp.float32)],axis=1)
            rolled=pltpu.roll(wide,half-(sq-1),1,stride=1,stride_axis=0)
            dt_ref[0,h:h+1,:]=jnp.sum(rolled,axis=0,keepdims=True)

def attn(kernel,mode,half,outs,q,k,v,extra,qc,kc,table):
    sq,width=q.shape; sk=k.shape[0]
    qs=pl.BlockSpec((sq,128),lambda i:(0,i)); ks=pl.BlockSpec((sk,128),lambda i:(0,i))
    ts=pl.BlockSpec((1,2,SPAN),lambda i:(i,0,0))
    ins=[q,k,v]+extra+[qc,kc]; specs=[qs,ks,ks]+[qs]*len(extra)+[pl.BlockSpec((sq,1),lambda i:(0,0)),pl.BlockSpec((1,sk),lambda i:(0,0))]
    if table is not None: ins.append(table); specs.append(ts)
    shapes={"q":(jax.ShapeDtypeStruct((sq,width),jnp.bfloat16),qs),"k":(jax.ShapeDtypeStruct((sk,width),jnp.bfloat16),ks),"t":(jax.ShapeDtypeStruct((width//128,2,SPAN),jnp.float32),ts)}
    return pl.pallas_call(functools.partial(kernel,mode,half),grid=(width//128,),in_specs=specs,
        out_shape=[shapes[o][0] for o in outs],out_specs=[shapes[o][1] for o in outs],
        compiler_params=pltpu.CompilerParams(vmem_limit_bytes=48*2**20))(*ins)

def attn_fwd(mode,half,q,k,v,qc,kc,table):
    return attn(fwd_kernel,mode,half,"q",q,k,v,[],qc,kc,table)[0]
def attn_bwd(mode,half,q,k,v,g,qc,kc,table):
    return attn(bwd_kernel,mode,half,"qkk"+("t" if table is not None else ""),q,k,v,[g],qc,kc,table)


def flat_index(z, x, core, y):
    return ((z * 2 + x) * 2 + core) * 2 + y


def every_device():
    return [(z, x, c, y) for z in range(CHAIN) for x in range(2) for c in range(2) for y in range(2)]


def swap(value, axis):
    pairs = []
    for place in every_device():
        other = list(place)
        other["zxcy".index(axis)] ^= 1
        pairs.append((flat_index(*place), flat_index(*other)))
    return lax.ppermute(value, BOTH, pairs)


def shift(value, step, reach):
    pairs = []
    for z, x, c, y in every_device():
        if 0 <= z + step < CHAIN and 0 <= z + reach < CHAIN:
            pairs.append((flat_index(z, x, c, y), flat_index(z + step, x, c, y)))
    return lax.ppermute(value, BOTH, pairs)


def hop(value, bit):
    size = 4 * CHAIN * 2
    return lax.ppermute(value, BOTH, [(i, i ^ bit) for i in range(size)])


def place_of():
    row = lax.axis_index("rows")
    return {"z": row // 4, "x": (row // 2) % 2, "c": row % 2, "y": lax.axis_index("seq")}


def assemble_kernel(count, shifts, *refs):
    pieces = refs[:8]
    outs = refs[8 : 8 + count]
    sem = refs[8 + count]
    row = lax.axis_index("rows")
    here = {"x": (row // 2) % 2, "c": row % 2, "y": lax.axis_index("seq")}
    copies = []
    for number, piece in enumerate(pieces):
        moved = shifts[number]
        slot = {a: here[a] + (1 - 2 * here[a]) * (1 if a in moved else 0) for a in "xcy"}
        index = slot["x"] * 4 + slot["c"] * 2 + slot["y"]
        for item in range(count):
            copy = pltpu.make_async_copy(
                piece.at[item], outs[item].at[:, index], sem.at[number, item]
            )
            copy.start()
            copies.append(copy)
    for copy in copies:
        copy.wait()


def assemble(pieces, shifts):
    count, chain, height, width = pieces[0].shape
    outs = pl.pallas_call(
        functools.partial(assemble_kernel, count, shifts),
        out_shape=[jax.ShapeDtypeStruct((chain, 8, height, width), pieces[0].dtype)] * count,
        in_specs=[pl.BlockSpec(memory_space=pl.ANY)] * 8,
        out_specs=[pl.BlockSpec(memory_space=pl.ANY)] * count,
        scratch_shapes=[pltpu.SemaphoreType.DMA((8, count))],
        cost_estimate=pl.CostEstimate(
            flops=0, bytes_accessed=2 * 8 * pieces[0].size * 2, transcendentals=0
        ),
    )(*pieces)
    return [out.reshape(chain * 8 * height, width) for out in outs]


def gather_group(shards, order):
    own = jnp.stack(shards)
    place = place_of()
    up, down = own, own
    ups, downs = {}, {}
    for step in range(1, CHAIN):
        up = shift(up, 1, 1 - step)
        down = shift(down, -1, step - 1)
        ups[step], downs[step] = up, down
    blocks = []
    for k in range(CHAIN):
        block = own
        for step in range(1, CHAIN):
            if k + step < CHAIN:
                block = jnp.where(place["z"] == k + step, ups[step], block)
            if k - step >= 0:
                block = jnp.where(place["z"] == k - step, downs[step], block)
        blocks.append(block)
    pieces = {"": jnp.stack(blocks, axis=1)}
    for axis in order:
        for name in list(pieces):
            pieces[name + axis] = swap(pieces[name], axis)
    names = list(pieces)
    return assemble([pieces[name] for name in names], names)


def reduce_group(grads, order):
    place = place_of()
    axes = ["z", "x", "c", "y"]
    parts = [
        grad.reshape(CHAIN, 2, 2, 2, grad.shape[0] // (8 * CHAIN), grad.shape[1]) for grad in grads
    ]
    held = None
    for axis in reversed(order):
        at = axes.index(axis)
        axes.remove(axis)
        mine = place[axis]
        if held is None:
            pick = lambda where: jnp.stack(
                [lax.dynamic_index_in_dim(part, where, at, keepdims=False) for part in parts]
            )
        else:
            pick = lambda where: lax.dynamic_index_in_dim(held, where, at + 1, keepdims=False)
        sent = swap(pick(1 - mine), axis)
        held = (pick(mine).astype(jnp.float32) + sent.astype(jnp.float32)).astype(jnp.bfloat16)
    pick = lambda where: lax.dynamic_index_in_dim(
        held, jnp.clip(where, 0, CHAIN - 1), 1, keepdims=False
    ).astype(jnp.float32)
    total = pick(place["z"])
    for sign in (1, -1):
        moving = None
        for step in range(CHAIN - 1, 0, -1):
            term = pick(place["z"] + sign * step)
            if moving is not None:
                term = term + moving.astype(jnp.float32)
            moving = shift(term.astype(jnp.bfloat16), sign, sign * step)
        total = total + moving.astype(jnp.float32)
    return [total[i] for i in range(len(grads))]


def sum_everywhere(value):
    for bit in (1, 2, 4, 8, 16):
        value = value + hop(value, bit)
    return value


def whole_row(halves):
    mine = lax.axis_index("seq")
    keep = lax.dynamic_index_in_dim(halves, mine, 0, keepdims=False)
    other = lax.ppermute(
        lax.dynamic_index_in_dim(halves, 1 - mine, 0, keepdims=False), "seq", [(0, 1), (1, 0)]
    )
    first = jnp.where(mine == 0, keep, other)
    second = jnp.where(mine == 0, other, keep)
    return jnp.concatenate([first, second], axis=0)


def own_slots(row):
    mine = lax.axis_index("seq")
    half = row.shape[0] // 2
    keep = lax.dynamic_slice_in_dim(row, mine * half, half, 0)
    sent = lax.dynamic_slice_in_dim(row, (1 - mine) * half, half, 0).astype(jnp.bfloat16)
    other = lax.ppermute(sent, "seq", [(0, 1), (1, 0)]).astype(row.dtype)
    return jnp.stack([jnp.where(mine == 0, keep, other), jnp.where(mine == 0, other, keep)])


def matmul(left, right):
    return jnp.dot(left, right, preferred_element_type=jnp.float32)


def matmul_back(grads, weight):
    return dotf(grads, weight, CONTRACT_LAST)


def weight_grad(inputs, grads):
    return dotf(inputs, grads, CONTRACT_FIRST).astype(jnp.bfloat16)


def rms_scale(values, gain_vec):
    return (
        values * lax.rsqrt(jnp.mean(values * values, axis=-1, keepdims=True) + EPSILON) * gain_vec
    )


def gelu_float(values):
    return jax.nn.gelu(values, approximate=True)


def norm_back(values, gain_vec, upstream):
    unused_value, pullback = jax.vjp(rms_scale, values, gain_vec)
    return pullback(upstream)


def low(values):
    return values.astype(jnp.bfloat16)


def feedforward_back(normed, pre_values, active, widen, narrow, upstream):
    branch_low = low(upstream)
    narrow_grad = weight_grad(active, branch_low)
    active_grad = matmul_back(branch_low, narrow)
    unused_value, gelu_pull = jax.vjp(gelu_float, pre_values)
    pre_low = low(gelu_pull(active_grad)[0])
    return (matmul_back(pre_low, widen), weight_grad(normed, pre_low), narrow_grad)


def distance_table(table_in, buckets):
    ids = jnp.arange(BUCKETS, dtype=jnp.int32)
    selector = (buckets[:, None] == ids[None, :]).astype(jnp.float32)
    by_distance = jnp.einsum("db,bh->hd", selector, table_in, precision=HIGHEST_PRECISION)
    padded = jnp.pad(by_distance, ((0, 0), (0, SPAN - by_distance.shape[1])))
    return padded.reshape(HEADS // 2, 2, SPAN), selector


def table_grad(selector, by_distance):
    flat = by_distance.reshape(HEADS, SPAN)[:, : selector.shape[0]]
    return jnp.einsum("db,hd->bh", selector, flat, precision=HIGHEST_PRECISION)


def layers(encoder_row, decoder_row, lengths_row, target_length, buckets, gains, weights, encoder_cotangent, decoder_cotangent, encoder_table_in, decoder_table_in):
    encoder_length, feature_count = encoder_row.shape
    decoder_length = decoder_row.shape[0]
    half = encoder_length - 1
    positions = jnp.arange(encoder_length, dtype=jnp.int32)
    target_positions = jnp.arange(decoder_length, dtype=jnp.int32)
    count = lengths_row.shape[0]
    order = jnp.arange(count, dtype=jnp.int32)
    ends = jnp.sum(jnp.where(order[None, :] <= order[:, None], lengths_row[None, :], 0), axis=1)
    segment = jnp.sum((ends[None, :] <= positions[:, None]).astype(jnp.int32), axis=1)
    valid = positions < jnp.sum(lengths_row)
    target_valid = target_positions < target_length
    column = lambda code: code.astype(jnp.int32)[:, None]
    line = lambda code: code.astype(jnp.int32)[None, :]
    encoder_codes = (column(segment), line(segment))
    self_codes = (column(target_valid), line(target_valid))
    cross_codes = (column(target_valid), line(valid))
    encoder_table, selector = distance_table(encoder_table_in, buckets)
    decoder_table, unused_selector = distance_table(decoder_table_in, buckets)
    (
        first_gain,
        second_gain,
        final_gain,
        self_gain,
        cross_gain,
        third_gain,
    ) = [gains[i] for i in range(6)]
    w = weights

    residual = encoder_row.astype(jnp.float32)
    first_normed = low(rms_scale(residual, first_gain))
    queries = low(matmul(first_normed, w["eq"]))
    keys = low(matmul(first_normed, w["ek"]))
    values = low(matmul(first_normed, w["ev"]))
    attended = attn_fwd("segment", half, queries, keys, values, *encoder_codes, encoder_table)
    middle = residual + matmul(attended, w["eo"])
    second_normed = low(rms_scale(middle, second_gain))
    pre = matmul(second_normed, w["ew"])
    active = low(gelu_float(pre))
    branch = matmul(active, w["en"])
    output = middle + branch
    memory = low(rms_scale(output, final_gain))

    target = decoder_row.astype(jnp.float32)
    self_normed = low(rms_scale(target, self_gain))
    self_queries = low(matmul(self_normed, w["dq"]))
    self_keys = low(matmul(self_normed, w["dk"]))
    self_values = low(matmul(self_normed, w["dv"]))
    self_attended = attn_fwd(
        "causal", half, self_queries, self_keys, self_values, *self_codes, decoder_table
    )
    target_middle = target + matmul(self_attended, w["do"])
    cross_normed = low(rms_scale(target_middle, cross_gain))
    cross_queries = low(matmul(cross_normed, w["cq"]))
    cross_keys = low(matmul(memory, w["ck"]))
    cross_values = low(matmul(memory, w["cv"]))
    cross_attended = attn_fwd(
        "cross", half, cross_queries, cross_keys, cross_values, *cross_codes, None
    )
    crossed = target_middle + matmul(cross_attended, w["co"])
    third_normed = low(rms_scale(crossed, third_gain))
    decoder_pre = matmul(third_normed, w["dw"])
    decoder_active = low(gelu_float(decoder_pre))
    decoder_branch = matmul(decoder_active, w["dn"])
    decoder_output = crossed + decoder_branch

    grads = {}
    upstream = decoder_cotangent.astype(jnp.float32)
    normed_grad, grads["dw"], grads["dn"] = feedforward_back(
        third_normed, decoder_pre, decoder_active, w["dw"], w["dn"], upstream
    )
    part, third_gain_grad = norm_back(crossed, third_gain, normed_grad)
    crossed_grad = upstream + part

    crossed_low = low(crossed_grad)
    grads["co"] = weight_grad(cross_attended, crossed_low)
    mixed_grad = low(matmul_back(crossed_low, w["co"]))
    query_low, key_low, value_low = attn_bwd(
        "cross", half, cross_queries, cross_keys, cross_values, mixed_grad, *cross_codes, None
    )
    grads["cq"] = weight_grad(cross_normed, query_low)
    grads["ck"] = weight_grad(memory, key_low)
    grads["cv"] = weight_grad(memory, value_low)
    memory_grad = matmul_back(key_low, w["ck"]) + matmul_back(value_low, w["cv"])
    part, cross_gain_grad = norm_back(target_middle, cross_gain, matmul_back(query_low, w["cq"]))
    middle_grad = crossed_grad + part

    middle_low = low(middle_grad)
    grads["do"] = weight_grad(self_attended, middle_low)
    mixed_grad = low(matmul_back(middle_low, w["do"]))
    query_low, key_low, value_low, decoder_distance = attn_bwd(
        "causal", half, self_queries, self_keys, self_values, mixed_grad, *self_codes, decoder_table
    )
    grads["dq"] = weight_grad(self_normed, query_low)
    grads["dk"] = weight_grad(self_normed, key_low)
    grads["dv"] = weight_grad(self_normed, value_low)
    normed_grad = (
        matmul_back(query_low, w["dq"])
        + matmul_back(key_low, w["dk"])
        + matmul_back(value_low, w["dv"])
    )
    part, self_gain_grad = norm_back(target, self_gain, normed_grad)
    decoder_input_grad = middle_grad + part

    part, final_gain_grad = norm_back(output, final_gain, memory_grad)
    output_grad = encoder_cotangent.astype(jnp.float32) + part
    normed_grad, grads["ew"], grads["en"] = feedforward_back(
        second_normed, pre, active, w["ew"], w["en"], output_grad
    )
    part, second_gain_grad = norm_back(middle, second_gain, normed_grad)
    encoder_middle_grad = output_grad + part

    middle_low = low(encoder_middle_grad)
    grads["eo"] = weight_grad(attended, middle_low)
    mixed_grad = low(matmul_back(middle_low, w["eo"]))
    query_low, key_low, value_low, encoder_distance = attn_bwd(
        "segment", half, queries, keys, values, mixed_grad, *encoder_codes, encoder_table
    )
    grads["eq"] = weight_grad(first_normed, query_low)
    grads["ek"] = weight_grad(first_normed, key_low)
    grads["ev"] = weight_grad(first_normed, value_low)
    normed_grad = (
        matmul_back(query_low, w["eq"])
        + matmul_back(key_low, w["ek"])
        + matmul_back(value_low, w["ev"])
    )
    part, first_gain_grad = norm_back(residual, first_gain, normed_grad)
    encoder_input_grad = encoder_middle_grad + part

    keep = valid[:, None]
    target_keep = target_valid[:, None]
    sums = jnp.stack(
        [
            jnp.sum(jnp.where(keep, output * output, 0.0)),
            jnp.sum(jnp.where(keep, branch * branch, 0.0)),
            jnp.sum(jnp.where(target_keep, decoder_output * decoder_output, 0.0)),
            jnp.sum(jnp.where(target_keep, decoder_branch * decoder_branch, 0.0)),
            jnp.sum(valid.astype(jnp.float32)),
            jnp.sum(target_valid.astype(jnp.float32)),
        ]
    )
    small = jnp.concatenate(
        [
            first_gain_grad,
            second_gain_grad,
            final_gain_grad,
            self_gain_grad,
            cross_gain_grad,
            third_gain_grad,
            table_grad(selector, encoder_distance).reshape(-1),
            table_grad(selector, decoder_distance).reshape(-1),
            sums,
        ]
    )
    return (output, decoder_output, encoder_input_grad, decoder_input_grad, grads, small)


GROUPS = (
    (("eq", "ek"), "xyc"),
    (("ev", "eo"), "yxc"),
    (("ew",), "xyc"),
    (("en",), "yxc"),
    (("dq", "dk", "dv", "do"), "xyc"),
    (("cq", "ck", "cv", "co"), "yxc"),
    (("dw",), "xyc"),
    (("dn",), "yxc"),
)
WEIGHT_ARGS = {
    "eq": 6, "ek": 7, "ev": 8, "eo": 9, "ew": 12, "en": 13, "dq": 16, "dk": 17, "dv": 18, "do": 19,
    "cq": 22, "ck": 23, "cv": 24, "co": 25, "dw": 27, "dn": 28,
}
GAIN_ARGS = (5, 11, 14, 15, 21, 26)
WEIGHT_OUTS = {
    "eq": 5, "ek": 6, "ev": 7, "eo": 8, "ew": 11, "en": 12, "dq": 15, "dk": 16, "dv": 17, "do": 18,
    "cq": 21, "ck": 22, "cv": 23, "co": 24, "dw": 26, "dn": 27,
}
GAIN_OUTS = (4, 10, 13, 14, 20, 25)


def body(near, *args):
    row_count = lax.axis_size("rows") * lax.axis_size("seq")
    me = lax.axis_index("rows") * lax.axis_size("seq") + lax.axis_index("seq")
    seq_index = lax.axis_index("seq")
    shards = {name: args[i] for name, i in WEIGHT_ARGS.items()}
    own_gains = jnp.stack([args[i] for i in GAIN_ARGS])
    weights = {}
    if near:
        spread = jnp.zeros((6, row_count * own_gains.shape[1]), jnp.bfloat16)
        spread = lax.dynamic_update_slice_in_dim(spread, own_gains, me * own_gains.shape[1], 1)
        gains = sum_everywhere(spread)
        for names, order in GROUPS:
            weights.update(zip(names, gather_group([shards[n] for n in names], order)))
    else:
        gains = lax.all_gather(own_gains, BOTH, axis=1, tiled=True)
        for name, shard in shards.items():
            weights[name] = lax.all_gather(shard, BOTH, axis=0, tiled=True)
    encoder_row = whole_row(args[0])
    decoder_row = whole_row(args[1])
    lengths_row = lax.dynamic_index_in_dim(args[2], seq_index, 0, keepdims=False)
    target_length = lax.dynamic_index_in_dim(args[3], seq_index, 0, keepdims=False)
    output, decoder_output, encoder_input_grad, decoder_input_grad, grads, small = layers(
        encoder_row,
        decoder_row,
        lengths_row,
        target_length,
        args[4],
        gains.astype(jnp.float32),
        weights,
        whole_row(args[29]),
        whole_row(args[30]),
        args[10],
        args[20],
    )
    outs = [None] * 29
    for i, value in enumerate((output, decoder_output, encoder_input_grad, decoder_input_grad)):
        outs[i] = own_slots(value)
    reduced = {}
    if near:
        for names, order in reversed(GROUPS):
            reduced.update(zip(names, reduce_group([grads[n] for n in names], order)))
        small = sum_everywhere(small)
    else:
        for name, grad in grads.items():
            reduced[name] = lax.psum_scatter(
                grad.astype(jnp.float32), BOTH, scatter_dimension=0, tiled=True
            )
        small = lax.psum(small, BOTH)
    for name, i in WEIGHT_OUTS.items():
        outs[i] = reduced[name]
    feature_count = args[0].shape[2]
    share = feature_count // row_count
    for number, i in enumerate(GAIN_OUTS):
        outs[i] = lax.dynamic_slice_in_dim(small, number * feature_count + me * share, share)
    offset = 6 * feature_count
    size = BUCKETS * HEADS
    outs[9] = small[offset : offset + size].reshape(BUCKETS, HEADS)
    outs[19] = small[offset + size : offset + 2 * size].reshape(BUCKETS, HEADS)
    sums = small[offset + 2 * size :]
    divisors = jnp.stack([sums[4], sums[4], sums[5], sums[5]]) * feature_count
    outs[28] = jnp.sqrt(sums[:4] / divisors)
    return tuple(outs)


def solution(mesh):
    row_spec = P("rows", "seq", None)
    matrix = P(BOTH, None)
    vector = P(BOTH)
    in_specs = [row_spec, row_spec, P("rows", None), P("rows"), P()] + [None] * 26
    in_specs[10] = in_specs[20] = P()
    in_specs[29] = in_specs[30] = row_spec
    for i in GAIN_ARGS:
        in_specs[i] = vector
    for i in WEIGHT_ARGS.values():
        in_specs[i] = matrix
    out_specs = [row_spec] * 4 + [None] * 25
    out_specs[9] = out_specs[19] = out_specs[28] = P()
    for i in GAIN_OUTS:
        out_specs[i] = vector
    for i in WEIGHT_OUTS.values():
        out_specs[i] = matrix
    near = mesh.shape["rows"] == 4 * CHAIN and mesh.shape["seq"] == 2
    return jax.shard_map(
        functools.partial(body, near),
        mesh=mesh,
        in_specs=tuple(in_specs),
        out_specs=tuple(out_specs),
        check_vma=False,
    )
```

time: 3130 us -> 1920 us (0.61)
  waiting for transfers between devices: 2040 us -> 232 us
  Pallas kernels: 0 us -> 1090 us
  local copies, waits for them, and re-layouts: 698 us -> 85.1 us
  starting transfers between devices: 2.4 us -> 325 us
  matrix products: 228 us -> 114 us
  blocking collectives: 97.6 us -> 0 us
    reduce_scatter x20 -> x0, waiting for transfers between devices: 1720 us -> none  [the longest x16 1700 us: reduce_weights(): lax.psum_scatter(grads, ('rows', 'seq'), scatter_dimension=0, tiled=True)]
    pallas_call x0 -> x14, Pallas kernels: none -> 1090 us  [the longest x8 1010 us: assemble(): pl.pallas_call(functools.partial(assemble_kernel, count, shifts), out_sha...]
    gather x3 -> x0, local copies, waits for them, and re-layouts: 554 us -> none  [position_bias(): bucket_index = jnp.take(buckets, distance_index, axis=0)]
    ppermute x0 -> x194, starting transfers between devices: none -> 325 us  [the longest x96 250 us: shift(): return lax.ppermute(value, BOTH, pairs)]
    all_gather x20 -> x0, waiting for transfers between devices: 305 us -> none  [the longest x16 253 us: gather_weights(): lax.all_gather(as_sent(shards), ('rows', 'seq'), axis=0, tiled=True)]
    ppermute x0 -> x194, waiting for transfers between devices: none -> 232 us  [the longest x80 142 us: swap(): return lax.ppermute(value, BOTH, pairs)]
    dot_general x94 -> x52, matrix products: 228 us -> 114 us  [the longest x32 71.9 us: dotf(): return lax.dot_general(a, b, dims, preferred_element_type=jnp.float32)]
    unnamed x2 -> x0, blocking collectives: 82.5 us -> none
  transfers between devices with their start and end apart: 41 -> 194, of which waited for: 25 -> 57; matrix products, arithmetic and copies ran while one was open for 29% -> 8% of each run, Pallas kernels for 0% -> 47%
where the time goes in v1:
time: 1920 us; the launch traced here: 1910 us
  Pallas kernels  1090 us (57%)
  starting transfers between devices  325 us (17%)
  waiting for transfers between devices  232 us (12%)
  matrix products  114 us (6%)
  local copies, waits for them, and re-layouts  85.1 us (4%)
  other arithmetic  55.2 us (3%)
    pallas_call x8, Pallas kernels, assemble(): pl.pallas_call(functools.partial(assemble_kernel, count, shifts), out_sha...  1010 us
    ppermute x96, starting transfers between devices, shift(): return lax.ppermute(value, BOTH, pairs)  250 us
    ppermute x80, waiting for transfers between devices, swap(): return lax.ppermute(value, BOTH, pairs)  142 us
    pallas_call x6, Pallas kernels, attn(): pl.pallas_call(functools.partial(kernel, mode, half), grid=(width // 128,...  77.9 us
    dot_general x32, matrix products, dotf(): return lax.dot_general(a, b, dims, preferred_element_type=jnp.float32)  71.9 us
    ppermute x96, waiting for transfers between devices, shift(): return lax.ppermute(value, BOTH, pairs)  69.7 us
    ppermute x80, starting transfers between devices, swap(): return lax.ppermute(value, BOTH, pairs)  54 us
    dot_general x16, matrix products, matmul(): return jnp.dot(left, right, preferred_element_type=jnp.float32)  39 us
  transfers between devices with their start and end apart: 194, of which 57 were waited for; matrix products, arithmetic and copies ran while one was open for 8% of the time, Pallas kernels for 47%

profile of v1, /device:TPU:0, one launch (start us, length us, event | category | flops | bytes accessed | tf_op | source)
XLA Modules:
  0.0 1905.5 jit_solution(3021332433148899609)
XLA Ops:
  2.4 5.6 collective-permute-start.19
  11.9 5.2 collective-permute-start.6
  45.0 4.5 collective-permute-done.59
  65.3 6.4 collective-permute-start.32
  81.0 4.6 collective-permute-start.86
  86.9 4.6 collective-permute-start.45
  94.2 4.6 collective-permute-start.73
  100.1 4.6 collective-permute-start.60
  130.7 11.4 collective-permute-start.77
  166.3 5.6 collective-permute-done.78
  191.8 8.0 collective-permute-done.66
  203.2 8.6 collective-permute-done.38.refs_1_
  224.9 72.7 %shard_map.519 = (bf16[4,8,24,768]{3,2,1,0:T(8,128)(2,1)}, bf16[4,8,24,768]{3,2,1,0:T(8,128)(2,1)}) custom-call(bf16[2,4,24,768]{3,2,1,0:T(8,128)(2,1)} %copy-done.83, bf16[2,4,24,768]{3,2,1,0:T(8,128)(2,1)} %copy-done.117, bf16[2,4,24,768]{3,2,1,0:T(8,128)(2,1)} %copy-done.118, bf16[2,4,24,768]{3,2,1,0:T(8,128)(2,1)} %copy-done.120, ...), custom_call_target="tpu_custom_call" | custom-call | bytes 4718592 | tf_op jit(solution)/shard_map/pallas_call | solution.py:152
  301.1 72.7 %shard_map.518 = (bf16[4,8,24,768]{3,2,1,0:T(8,128)(2,1)}, bf16[4,8,24,768]{3,2,1,0:T(8,128)(2,1)}) custom-call(bf16[2,4,24,768]{3,2,1,0:T(8,128)(2,1)} %copy.174.refs_0_, bf16[2,4,24,768]{3,2,1,0:T(8,128)(2,1)} %copy.175.refs_1_, bf16[2,4,24,768]{3,2,1,0:T(8,128)(2,1)} %copy.176.refs_2_, bf16[2,4,24,768]{3,2,1,0:T(8,128)(2,1)} %copy.177.refs_3_, ...), custom_call_target="tpu_custom_call" | custom-call | bytes 4718592 | tf_op jit(solution)/shard_map/pallas_call | solution.py:152
  379.1 21.7 %shard_map.520 = bf16[512,768]{1,0:T(8,128)(2,1)S(1)} custom-call(bf16[512,768]{1,0:T(8,128)(2,1)S(1)} %convolution_convert_fusion.21.refs_0_, bf16[512,768]{1,0:T(8,128)(2,1)S(1)} %convolution_convert_fusion.20.refs_1_, bf16[512,768]{1,0:T(8,128)(2,1)S(1)} %convolution_convert_fusion.19.refs_2_, s32[512,1]{1,0:T(8,128)S(1)} %copy.185.refs_3_.refs_4_, ...), custom_call_target="tpu_custom_call" | custom-call | tf_op jit(solution)/shard_map/pallas_call | solution.py:84
  410.8 144.3 %shard_map.523 = (bf16[4,8,24,768]{3,2,1,0:T(8,128)(2,1)}, bf16[4,8,24,768]{3,2,1,0:T(8,128)(2,1)}, bf16[4,8,24,768]{3,2,1,0:T(8,128)(2,1)}, bf16[4,8,24,768]{3,2,1,0:T(8,128)(2,1)}) custom-call(bf16[4,4,24,768]{3,2,1,0:T(8,128)(2,1)} %copy.186.refs_0_, bf16[4,4,24,768]{3,2,1,0:T(8,128)(2,1)} %copy.187.refs_1_, bf16[4,4,24,768]{3,2,1,0:T(8,128)(2,1)} %copy.188.refs_2_, ...), custom_call_target="tpu_custom_call" | custom-call | bytes 9437184 | tf_op jit(solution)/shard_map/pallas_call | solution.py:152
  560.1 144.1 %shard_map.521 = bf16[4,8,24,3072]{3,2,1,0:T(8,128)(2,1)} custom-call(bf16[1,4,24,3072]{3,2,1,0:T(8,128)(2,1)} %pad_maximum_fusion.7.refs_0_, bf16[1,4,24,3072]{3,2,1,0:T(8,128)(2,1)} %collective-permute-done.38.refs_1_, bf16[1,4,24,3072]{3,2,1,0:T(8,128)(2,1)} %collective-permute-done.39.refs_2_, bf16[1,4,24,3072]{3,2,1,0:T(8,128)(2,1)} %collective-permute-done.40.refs_3_, ...), custom_call_target="tpu_custom_call" | custom-call | bytes 9437184 | tf_op jit(solution)/shard_map/pallas_call | solution.py:152
  709.2 6.9 fusion.141
  717.2 7.0 collective-permute-done.81.refs_3_
  724.8 144.1 %shard_map.522 = bf16[4,8,96,768]{3,2,1,0:T(8,128)(2,1)} custom-call(bf16[1,4,96,768]{3,2,1,0:T(8,128)(2,1)} %pad_maximum_fusion.8.refs_0_, bf16[1,4,96,768]{3,2,1,0:T(8,128)(2,1)} %collective-permute-done.51.refs_1_, bf16[1,4,96,768]{3,2,1,0:T(8,128)(2,1)} %collective-permute-done.52.refs_2_, bf16[1,4,96,768]{3,2,1,0:T(8,128)(2,1)} %collective-permute-done.53.refs_3_, ...), custom_call_target="tpu_custom_call" | custom-call | bytes 9437184 | tf_op jit(solution)/shard_map/pallas_call | solution.py:152
  868.9 9.2 multiply_reduce_fusion.5
  878.2 5.8 shard_map.524
  891.8 144.4 %shard_map.525 = (bf16[4,8,24,768]{3,2,1,0:T(8,128)(2,1)}, bf16[4,8,24,768]{3,2,1,0:T(8,128)(2,1)}, bf16[4,8,24,768]{3,2,1,0:T(8,128)(2,1)}, bf16[4,8,24,768]{3,2,1,0:T(8,128)(2,1)}) custom-call(bf16[4,4,24,768]{3,2,1,0:T(8,128)(2,1)} %pad_maximum_fusion.10.refs_0_, bf16[4,4,24,768]{3,2,1,0:T(8,128)(2,1)} %collective-permute-done.79.refs_1_, ...), custom_call_target="tpu_custom_call" | custom-call | bytes 9437184 | tf_op jit(solution)/shard_map/pallas_call | solution.py:152
  1041.3 6.2 shard_map.526
  1050.3 5.1 collective-permute-done.107.refs_3_
  1056.1 144.1 %shard_map.527 = bf16[4,8,24,3072]{3,2,1,0:T(8,128)(2,1)} custom-call(bf16[1,4,24,3072]{3,2,1,0:T(8,128)(2,1)} %pad_maximum_fusion.11.refs_0_, bf16[1,4,24,3072]{3,2,1,0:T(8,128)(2,1)} %collective-permute-done.92.refs_1_, bf16[1,4,24,3072]{3,2,1,0:T(8,128)(2,1)} %collective-permute-done.93.refs_2_, bf16[1,4,24,3072]{3,2,1,0:T(8,128)(2,1)} %collective-permute-done.94.refs_3_, ...), custom_call_target="tpu_custom_call" | custom-call | bytes 9437184 | tf_op jit(solution)/shard_map/pallas_call | solution.py:152
  1207.4 144.1 %shard_map.528 = bf16[4,8,96,768]{3,2,1,0:T(8,128)(2,1)} custom-call(bf16[1,4,96,768]{3,2,1,0:T(8,128)(2,1)} %pad_maximum_fusion.12.refs_0_, bf16[1,4,96,768]{3,2,1,0:T(8,128)(2,1)} %collective-permute-done.105.refs_1_, bf16[1,4,96,768]{3,2,1,0:T(8,128)(2,1)} %collective-permute-done.106.refs_2_, bf16[1,4,96,768]{3,2,1,0:T(8,128)(2,1)} %collective-permute-done.107.refs_3_, ...), custom_call_target="tpu_custom_call" | custom-call | bytes 9437184 | tf_op jit(solution)/shard_map/pallas_call | solution.py:152
  1351.6 4.8 fusion.27
  1356.5 4.9 multiply_reduce_fusion.6
  1368.5 9.0 shard_map.529
  1386.9 9.8 shard_map.531
  1403.1 7.9 fusion.6
  1411.0 5.5 convolution_convert_fusion.2
  1419.4 4.5 convolution_convert_fusion.3
  1428.2 25.5 %shard_map.530 = (bf16[512,768]{1,0:T(8,128)(2,1)S(1)}, bf16[512,768]{1,0:T(8,128)(2,1)S(1)}, bf16[512,768]{1,0:T(8,128)(2,1)S(1)}, f32[6,2,1024]{2,1,0:T(2,128)S(1)}) custom-call(bf16[512,768]{1,0:T(8,128)(2,1)S(1)} %copy-done.5, bf16[512,768]{1,0:T(8,128)(2,1)S(1)} %copy-done.3, bf16[512,768]{1,0:T(8,128)(2,1)S(1)} %convolution_convert_fusion.19.refs_2_, ...), custom_call_target="tpu_custom_call" | custom-call | tf_op jit(solution)/shard_map/pallas_call | solution.py:84
  1477.1 4.3 constant_dynamic-slice_fusion.1
  1536.5 9.2 collective-permute-done.112
  1569.7 8.4 collective-permute-done.132
  1582.0 5.3 collective-permute-done.133
  1591.8 4.3 collective-permute-start.125
  1598.0 4.3 collective-permute-start.135
  1610.9 4.4 collective-permute-start.136
  1617.4 8.2 collective-permute-start.127
  1648.0 16.8 collective-permute-done.186
  1669.2 21.0 %collective-permute-done.168 = bf16[4,4,2,24,768]{4,3,0,1,2:T(8,128)(2,1)S(1)} collective-permute-done((bf16[4,4,2,24,768]{4,3,0,1,2:T(8,128)(2,1)S(1)}, bf16[4,4,2,24,768]{4,3,0,1,2:T(8,128)(2,1)S(1)}, u32[]{:S(2)}, u32[]{:S(2)}) %collective-permute-start.168) | collective-permute-done | bytes 1179680 | tf_op jit(solution)/shard_map/ppermute | solution.py:108
  1694.4 21.1 %collective-permute-done.150 = bf16[1,4,2,96,768]{4,3,1,2,0:T(8,128)(2,1)S(1)} collective-permute-done((bf16[1,4,2,96,768]{4,3,1,2,0:T(8,128)(2,1)S(1)}, bf16[1,4,2,96,768]{4,3,1,2,0:T(8,128)(2,1)S(1)}, u32[]{:S(2)}, u32[]{:S(2)}) %collective-permute-start.150) | collective-permute-done | bytes 1179680 | tf_op jit(solution)/shard_map/ppermute | solution.py:108
  1719.7 10.9 collective-permute-done.187
  1735.8 7.5 collective-permute-done.169
  1744.2 8.2 collective-permute-done.142
  1759.8 4.4 collective-permute-start.143
  1767.5 4.4 collective-permute-start.161
  1774.6 4.4 collective-permute-start.152
  1782.7 4.4 collective-permute-start.180
  1790.6 4.4 collective-permute-start.144
  1797.7 4.4 collective-permute-start.189
  1815.8 7.6 collective-permute-start.190
  1824.2 4.4 collective-permute-start.181
  1828.7 6.2 collective-permute-start.174
  1835.7 14.6 collective-permute-start.172
  1851.1 8.7 collective-permute-start.163
  1862.0 11.5 collective-permute-start.154
  1876.9 4.5 collective-permute-start.145
  1884.0 7.4 collective-permute-start.166
  1894.0 4.4 collective-permute-done.166
  (1040 shorter events, 452.1 us)
Async XLA Ops:
  2.4 47.7 %collective-permute-start.19 = (bf16[2,24,768]{2,1,0:T(8,128)(2,1)}, bf16[2,24,768]{2,1,0:T(8,128)(2,1)}, u32[]{:S(2)}, u32[]{:S(2)}) collective-permute-start(bf16[2,24,768]{2,1,0:T(8,128)(2,1)} %pad_maximum_fusion.22), channel_id=1, source_target_pairs={{0,8},{1,9},{2,10},{3,11},{4,12},{5,13},{6,14},{7,15},{8,16},{9,17... | collective-permute-start | bytes 221192 | tf_op jit(solution)/shard_map/ppermute | solution.py:116
  7.9 44.1 %collective-permute-start.22 = (bf16[2,24,768]{2,1,0:T(8,128)(2,1)}, bf16[2,24,768]{2,1,0:T(8,128)(2,1)}, u32[]{:S(2)}, u32[]{:S(2)}) collective-permute-start(bf16[2,24,768]{2,1,0:T(8,128)(2,1)} %pad_maximum_fusion.22), channel_id=1, source_target_pairs={{8,0},{9,1},{10,2},{11,3},{12,4},{13,5},{14,6},{15,7},{16,8},{17,9... | collective-permute-start | bytes 221192 | tf_op jit(solution)/shard_map/ppermute | solution.py:116
  10.6 42.1 %collective-permute-start.9 = (bf16[2,24,768]{2,1,0:T(8,128)(2,1)}, bf16[2,24,768]{2,1,0:T(8,128)(2,1)S(1)}, u32[]{:S(2)}, u32[]{:S(2)}) collective-permute-start(bf16[2,24,768]{2,1,0:T(8,128)(2,1)} %pad_maximum_fusion.21), channel_id=1, source_target_pairs={{8,0},{9,1},{10,2},{11,3},{12,4},{13,5},{14,6},{15,7},{16,8},{17,9... | collective-permute-start | bytes 221192 | tf_op jit(solution)/shard_map/ppermute | solution.py:116
  11.9 42.1 %collective-permute-start.6 = (bf16[2,24,768]{2,1,0:T(8,128)(2,1)}, bf16[2,24,768]{2,1,0:T(8,128)(2,1)S(1)}, u32[]{:S(2)}, u32[]{:S(2)}) collective-permute-start(bf16[2,24,768]{2,1,0:T(8,128)(2,1)} %pad_maximum_fusion.21), channel_id=1, source_target_pairs={{0,8},{1,9},{2,10},{3,11},{4,12},{5,13},{6,14},{7,15},{8,16},{9,17... | collective-permute-start | bytes 221192 | tf_op jit(solution)/shard_map/ppermute | solution.py:116
  50.0 30.9 %collective-permute-start.99 = (bf16[1,96,768]{2,1,0:T(8,128)(2,1)S(1)}, bf16[1,96,768]{2,1,0:T(8,128)(2,1)S(1)}, u32[]{:S(2)}, u32[]{:S(2)}) collective-permute-start(bf16[1,96,768]{2,1,0:T(8,128)(2,1)S(1)} %bitcast.739), channel_id=1, source_target_pairs={{0,8},{1,9},{2,10},{3,11},{4,12},{5,13},{6,14},{7,15},{8,16},{9,17... | collective-permute-start | bytes 442376 | tf_op jit(solution)/shard_map/ppermute | solution.py:116
  199.9 97.8 %collective-permute-start.68 = (bf16[4,4,24,768]{3,2,0,1:T(8,128)(2,1)S(1)}, bf16[4,4,24,768]{3,2,0,1:T(8,128)(2,1)}, u32[]{:S(2)}, u32[]{:S(2)}) collective-permute-start(bf16[4,4,24,768]{3,2,0,1:T(8,128)(2,1)S(1)} %collective-permute-done.66), channel_id=1, source_target_pairs={{0,1},{1,0},{2,3},{3,2},{4,5},{5,4},{6,7},{7,6},{8,9},{9,8},{10,11... | collective-permute-start | bytes 1769480 | tf_op jit(solution)/shard_map/ppermute | solution.py:108
  212.8 163.3 %collective-permute-start.39 = (bf16[1,4,24,3072]{3,2,1,0:T(8,128)(2,1)}, bf16[1,4,24,3072]{3,2,1,0:T(8,128)(2,1)}, u32[]{:S(2)}, u32[]{:S(2)}) collective-permute-start(bf16[1,4,24,3072]{3,2,1,0:T(8,128)(2,1)} %pad_maximum_fusion.7.refs_0_), channel_id=1, source_target_pairs={{0,1},{1,0},{2,3},{3,2},{4,5},{5,4},{6,7},{7,6},{8,9},{9,8},{10,11... | collective-permute-start | bytes 1769480 | tf_op jit(solution)/shard_map/ppermute | solution.py:108
  214.4 163.4 %collective-permute-start.70 = (bf16[4,4,24,768]{3,2,0,1:T(8,128)(2,1)S(1)}, bf16[4,4,24,768]{3,2,0,1:T(8,128)(2,1)}, u32[]{:S(2)}, u32[]{:S(2)}) collective-permute-start(bf16[4,4,24,768]{3,2,0,1:T(8,128)(2,1)S(1)} %collective-permute-done.66), channel_id=1, source_target_pairs={{0,2},{1,3},{2,0},{3,1},{4,6},{5,7},{6,4},{7,5},{8,10},{9,11},{10,... | collective-permute-start | bytes 1769480 | tf_op jit(solution)/shard_map/ppermute | solution.py:108
  214.6 161.6 %collective-permute-start.40 = (bf16[1,4,24,3072]{3,2,1,0:T(8,128)(2,1)}, bf16[1,4,24,3072]{3,2,1,0:T(8,128)(2,1)}, u32[]{:S(2)}, u32[]{:S(2)}) collective-permute-start(bf16[1,4,24,3072]{3,2,1,0:T(8,128)(2,1)} %collective-permute-done.38.refs_1_), channel_id=1, source_target_pairs={{0,1},{1,0},{2,3},{3,2},{4,5},{5,4},{6,7},{7,6},{8,9},{9,8},{10,11... | collective-permute-start | bytes 1769480 | tf_op jit(solution)/shard_map/ppermute | solution.py:108
  215.1 162.8 %collective-permute-start.71 = (bf16[4,4,24,768]{3,2,0,1:T(8,128)(2,1)}, bf16[4,4,24,768]{3,2,0,1:T(8,128)(2,1)}, u32[]{:S(2)}, u32[]{:S(2)}) collective-permute-start(bf16[4,4,24,768]{3,2,0,1:T(8,128)(2,1)} %collective-permute-done.67), channel_id=1, source_target_pairs={{0,2},{1,3},{2,0},{3,1},{4,6},{5,7},{6,4},{7,5},{8,10},{9,11},{10,... | collective-permute-start | bytes 1769480 | tf_op jit(solution)/shard_map/ppermute | solution.py:108
  297.7 103.2 %collective-permute-start.72 = (bf16[4,4,24,768]{3,2,0,1:T(8,128)(2,1)}, bf16[4,4,24,768]{3,2,0,1:T(8,128)(2,1)}, u32[]{:S(2)}, u32[]{:S(2)}) collective-permute-start(bf16[4,4,24,768]{3,2,0,1:T(8,128)(2,1)} %collective-permute-done.68), channel_id=1, source_target_pairs={{0,2},{1,3},{2,0},{3,1},{4,6},{5,7},{6,4},{7,5},{8,10},{9,11},{10,... | collective-permute-start | bytes 1769480 | tf_op jit(solution)/shard_map/ppermute | solution.py:108
  376.1 179.0 %collective-permute-start.41 = (bf16[1,4,24,3072]{3,2,1,0:T(8,128)(2,1)}, bf16[1,4,24,3072]{3,2,1,0:T(8,128)(2,1)}, u32[]{:S(2)}, u32[]{:S(2)}) collective-permute-start(bf16[1,4,24,3072]{3,2,1,0:T(8,128)(2,1)} %pad_maximum_fusion.7.refs_0_), channel_id=1, source_target_pairs={{0,2},{1,3},{2,0},{3,1},{4,6},{5,7},{6,4},{7,5},{8,10},{9,11},{10,... | collective-permute-start | bytes 1769480 | tf_op jit(solution)/shard_map/ppermute | solution.py:108
  376.2 179.5 %collective-permute-start.51 = (bf16[1,4,96,768]{3,2,1,0:T(8,128)(2,1)}, bf16[1,4,96,768]{3,2,1,0:T(8,128)(2,1)}, u32[]{:S(2)}, u32[]{:S(2)}) collective-permute-start(bf16[1,4,96,768]{3,2,1,0:T(8,128)(2,1)} %pad_maximum_fusion.8.refs_0_), channel_id=1, source_target_pairs={{0,1},{1,0},{2,3},{3,2},{4,5},{5,4},{6,7},{7,6},{8,9},{9,8},{10,11... | collective-permute-start | bytes 1769480 | tf_op jit(solution)/shard_map/ppermute | solution.py:108
  377.7 178.1 %collective-permute-start.42 = (bf16[1,4,24,3072]{3,2,1,0:T(8,128)(2,1)}, bf16[1,4,24,3072]{3,2,1,0:T(8,128)(2,1)}, u32[]{:S(2)}, u32[]{:S(2)}) collective-permute-start(bf16[1,4,24,3072]{3,2,1,0:T(8,128)(2,1)} %collective-permute-done.38.refs_1_), channel_id=1, source_target_pairs={{0,2},{1,3},{2,0},{3,1},{4,6},{5,7},{6,4},{7,5},{8,10},{9,11},{10,... | collective-permute-start | bytes 1769480 | tf_op jit(solution)/shard_map/ppermute | solution.py:108
  377.9 178.5 %collective-permute-start.43 = (bf16[1,4,24,3072]{3,2,1,0:T(8,128)(2,1)}, bf16[1,4,24,3072]{3,2,1,0:T(8,128)(2,1)}, u32[]{:S(2)}, u32[]{:S(2)}) collective-permute-start(bf16[1,4,24,3072]{3,2,1,0:T(8,128)(2,1)} %collective-permute-done.39.refs_2_), channel_id=1, source_target_pairs={{0,2},{1,3},{2,0},{3,1},{4,6},{5,7},{6,4},{7,5},{8,10},{9,11},{10,... | collective-permute-start | bytes 1769480 | tf_op jit(solution)/shard_map/ppermute | solution.py:108
  400.9 158.6 %collective-permute-start.44 = (bf16[1,4,24,3072]{3,2,1,0:T(8,128)(2,1)}, bf16[1,4,24,3072]{3,2,1,0:T(8,128)(2,1)}, u32[]{:S(2)}, u32[]{:S(2)}) collective-permute-start(bf16[1,4,24,3072]{3,2,1,0:T(8,128)(2,1)} %collective-permute-done.40.refs_3_), channel_id=1, source_target_pairs={{0,2},{1,3},{2,0},{3,1},{4,6},{5,7},{6,4},{7,5},{8,10},{9,11},{10,... | collective-permute-start | bytes 1769480 | tf_op jit(solution)/shard_map/ppermute | solution.py:108
  555.1 152.1 %collective-permute-start.52 = (bf16[1,4,96,768]{3,2,1,0:T(8,128)(2,1)}, bf16[1,4,96,768]{3,2,1,0:T(8,128)(2,1)}, u32[]{:S(2)}, u32[]{:S(2)}) collective-permute-start(bf16[1,4,96,768]{3,2,1,0:T(8,128)(2,1)} %pad_maximum_fusion.8.refs_0_), channel_id=1, source_target_pairs={{0,4},{1,5},{2,6},{3,7},{4,0},{5,1},{6,2},{7,3},{8,12},{9,13},{10,... | collective-permute-start | bytes 1769480 | tf_op jit(solution)/shard_map/ppermute | solution.py:108
  555.7 151.5 %collective-permute-start.54 = (bf16[1,4,96,768]{3,2,1,0:T(8,128)(2,1)}, bf16[1,4,96,768]{3,2,1,0:T(8,128)(2,1)}, u32[]{:S(2)}, u32[]{:S(2)}) collective-permute-start(bf16[1,4,96,768]{3,2,1,0:T(8,128)(2,1)} %pad_maximum_fusion.8.refs_0_), channel_id=1, source_target_pairs={{0,2},{1,3},{2,0},{3,1},{4,6},{5,7},{6,4},{7,5},{8,10},{9,11},{10,... | collective-permute-start | bytes 1769480 | tf_op jit(solution)/shard_map/ppermute | solution.py:108
  555.8 152.0 %collective-permute-start.79 = (bf16[4,4,24,768]{3,2,1,0:T(8,128)(2,1)S(1)}, bf16[4,4,24,768]{3,2,1,0:T(8,128)(2,1)}, u32[]{:S(2)}, u32[]{:S(2)}) collective-permute-start(bf16[4,4,24,768]{3,2,1,0:T(8,128)(2,1)S(1)} %copy-done.70), channel_id=1, source_target_pairs={{0,1},{1,0},{2,3},{3,2},{4,5},{5,4},{6,7},{7,6},{8,9},{9,8},{10,11... | collective-permute-start | bytes 1769480 | tf_op jit(solution)/shard_map/ppermute | solution.py:108
  556.4 152.9 %collective-permute-start.53 = (bf16[1,4,96,768]{3,2,1,0:T(8,128)(2,1)}, bf16[1,4,96,768]{3,2,1,0:T(8,128)(2,1)}, u32[]{:S(2)}, u32[]{:S(2)}) collective-permute-start(bf16[1,4,96,768]{3,2,1,0:T(8,128)(2,1)} %collective-permute-done.51.refs_1_), channel_id=1, source_target_pairs={{0,4},{1,5},{2,6},{3,7},{4,0},{5,1},{6,2},{7,3},{8,12},{9,13},{10,... | collective-permute-start | bytes 1769480 | tf_op jit(solution)/shard_map/ppermute | solution.py:108
  559.5 156.7 %collective-permute-start.80 = (bf16[4,4,24,768]{3,2,1,0:T(8,128)(2,1)S(1)}, bf16[4,4,24,768]{3,2,1,0:T(8,128)(2,1)}, u32[]{:S(2)}, u32[]{:S(2)}) collective-permute-start(bf16[4,4,24,768]{3,2,1,0:T(8,128)(2,1)S(1)} %copy-done.70), channel_id=1, source_target_pairs={{0,4},{1,5},{2,6},{3,7},{4,0},{5,1},{6,2},{7,3},{8,12},{9,13},{10,... | collective-permute-start | bytes 1769480 | tf_op jit(solution)/shard_map/ppermute | solution.py:108
  716.2 171.6 %collective-permute-start.82 = (bf16[4,4,24,768]{3,2,1,0:T(8,128)(2,1)S(1)}, bf16[4,4,24,768]{3,2,1,0:T(8,128)(2,1)}, u32[]{:S(2)}, u32[]{:S(2)}) collective-permute-start(bf16[4,4,24,768]{3,2,1,0:T(8,128)(2,1)S(1)} %copy-done.70), channel_id=1, source_target_pairs={{0,2},{1,3},{2,0},{3,1},{4,6},{5,7},{6,4},{7,5},{8,10},{9,11},{10,... | collective-permute-start | bytes 1769480 | tf_op jit(solution)/shard_map/ppermute | solution.py:108
  716.7 169.6 %collective-permute-start.92 = (bf16[1,4,24,3072]{3,2,1,0:T(8,128)(2,1)}, bf16[1,4,24,3072]{3,2,1,0:T(8,128)(2,1)}, u32[]{:S(2)}, u32[]{:S(2)}) collective-permute-start(bf16[1,4,24,3072]{3,2,1,0:T(8,128)(2,1)} %pad_maximum_fusion.11.refs_0_), channel_id=1, source_target_pairs={{0,4},{1,5},{2,6},{3,7},{4,0},{5,1},{6,2},{7,3},{8,12},{9,13},{10,... | collective-permute-start | bytes 1769480 | tf_op jit(solution)/shard_map/ppermute | solution.py:108
  717.2 172.0 %collective-permute-start.83 = (bf16[4,4,24,768]{3,2,1,0:T(8,128)(2,1)}, bf16[4,4,24,768]{3,2,1,0:T(8,128)(2,1)}, u32[]{:S(2)}, u32[]{:S(2)}) collective-permute-start(bf16[4,4,24,768]{3,2,1,0:T(8,128)(2,1)} %collective-permute-done.79.refs_1_), channel_id=1, source_target_pairs={{0,2},{1,3},{2,0},{3,1},{4,6},{5,7},{6,4},{7,5},{8,10},{9,11},{10,... | collective-permute-start | bytes 1769480 | tf_op jit(solution)/shard_map/ppermute | solution.py:108
  724.3 165.5 %collective-permute-start.84 = (bf16[4,4,24,768]{3,2,1,0:T(8,128)(2,1)}, bf16[4,4,24,768]{3,2,1,0:T(8,128)(2,1)}, u32[]{:S(2)}, u32[]{:S(2)}) collective-permute-start(bf16[4,4,24,768]{3,2,1,0:T(8,128)(2,1)} %collective-permute-done.80.refs_2_), channel_id=1, source_target_pairs={{0,2},{1,3},{2,0},{3,1},{4,6},{5,7},{6,4},{7,5},{8,10},{9,11},{10,... | collective-permute-start | bytes 1769480 | tf_op jit(solution)/shard_map/ppermute | solution.py:108
  724.3 167.6 %collective-permute-start.85 = (bf16[4,4,24,768]{3,2,1,0:T(8,128)(2,1)}, bf16[4,4,24,768]{3,2,1,0:T(8,128)(2,1)}, u32[]{:S(2)}, u32[]{:S(2)}) collective-permute-start(bf16[4,4,24,768]{3,2,1,0:T(8,128)(2,1)} %collective-permute-done.81.refs_3_), channel_id=1, source_target_pairs={{0,2},{1,3},{2,0},{3,1},{4,6},{5,7},{6,4},{7,5},{8,10},{9,11},{10,... | collective-permute-start | bytes 1769480 | tf_op jit(solution)/shard_map/ppermute | solution.py:108
  886.2 153.0 %collective-permute-start.105 = (bf16[1,4,96,768]{3,2,1,0:T(8,128)(2,1)}, bf16[1,4,96,768]{3,2,1,0:T(8,128)(2,1)}, u32[]{:S(2)}, u32[]{:S(2)}) collective-permute-start(bf16[1,4,96,768]{3,2,1,0:T(8,128)(2,1)} %pad_maximum_fusion.12.refs_0_), channel_id=1, source_target_pairs={{0,1},{1,0},{2,3},{3,2},{4,5},{5,4},{6,7},{7,6},{8,9},{9,8},{10,11... | collective-permute-start | bytes 1769480 | tf_op jit(solution)/shard_map/ppermute | solution.py:108
  887.8 152.0 %collective-permute-start.106 = (bf16[1,4,96,768]{3,2,1,0:T(8,128)(2,1)}, bf16[1,4,96,768]{3,2,1,0:T(8,128)(2,1)}, u32[]{:S(2)}, u32[]{:S(2)}) collective-permute-start(bf16[1,4,96,768]{3,2,1,0:T(8,128)(2,1)} %pad_maximum_fusion.12.refs_0_), channel_id=1, source_target_pairs={{0,4},{1,5},{2,6},{3,7},{4,0},{5,1},{6,2},{7,3},{8,12},{9,13},{10,... | collective-permute-start | bytes 1769480 | tf_op jit(solution)/shard_map/ppermute | solution.py:108
  889.3 151.1 %collective-permute-start.93 = (bf16[1,4,24,3072]{3,2,1,0:T(8,128)(2,1)}, bf16[1,4,24,3072]{3,2,1,0:T(8,128)(2,1)}, u32[]{:S(2)}, u32[]{:S(2)}) collective-permute-start(bf16[1,4,24,3072]{3,2,1,0:T(8,128)(2,1)} %pad_maximum_fusion.11.refs_0_), channel_id=1, source_target_pairs={{0,1},{1,0},{2,3},{3,2},{4,5},{5,4},{6,7},{7,6},{8,9},{9,8},{10,11... | collective-permute-start | bytes 1769480 | tf_op jit(solution)/shard_map/ppermute | solution.py:108
  889.8 150.6 %collective-permute-start.94 = (bf16[1,4,24,3072]{3,2,1,0:T(8,128)(2,1)}, bf16[1,4,24,3072]{3,2,1,0:T(8,128)(2,1)}, u32[]{:S(2)}, u32[]{:S(2)}) collective-permute-start(bf16[1,4,24,3072]{3,2,1,0:T(8,128)(2,1)} %collective-permute-done.92.refs_1_), channel_id=1, source_target_pairs={{0,1},{1,0},{2,3},{3,2},{4,5},{5,4},{6,7},{7,6},{8,9},{9,8},{10,11... | collective-permute-start | bytes 1769480 | tf_op jit(solution)/shard_map/ppermute | solution.py:108
  891.8 158.5 %collective-permute-start.95 = (bf16[1,4,24,3072]{3,2,1,0:T(8,128)(2,1)}, bf16[1,4,24,3072]{3,2,1,0:T(8,128)(2,1)}, u32[]{:S(2)}, u32[]{:S(2)}) collective-permute-start(bf16[1,4,24,3072]{3,2,1,0:T(8,128)(2,1)} %pad_maximum_fusion.11.refs_0_), channel_id=1, source_target_pairs={{0,2},{1,3},{2,0},{3,1},{4,6},{5,7},{6,4},{7,5},{8,10},{9,11},{10,... | collective-permute-start | bytes 1769480 | tf_op jit(solution)/shard_map/ppermute | solution.py:108
  1050.3 157.1 %collective-permute-start.108 = (bf16[1,4,96,768]{3,2,1,0:T(8,128)(2,1)}, bf16[1,4,96,768]{3,2,1,0:T(8,128)(2,1)}, u32[]{:S(2)}, u32[]{:S(2)}) collective-permute-start(bf16[1,4,96,768]{3,2,1,0:T(8,128)(2,1)} %pad_maximum_fusion.12.refs_0_), channel_id=1, source_target_pairs={{0,2},{1,3},{2,0},{3,1},{4,6},{5,7},{6,4},{7,5},{8,10},{9,11},{10,... | collective-permute-start | bytes 1769480 | tf_op jit(solution)/shard_map/ppermute | solution.py:108
  1055.5 151.9 %collective-permute-start.109 = (bf16[1,4,96,768]{3,2,1,0:T(8,128)(2,1)}, bf16[1,4,96,768]{3,2,1,0:T(8,128)(2,1)}, u32[]{:S(2)}, u32[]{:S(2)}) collective-permute-start(bf16[1,4,96,768]{3,2,1,0:T(8,128)(2,1)} %collective-permute-done.105.refs_1_), channel_id=1, source_target_pairs={{0,2},{1,3},{2,0},{3,1},{4,6},{5,7},{6,4},{7,5},{8,10},{9,11},{10,... | collective-permute-start | bytes 1769480 | tf_op jit(solution)/shard_map/ppermute | solution.py:108
  1055.5 151.9 %collective-permute-start.110 = (bf16[1,4,96,768]{3,2,1,0:T(8,128)(2,1)}, bf16[1,4,96,768]{3,2,1,0:T(8,128)(2,1)}, u32[]{:S(2)}, u32[]{:S(2)}) collective-permute-start(bf16[1,4,96,768]{3,2,1,0:T(8,128)(2,1)} %collective-permute-done.106.refs_2_), channel_id=1, source_target_pairs={{0,2},{1,3},{2,0},{3,1},{4,6},{5,7},{6,4},{7,5},{8,10},{9,11},{10,... | collective-permute-start | bytes 1769480 | tf_op jit(solution)/shard_map/ppermute | solution.py:108
  1056.0 151.4 %collective-permute-start.111 = (bf16[1,4,96,768]{3,2,1,0:T(8,128)(2,1)}, bf16[1,4,96,768]{3,2,1,0:T(8,128)(2,1)}, u32[]{:S(2)}, u32[]{:S(2)}) collective-permute-start(bf16[1,4,96,768]{3,2,1,0:T(8,128)(2,1)} %collective-permute-done.107.refs_3_), channel_id=1, source_target_pairs={{0,2},{1,3},{2,0},{3,1},{4,6},{5,7},{6,4},{7,5},{8,10},{9,11},{10,... | collective-permute-start | bytes 1769480 | tf_op jit(solution)/shard_map/ppermute | solution.py:108
  1476.6 37.6 %collective-permute-start.117 = (f32[5382]{0:T(1024)S(1)}, f32[5382]{0:T(1024)S(1)}, u32[]{:S(2)}, u32[]{:S(2)}) collective-permute-start(f32[5382]{0:T(1024)S(1)} %concatenate.19), channel_id=1, source_target_pairs={{0,1},{1,0},{2,3},{3,2},{4,5},{5,4},{6,7},{7,6},{8,9},{9,8},{10,11... | collective-permute-start | bytes 64592 | tf_op jit(solution)/shard_map/ppermute | solution.py:121
  1483.1 149.9 %collective-permute-start.185 = (bf16[1,4,2,2,96,768]{5,4,1,3,2,0:T(8,128)(2,1)}, bf16[1,4,2,2,96,768]{5,4,1,3,2,0:T(8,128)(2,1)}, u32[]{:S(2)}, u32[]{:S(2)}) collective-permute-start(bf16[1,4,2,2,96,768]{5,4,1,3,2,0:T(8,128)(2,1)} %bitcast.603), channel_id=1, source_target_pairs={{0,2},{1,3},{2,0},{3,1},{4,6},{5,7},{6,4},{7,5},{8,10},{9,11},{10,... | collective-permute-start | bytes 7077896 | tf_op jit(solution)/shard_map/ppermute | solution.py:108
  1504.6 56.3 %collective-permute-start.131 = (bf16[2,4,2,2,24,768]{5,4,0,1,3,2:T(8,128)(2,1)}, bf16[2,4,2,2,24,768]{5,4,0,1,3,2:T(8,128)(2,1)}, u32[]{:S(2)}, u32[]{:S(2)}) collective-permute-start(bf16[2,4,2,2,24,768]{5,4,0,1,3,2:T(8,128)(2,1)} %pad_maximum_fusion.5), channel_id=1, source_target_pairs={{0,2},{1,3},{2,0},{3,1},{4,6},{5,7},{6,4},{7,5},{8,10},{9,11},{10,... | collective-permute-start | bytes 3538952 | tf_op jit(solution)/shard_map/ppermute | solution.py:108
  1507.8 56.5 %collective-permute-start.122 = (bf16[2,4,2,2,24,768]{5,4,0,1,2,3:T(8,128)(2,1)}, bf16[2,4,2,2,24,768]{5,4,0,1,2,3:T(8,128)(2,1)}, u32[]{:S(2)}, u32[]{:S(2)}) collective-permute-start(bf16[2,4,2,2,24,768]{5,4,0,1,2,3:T(8,128)(2,1)} %pad_maximum_fusion.4), channel_id=1, source_target_pairs={{0,2},{1,3},{2,0},{3,1},{4,6},{5,7},{6,4},{7,5},{8,10},{9,11},{10,... | collective-permute-start | bytes 3538952 | tf_op jit(solution)/shard_map/ppermute | solution.py:108
  1559.0 76.9 %collective-permute-start.176 = (bf16[1,4,2,2,24,3072]{5,4,1,2,3,0:T(8,128)(2,1)}, bf16[1,4,2,2,24,3072]{5,4,1,2,3,0:T(8,128)(2,1)S(1)}, u32[]{:S(2)}, u32[]{:S(2)}) collective-permute-start(bf16[1,4,2,2,24,3072]{5,4,1,2,3,0:T(8,128)(2,1)} %bitcast.693), channel_id=1, source_target_pairs={{0,2},{1,3},{2,0},{3,1},{4,6},{5,7},{6,4},{7,5},{8,10},{9,11},{10,... | collective-permute-start | bytes 7077896 | tf_op jit(solution)/shard_map/ppermute | solution.py:108
  1559.3 79.3 %collective-permute-start.167 = (bf16[4,4,2,2,24,768]{5,4,0,1,3,2:T(8,128)(2,1)S(1)}, bf16[4,4,2,2,24,768]{5,4,0,1,3,2:T(8,128)(2,1)S(1)}, u32[]{:S(2)}, u32[]{:S(2)}) collective-permute-start(bf16[4,4,2,2,24,768]{5,4,0,1,3,2:T(8,128)(2,1)S(1)} %copy-done.77), channel_id=1, source_target_pairs={{0,2},{1,3},{2,0},{3,1},{4,6},{5,7},{6,4},{7,5},{8,10},{9,11},{10,... | collective-permute-start | bytes 7077896 | tf_op jit(solution)/shard_map/ppermute | solution.py:108
  1636.0 28.9 %collective-permute-start.186 = (bf16[1,4,2,96,768]{4,3,1,2,0:T(8,128)(2,1)S(1)}, bf16[1,4,2,96,768]{4,3,1,2,0:T(8,128)(2,1)S(1)}, u32[]{:S(2)}, u32[]{:S(2)}) collective-permute-start(bf16[1,4,2,96,768]{4,3,1,2,0:T(8,128)(2,1)S(1)} %dynamic-slice_bitcast_fusion), channel_id=1, source_target_pairs={{0,4},{1,5},{2,6},{3,7},{4,0},{5,1},{6,2},{7,3},{8,12},{9,13},{10,... | collective-permute-start | bytes 3538952 | tf_op jit(solution)/shard_map/ppermute | solution.py:108
  1638.6 28.9 %collective-permute-start.177 = (bf16[1,4,2,24,3072]{4,3,1,2,0:T(8,128)(2,1)S(1)}, bf16[1,4,2,24,3072]{4,3,1,2,0:T(8,128)(2,1)S(1)}, u32[]{:S(2)}, u32[]{:S(2)}) collective-permute-start(bf16[1,4,2,24,3072]{4,3,1,2,0:T(8,128)(2,1)S(1)} %dynamic-slice_bitcast_fusion.1), channel_id=1, source_target_pairs={{0,1},{1,0},{2,3},{3,2},{4,5},{5,4},{6,7},{7,6},{8,9},{9,8},{10,11... | collective-permute-start | bytes 3538952 | tf_op jit(solution)/shard_map/ppermute | solution.py:108
  1640.8 49.3 %collective-permute-start.168 = (bf16[4,4,2,24,768]{4,3,0,1,2:T(8,128)(2,1)S(1)}, bf16[4,4,2,24,768]{4,3,0,1,2:T(8,128)(2,1)S(1)}, u32[]{:S(2)}, u32[]{:S(2)}) collective-permute-start(bf16[4,4,2,24,768]{4,3,0,1,2:T(8,128)(2,1)S(1)} %dynamic-slice_bitcast_fusion.2), channel_id=1, source_target_pairs={{0,4},{1,5},{2,6},{3,7},{4,0},{5,1},{6,2},{7,3},{8,12},{9,13},{10,... | collective-permute-start | bytes 3538952 | tf_op jit(solution)/shard_map/ppermute | solution.py:108
  1643.1 49.7 %collective-permute-start.159 = (bf16[4,4,2,24,768]{4,3,0,1,2:T(8,128)(2,1)S(1)}, bf16[4,4,2,24,768]{4,3,0,1,2:T(8,128)(2,1)S(1)}, u32[]{:S(2)}, u32[]{:S(2)}) collective-permute-start(bf16[4,4,2,24,768]{4,3,0,1,2:T(8,128)(2,1)S(1)} %dynamic-slice_bitcast_fusion.3), channel_id=1, source_target_pairs={{0,1},{1,0},{2,3},{3,2},{4,5},{5,4},{6,7},{7,6},{8,9},{9,8},{10,11... | collective-permute-start | bytes 3538952 | tf_op jit(solution)/shard_map/ppermute | solution.py:108
  1645.5 70.0 %collective-permute-start.150 = (bf16[1,4,2,96,768]{4,3,1,2,0:T(8,128)(2,1)S(1)}, bf16[1,4,2,96,768]{4,3,1,2,0:T(8,128)(2,1)S(1)}, u32[]{:S(2)}, u32[]{:S(2)}) collective-permute-start(bf16[1,4,2,96,768]{4,3,1,2,0:T(8,128)(2,1)S(1)} %dynamic-slice_bitcast_fusion.4), channel_id=1, source_target_pairs={{0,4},{1,5},{2,6},{3,7},{4,0},{5,1},{6,2},{7,3},{8,12},{9,13},{10,... | collective-permute-start | bytes 3538952 | tf_op jit(solution)/shard_map/ppermute | solution.py:108
  1664.9 53.2 %collective-permute-start.141 = (bf16[1,4,2,24,3072]{4,3,1,2,0:T(8,128)(2,1)S(1)}, bf16[1,4,2,24,3072]{4,3,1,2,0:T(8,128)(2,1)S(1)}, u32[]{:S(2)}, u32[]{:S(2)}) collective-permute-start(bf16[1,4,2,24,3072]{4,3,1,2,0:T(8,128)(2,1)S(1)} %dynamic-slice_bitcast_fusion.5), channel_id=1, source_target_pairs={{0,1},{1,0},{2,3},{3,2},{4,5},{5,4},{6,7},{7,6},{8,9},{9,8},{10,11... | collective-permute-start | bytes 3538952 | tf_op jit(solution)/shard_map/ppermute | solution.py:108
  1667.5 63.2 %collective-permute-start.187 = (bf16[1,4,96,768]{3,2,1,0:T(8,128)(2,1)S(1)}, bf16[1,4,96,768]{3,2,1,0:T(8,128)(2,1)S(1)}, u32[]{:S(2)}, u32[]{:S(2)}) collective-permute-start(bf16[1,4,96,768]{3,2,1,0:T(8,128)(2,1)S(1)} %dynamic-slice_bitcast_fusion.6), channel_id=1, source_target_pairs={{0,1},{1,0},{2,3},{3,2},{4,5},{5,4},{6,7},{7,6},{8,9},{9,8},{10,11... | collective-permute-start | bytes 1769480 | tf_op jit(solution)/shard_map/ppermute | solution.py:108
  1690.1 41.5 %collective-permute-start.178 = (bf16[1,4,24,3072]{3,2,1,0:T(8,128)(2,1)S(1)}, bf16[1,4,24,3072]{3,2,1,0:T(8,128)(2,1)S(1)}, u32[]{:S(2)}, u32[]{:S(2)}) collective-permute-start(bf16[1,4,24,3072]{3,2,1,0:T(8,128)(2,1)S(1)} %dynamic-slice_bitcast_fusion.7), channel_id=1, source_target_pairs={{0,4},{1,5},{2,6},{3,7},{4,0},{5,1},{6,2},{7,3},{8,12},{9,13},{10,... | collective-permute-start | bytes 1769480 | tf_op jit(solution)/shard_map/ppermute | solution.py:108
  1692.8 50.6 %collective-permute-start.169 = (bf16[4,4,24,768]{3,2,0,1:T(8,128)(2,1)S(1)}, bf16[4,4,24,768]{3,2,0,1:T(8,128)(2,1)S(1)}, u32[]{:S(2)}, u32[]{:S(2)}) collective-permute-start(bf16[4,4,24,768]{3,2,0,1:T(8,128)(2,1)S(1)} %dynamic-slice_bitcast_fusion.8), channel_id=1, source_target_pairs={{0,1},{1,0},{2,3},{3,2},{4,5},{5,4},{6,7},{7,6},{8,9},{9,8},{10,11... | collective-permute-start | bytes 1769480 | tf_op jit(solution)/shard_map/ppermute | solution.py:108
  1715.4 41.1 %collective-permute-start.160 = (bf16[4,4,24,768]{3,2,0,1:T(8,128)(2,1)S(1)}, bf16[4,4,24,768]{3,2,0,1:T(8,128)(2,1)S(1)}, u32[]{:S(2)}, u32[]{:S(2)}) collective-permute-start(bf16[4,4,24,768]{3,2,0,1:T(8,128)(2,1)S(1)} %dynamic-slice_bitcast_fusion.9), channel_id=1, source_target_pairs={{0,4},{1,5},{2,6},{3,7},{4,0},{5,1},{6,2},{7,3},{8,12},{9,13},{10,... | collective-permute-start | bytes 1769480 | tf_op jit(solution)/shard_map/ppermute | solution.py:108
  1718.0 39.3 %collective-permute-start.151 = (bf16[1,4,96,768]{3,2,1,0:T(8,128)(2,1)S(1)}, bf16[1,4,96,768]{3,2,1,0:T(8,128)(2,1)S(1)}, u32[]{:S(2)}, u32[]{:S(2)}) collective-permute-start(bf16[1,4,96,768]{3,2,1,0:T(8,128)(2,1)S(1)} %dynamic-slice_bitcast_fusion.10), channel_id=1, source_target_pairs={{0,1},{1,0},{2,3},{3,2},{4,5},{5,4},{6,7},{7,6},{8,9},{9,8},{10,11... | collective-permute-start | bytes 1769480 | tf_op jit(solution)/shard_map/ppermute | solution.py:108
  1731.7 35.8 %collective-permute-start.188 = (bf16[1,96,768]{2,1,0:T(8,128)(2,1)S(1)}, bf16[1,96,768]{2,1,0:T(8,128)(2,1)S(1)}, u32[]{:S(2)}, u32[]{:S(2)}) collective-permute-start(bf16[1,96,768]{2,1,0:T(8,128)(2,1)S(1)} %get-tuple-element.200), channel_id=1, source_target_pairs={{0,8},{1,9},{2,10},{3,11},{4,12},{5,13},{6,14},{7,15}} | collective-permute-start | bytes 442376 | tf_op jit(solution)/shard_map/ppermute | solution.py:116
  1743.3 58.8 %collective-permute-start.191 = (bf16[1,96,768]{2,1,0:T(8,128)(2,1)S(1)}, bf16[1,96,768]{2,1,0:T(8,128)(2,1)S(1)}, u32[]{:S(2)}, u32[]{:S(2)}) collective-permute-start(bf16[1,96,768]{2,1,0:T(8,128)(2,1)S(1)} %get-tuple-element.201), channel_id=1, source_target_pairs={{24,16},{25,17},{26,18},{27,19},{28,20},{29,21},{30,22},{31,23}} | collective-permute-start | bytes 442376 | tf_op jit(solution)/shard_map/ppermute | solution.py:116
  1756.5 30.7 %collective-permute-start.182 = (bf16[1,24,3072]{2,1,0:T(8,128)(2,1)S(1)}, bf16[1,24,3072]{2,1,0:T(8,128)(2,1)S(1)}, u32[]{:S(2)}, u32[]{:S(2)}) collective-permute-start(bf16[1,24,3072]{2,1,0:T(8,128)(2,1)S(1)} %get-tuple-element.205), channel_id=1, source_target_pairs={{24,16},{25,17},{26,18},{27,19},{28,20},{29,21},{30,22},{31,23}} | collective-permute-start | bytes 442376 | tf_op jit(solution)/shard_map/ppermute | solution.py:116
  1766.8 42.4 %collective-permute-start.173 = (bf16[4,24,768]{2,1,0:T(8,128)(2,1)S(1)}, bf16[4,24,768]{2,1,0:T(8,128)(2,1)S(1)}, u32[]{:S(2)}, u32[]{:S(2)}) collective-permute-start(bf16[4,24,768]{2,1,0:T(8,128)(2,1)S(1)} %get-tuple-element.209), channel_id=1, source_target_pairs={{24,16},{25,17},{26,18},{27,19},{28,20},{29,21},{30,22},{31,23}} | collective-permute-start | bytes 442376 | tf_op jit(solution)/shard_map/ppermute | solution.py:116
  1772.0 43.8 %collective-permute-start.164 = (bf16[4,24,768]{2,1,0:T(8,128)(2,1)S(1)}, bf16[4,24,768]{2,1,0:T(8,128)(2,1)S(1)}, u32[]{:S(2)}, u32[]{:S(2)}) collective-permute-start(bf16[4,24,768]{2,1,0:T(8,128)(2,1)S(1)} %get-tuple-element.213), channel_id=1, source_target_pairs={{24,16},{25,17},{26,18},{27,19},{28,20},{29,21},{30,22},{31,23}} | collective-permute-start | bytes 442376 | tf_op jit(solution)/shard_map/ppermute | solution.py:116
  1795.1 29.1 %collective-permute-start.155 = (bf16[1,96,768]{2,1,0:T(8,128)(2,1)S(1)}, bf16[1,96,768]{2,1,0:T(8,128)(2,1)S(1)}, u32[]{:S(2)}, u32[]{:S(2)}) collective-permute-start(bf16[1,96,768]{2,1,0:T(8,128)(2,1)S(1)} %get-tuple-element.217), channel_id=1, source_target_pairs={{24,16},{25,17},{26,18},{27,19},{28,20},{29,21},{30,22},{31,23}} | collective-permute-start | bytes 442376 | tf_op jit(solution)/shard_map/ppermute | solution.py:116
  1811.8 38.6 %collective-permute-start.192 = (bf16[1,96,768]{2,1,0:T(8,128)(2,1)S(1)}, bf16[1,96,768]{2,1,0:T(8,128)(2,1)S(1)}, u32[]{:S(2)}, u32[]{:S(2)}) collective-permute-start(bf16[1,96,768]{2,1,0:T(8,128)(2,1)S(1)} %get-tuple-element.199), channel_id=1, source_target_pairs={{16,8},{17,9},{18,10},{19,11},{20,12},{21,13},{22,14},{23,15},{24,... | collective-permute-start | bytes 442376 | tf_op jit(solution)/shard_map/ppermute | solution.py:116
  1815.8 61.1 %collective-permute-start.190 = (bf16[1,96,768]{2,1,0:T(8,128)(2,1)S(1)}, bf16[1,96,768]{2,1,0:T(8,128)(2,1)S(1)}, u32[]{:S(2)}, u32[]{:S(2)}) collective-permute-start(bf16[1,96,768]{2,1,0:T(8,128)(2,1)S(1)} %get-tuple-element.198), channel_id=1, source_target_pairs={{0,8},{1,9},{2,10},{3,11},{4,12},{5,13},{6,14},{7,15},{8,16},{9,17... | collective-permute-start | bytes 442376 | tf_op jit(solution)/shard_map/ppermute | solution.py:116
  1824.2 37.8 %collective-permute-start.181 = (bf16[1,24,3072]{2,1,0:T(8,128)(2,1)S(1)}, bf16[1,24,3072]{2,1,0:T(8,128)(2,1)S(1)}, u32[]{:S(2)}, u32[]{:S(2)}) collective-permute-start(bf16[1,24,3072]{2,1,0:T(8,128)(2,1)S(1)} %get-tuple-element.202), channel_id=1, source_target_pairs={{0,8},{1,9},{2,10},{3,11},{4,12},{5,13},{6,14},{7,15},{8,16},{9,17... | collective-permute-start | bytes 442376 | tf_op jit(solution)/shard_map/ppermute | solution.py:116
  1835.7 48.3 %collective-permute-start.172 = (bf16[4,24,768]{2,1,0:T(8,128)(2,1)S(1)}, bf16[4,24,768]{2,1,0:T(8,128)(2,1)S(1)}, u32[]{:S(2)}, u32[]{:S(2)}) collective-permute-start(bf16[4,24,768]{2,1,0:T(8,128)(2,1)S(1)} %get-tuple-element.206), channel_id=1, source_target_pairs={{0,8},{1,9},{2,10},{3,11},{4,12},{5,13},{6,14},{7,15},{8,16},{9,17... | collective-permute-start | bytes 442376 | tf_op jit(solution)/shard_map/ppermute | solution.py:116
  1851.1 41.6 %collective-permute-start.163 = (bf16[4,24,768]{2,1,0:T(8,128)(2,1)S(1)}, bf16[4,24,768]{2,1,0:T(8,128)(2,1)S(1)}, u32[]{:S(2)}, u32[]{:S(2)}) collective-permute-start(bf16[4,24,768]{2,1,0:T(8,128)(2,1)S(1)} %get-tuple-element.210), channel_id=1, source_target_pairs={{0,8},{1,9},{2,10},{3,11},{4,12},{5,13},{6,14},{7,15},{8,16},{9,17... | collective-permute-start | bytes 442376 | tf_op jit(solution)/shard_map/ppermute | solution.py:116
  1862.0 37.2 %collective-permute-start.154 = (bf16[1,96,768]{2,1,0:T(8,128)(2,1)S(1)}, bf16[1,96,768]{2,1,0:T(8,128)(2,1)S(1)}, u32[]{:S(2)}, u32[]{:S(2)}) collective-permute-start(bf16[1,96,768]{2,1,0:T(8,128)(2,1)S(1)} %get-tuple-element.214), channel_id=1, source_target_pairs={{0,8},{1,9},{2,10},{3,11},{4,12},{5,13},{6,14},{7,15},{8,16},{9,17... | collective-permute-start | bytes 442376 | tf_op jit(solution)/shard_map/ppermute | solution.py:116
  (325 other events, 8556.3 us)

commit v2 on v1

--- a/solution.py
+++ b/solution.py
@@ -91,135 +91,538 @@
     return attn(bwd_kernel,mode,half,"qkk"+("t" if table is not None else ""),q,k,v,[g],qc,kc,table)
 
 
-def flat_index(z, x, core, y):
-    return ((z * 2 + x) * 2 + core) * 2 + y
-
-
-def every_device():
-    return [(z, x, c, y) for z in range(CHAIN) for x in range(2) for c in range(2) for y in range(2)]
-
-
-def swap(value, axis):
-    pairs = []
-    for place in every_device():
-        other = list(place)
-        other["zxcy".index(axis)] ^= 1
-        pairs.append((flat_index(*place), flat_index(*other)))
-    return lax.ppermute(value, BOTH, pairs)
-
-
-def shift(value, step, reach):
-    pairs = []
-    for z, x, c, y in every_device():
-        if 0 <= z + step < CHAIN and 0 <= z + reach < CHAIN:
-            pairs.append((flat_index(z, x, c, y), flat_index(z + step, x, c, y)))
-    return lax.ppermute(value, BOTH, pairs)
+class Place:
+    def __init__(self):
+        row = lax.axis_index("rows")
+        self.z, self.x, self.c, self.y = row // 4, (row // 2) % 2, row % 2, lax.axis_index("seq")
+
+    def device(self, axis):
+        z, x, c, y = self.z, self.x, self.c, self.y
+        if axis == "up":
+            z = z + 1
+        if axis == "down":
+            z = z - 1
+        if axis == "x":
+            x = 1 - x
+        if axis == "c":
+            c = 1 - c
+        if axis == "y":
+            y = 1 - y
+        return {"rows": z * 4 + x * 2 + c, "seq": y}
+
+
+def greet(place):
+    barrier = pltpu.get_barrier_semaphore()
+
+    def signal(axis):
+        pl.semaphore_signal(
+            barrier, inc=1, device_id=place.device(axis), device_id_type=pl.DeviceIdType.MESH
+        )
+
+    for axis in "xcy":
+        signal(axis)
+    pl.when(place.z < CHAIN - 1)(lambda: signal("up"))
+    pl.when(place.z > 0)(lambda: signal("down"))
+    ends = (place.z == 0) | (place.z == CHAIN - 1)
+    pl.when(ends)(lambda: pl.semaphore_wait(barrier, 4))
+    pl.when(jnp.logical_not(ends))(lambda: pl.semaphore_wait(barrier, 5))
+
+
+def third_of(width, third):
+    if third is None:
+        return slice(None)
+    return slice(width // 3 * third, width // 3 * (third + 1))
+
+
+class GatherStream:
+    def __init__(self, place, own, out, third, kind, u, v, send, recv):
+        self.place, self.own, self.out, self.third = place, own, out, third
+        self.kind, self.u, self.v, self.send, self.recv = kind, u, v, send, recv
+        self.cols = third_of(own.shape[-1], third)
+
+    def block(self, z, pair):
+        p = self.place
+        x = slice(None) if pair and self.u == "x" else p.x
+        y = slice(None) if pair and self.u == "y" else p.y
+        return self.out.at[:, z, x, p.c, y, :, self.cols]
+
+    def other(self, z, axis, pair):
+        p = self.place
+        x, y = p.x, p.y
+        if pair and self.u == "x":
+            x = slice(None)
+        elif axis == "x":
+            x = 1 - x
+        if pair and self.u == "y":
+            y = slice(None)
+        elif axis == "y":
+            y = 1 - y
+        return self.out.at[:, z, x, p.c, y, :, self.cols]
+
+    def copy(self, slot, src, dst, axis):
+        return pltpu.make_async_remote_copy(
+            src_ref=src,
+            dst_ref=dst,
+            send_sem=self.send.at[slot],
+            recv_sem=self.recv.at[slot],
+            device_id=self.place.device(axis),
+            device_id_type=pl.DeviceIdType.MESH,
+        )
+
+    def first(self, z):
+        return self.own.at[:, :, self.cols]
+
+    def chain_copy(self, up, step):
+        pair = self.kind == "B"
+        z = self.place.z - (step - 1) if up else self.place.z + (step - 1)
+        src = self.first(z) if step == 1 and not pair else self.block(z, pair)
+        return self.copy(step - 1 if up else step + 2, src, self.block(z, pair), "up" if up else "down")
+
+    def chain_arrival(self, up, step):
+        pair = self.kind == "B"
+        z = self.place.z - step if up else self.place.z + step
+        ref = self.block(z, pair)
+        return self.copy(step - 1 if up else step + 2, ref, ref, "up" if up else "down")
+
+    def sends_at(self, up, step):
+        z = self.place.z
+        if up:
+            return (z < CHAIN - 1) & (z >= step - 1)
+        return (z > 0) & (z <= CHAIN - step)
+
+    def arrives_at(self, up, step):
+        z = self.place.z
+        return z >= step if up else z <= CHAIN - 1 - step
+
+    def side_copy(self, slot, z, axis, pair, fresh):
+        src = self.first(z) if fresh else self.block(z, pair)
+        return self.copy(slot, src, self.block(z, pair), axis)
+
+    def side_arrival(self, slot, z, axis, pair):
+        ref = self.other(z, axis, pair)
+        return self.copy(slot, ref, ref, axis)
+
+    def z_of(self, number):
+        if number == 0:
+            return self.place.z
+        return self.place.z - number if number <= CHAIN - 1 else self.place.z + (number - CHAIN + 1)
+
+    def u_copy(self, number):
+        return self.side_copy(6 + number, self.z_of(number), self.u, False, number == 0)
+
+    def u_arrival(self, number):
+        return self.side_arrival(6 + number, self.z_of(number), self.u, False)
+
+    def v_copy(self, number):
+        return self.side_copy(13 + number, self.z_of(number), self.v, True, False)
+
+    def v_arrival(self, number):
+        return self.side_arrival(13 + number, self.z_of(number), self.v, True)
+
+
+SLOTS = 20
+
+
+def each_arrival(stream, step, act):
+    for up in (True, False):
+        number = step if up else step + CHAIN - 1
+        pl.when(stream.arrives_at(up, step))(functools.partial(act, up, number))
+
+
+def gather_kernel(plans, count, *refs):
+    owns = refs[:count]
+    outs = refs[count : 2 * count]
+    send, recv, core_send, core_recv, local = refs[2 * count :]
+    place = Place()
+    streams = [
+        GatherStream(place, owns[a], outs[a], third, kind, u, v, send.at[i], recv.at[i])
+        for i, (a, third, kind, u, v) in enumerate(plans)
+    ]
+    kept = []
+    for a in range(count):
+        copy = pltpu.make_async_copy(
+            owns[a], outs[a].at[:, place.z, place.x, place.c, place.y], local.at[a]
+        )
+        copy.start()
+        kept.append(copy)
+    greet(place)
+
+    def when(cond, act):
+        pl.when(cond)(act)
+
+    for s in streams:
+        s.u_copy(0).start()
+    for s in streams:
+        if s.kind == "A":
+            for up in (True, False):
+                when(s.sends_at(up, 1), lambda: s.chain_copy(up, 1).start())
+    for copy in kept:
+        copy.wait()
+    for s in streams:
+        s.u_arrival(0).wait_recv()
+        if s.kind == "B":
+            for up in (True, False):
+                when(s.sends_at(up, 1), lambda: s.chain_copy(up, 1).start())
+        s.v_copy(0).start()
+
+    def core_copy(a, number):
+        z = GatherStream.z_of(streams[0], number)
+        slot = a * 7 + number
+        mine = outs[a].at[:, z, :, place.c]
+        theirs = outs[a].at[:, z, :, 1 - place.c]
+        made = functools.partial(
+            pltpu.make_async_remote_copy,
+            send_sem=core_send.at[slot],
+            recv_sem=core_recv.at[slot],
+            device_id=place.device("c"),
+            device_id_type=pl.DeviceIdType.MESH,
+        )
+        return made(src_ref=mine, dst_ref=mine), made(src_ref=theirs, dst_ref=theirs)
+
+    def finish(number):
+        for s in streams:
+            s.v_arrival(number).wait_recv()
+        for a in range(count):
+            core_copy(a, number)[0].start()
+
+    def arrival(s, step, up, number):
+        s.chain_arrival(up, step).wait_recv()
+        if step < CHAIN - 1:
+            when(s.sends_at(up, step + 1), lambda: s.chain_copy(up, step + 1).start())
+        if s.kind == "A":
+            s.u_copy(number).start()
+        else:
+            s.v_copy(number).start()
+
+    def side(s, up, number):
+        s.u_arrival(number).wait_recv()
+        s.v_copy(number).start()
+
+    for step in range(1, CHAIN):
+        for s in streams:
+            each_arrival(s, step, functools.partial(arrival, s, step))
+        if step == 1:
+            finish(0)
+        for s in streams:
+            if s.kind == "A":
+                each_arrival(s, step, functools.partial(side, s))
+        if step > 1:
+            each_arrival(streams[0], step - 1, lambda up, number: finish(number))
+    each_arrival(streams[0], CHAIN - 1, lambda up, number: finish(number))
+
+    def last(up, number):
+        for a in range(count):
+            core_copy(a, number)[1].wait_recv()
+            core_copy(a, number)[0].wait_send()
+        for s in streams:
+            if s.kind == "A":
+                s.u_copy(number).wait_send()
+            s.v_copy(number).wait_send()
+
+    last(True, 0)
+    for s in streams:
+        if s.kind == "B":
+            s.u_copy(0).wait_send()
+        for step in range(1, CHAIN):
+            for up in (True, False):
+                when(s.sends_at(up, step), lambda: s.chain_copy(up, step).wait_send())
+    for step in range(1, CHAIN):
+        each_arrival(streams[0], step, last)
+
+
+def plans_for(arrays):
+    plans = []
+    for a, array in enumerate(arrays):
+        u, v = ("x", "y") if a % 2 == 0 else ("y", "x")
+        if array.shape[-1] % 768 == 0:
+            plans += [(a, 0, "B", "x", "y"), (a, 1, "B", "y", "x"), (a, 2, "A", u, v)]
+        else:
+            plans.append((a, None, "A", u, v))
+    return tuple(plans)
+
+
+def gather_weights(arrays, collective_id):
+    plans = plans_for(arrays)
+    count = len(arrays)
+    shapes = [(a.shape[0], CHAIN, 2, 2, 2) + a.shape[1:] for a in arrays]
+    sems = pltpu.SemaphoreType.DMA
+    outs = pl.pallas_call(
+        functools.partial(gather_kernel, plans, count),
+        out_shape=[jax.ShapeDtypeStruct(s, a.dtype) for s, a in zip(shapes, arrays)],
+        in_specs=[pl.BlockSpec(memory_space=pltpu.VMEM)] * count,
+        out_specs=[pl.BlockSpec(memory_space=pltpu.HBM)] * count,
+        scratch_shapes=[
+            sems((len(plans), SLOTS)),
+            sems((len(plans), SLOTS)),
+            sems((count * 7,)),
+            sems((count * 7,)),
+            sems((count,)),
+        ],
+        compiler_params=pltpu.CompilerParams(collective_id=collective_id, has_side_effects=True),
+    )(*arrays)
+    return [o.reshape(a.shape[0], -1, a.shape[2]) for o, a in zip(outs, arrays)]
+
+
+def add_into(target, terms, cols):
+    lead = target.shape[:-2]
+    total = 1
+    for size in lead:
+        total *= size
+
+    def one(flat, unused):
+        index = []
+        for size in reversed(lead):
+            index.insert(0, flat % size)
+            flat = flat // size
+        value = target[(*index, slice(None), cols)].astype(jnp.float32)
+        for term in terms:
+            value = value + term[(*index, slice(None), cols)].astype(jnp.float32)
+        target[(*index, slice(None), cols)] = value.astype(target.dtype)
+        return unused
+
+    lax.fori_loop(0, total, one, 0)
+
+
+class ReduceStream:
+    def __init__(self, place, bufs, third, kind, u, v, send, recv):
+        self.place, self.kind, self.u, self.v, self.send, self.recv = place, kind, u, v, send, recv
+        self.acc, self.side_v, self.side_u, self.chain = bufs
+        self.cols = third_of(self.acc.shape[-1], third)
+
+    def z_of(self, number):
+        return GatherStream.z_of(self, number)
+
+    def pair(self, z, v_other=False):
+        p = self.place
+        flip = lambda at: 1 - at if v_other else at
+        if self.u == "x":
+            return self.acc.at[:, z, :, flip(p.y)]
+        return self.acc.at[:, z, flip(p.x), :]
+
+    def single(self, z, u_other=False):
+        p = self.place
+        x = 1 - p.x if u_other and self.u == "x" else p.x
+        y = 1 - p.y if u_other and self.u == "y" else p.y
+        return self.acc.at[:, z, x, y]
+
+    def copy(self, slot, src, dst, axis):
+        return pltpu.make_async_remote_copy(
+            src_ref=src.at[..., self.cols],
+            dst_ref=dst.at[..., self.cols],
+            send_sem=self.send.at[slot],
+            recv_sem=self.recv.at[slot],
+            device_id=self.place.device(axis),
+            device_id_type=pl.DeviceIdType.MESH,
+        )
+
+    def v_copy(self, number):
+        z = self.z_of(number)
+        return self.copy(6 + number, self.pair(z, True), self.side_v.at[:, z], self.v)
+
+    def v_add(self, number):
+        z = self.z_of(number)
+        self.v_copy(number).wait_recv()
+        add_into(self.pair(z), [self.side_v.at[:, z]], self.cols)
+
+    def u_copy(self, number):
+        z = self.z_of(number)
+        return self.copy(13 + number, self.single(z, True), self.side_u.at[:, z], self.u)
+
+    def u_add(self, number):
+        z = self.z_of(number)
+        self.u_copy(number).wait_recv()
+        add_into(self.single(z), [self.side_u.at[:, z]], self.cols)
+
+    def chain_block(self, z):
+        return self.pair(z) if self.kind == "B" else self.single(z)
+
+    def chain_slot(self, up, step):
+        at = self.chain.at[:, 0 if up else 1, step - 1]
+        return at if self.kind == "B" else at.at[:, 0]
+
+    def chain_copy(self, up, step):
+        z = self.place.z + step if up else self.place.z - step
+        return self.copy(
+            step - 1 if up else step + 2,
+            self.chain_block(z),
+            self.chain_slot(up, step),
+            "up" if up else "down",
+        )
+
+    def has_before(self, up):
+        return self.place.z > 0 if up else self.place.z < CHAIN - 1
+
+    def chain_arrival(self, up, step):
+        ref = self.chain_slot(up, step)
+        return self.copy(step - 1 if up else step + 2, ref, ref, "up" if up else "down")
+
+    def chain_step(self, up, step):
+        z = self.place.z + step if up else self.place.z - step
+        if step < CHAIN - 1:
+
+            @pl.when(self.has_before(up))
+            def arrived():
+                self.chain_arrival(up, step + 1).wait_recv()
+                add_into(self.chain_block(z), [self.chain_slot(up, step + 1)], self.cols)
+
+        self.chain_copy(up, step).start()
+
+    def chain_end(self):
+        for up in (True, False):
+
+            @pl.when(self.has_before(up))
+            def arrived():
+                self.chain_arrival(up, 1).wait_recv()
+                add_into(self.chain_block(self.place.z), [self.chain_slot(up, 1)], self.cols)
+
+
+def reduce_kernel(plans, count, *refs):
+    grads = refs[:count]
+    outs = refs[count : 2 * count]
+    bufs = refs[2 * count : 7 * count]
+    send, recv, core_send, core_recv, local = refs[7 * count :]
+    place = Place()
+    accs, cores = bufs[:count], bufs[count : 2 * count]
+    streams = [
+        ReduceStream(
+            place, [bufs[k * count + a] for k in (0, 2, 3, 4)], third, kind, u, v, send.at[i], recv.at[i]
+        )
+        for i, (a, third, kind, u, v) in enumerate(plans)
+    ]
+
+    def z_of(number):
+        return GatherStream.z_of(streams[0], number)
+
+    def valid(number):
+        return place.z >= number if number < CHAIN else place.z <= 2 * (CHAIN - 1) - number
+
+    def each(act):
+        for step in range(CHAIN - 1, 0, -1):
+            for number in (step, step + CHAIN - 1):
+                pl.when(valid(number))(functools.partial(act, number))
+        act(0)
+
+    def load(a, number):
+        z = z_of(number)
+        return pltpu.make_async_copy(
+            grads[a].at[:, z, :, place.c], accs[a].at[:, z], local.at[a * 7 + number]
+        )
+
+    def core_copy(a, number):
+        z = z_of(number)
+        return pltpu.make_async_remote_copy(
+            src_ref=grads[a].at[:, z, :, 1 - place.c],
+            dst_ref=cores[a].at[:, z],
+            send_sem=core_send.at[a * 7 + number],
+            recv_sem=core_recv.at[a * 7 + number],
+            device_id=place.device("c"),
+            device_id_type=pl.DeviceIdType.MESH,
+        )
+
+    def begin(number):
+        for a in range(count):
+            load(a, number).start()
+
+    def begin_core(number):
+        for a in range(count):
+            core_copy(a, number).start()
+
+    each(begin)
+    greet(place)
+    each(begin_core)
+
+    def first(number):
+        z = z_of(number)
+        for a in range(count):
+            load(a, number).wait()
+            core_copy(a, number).wait_recv()
+            add_into(accs[a].at[:, z], [cores[a].at[:, z]], slice(None))
+            for s, plan in zip(streams, plans):
+                if plan[0] == a:
+                    s.v_copy(number).start()
+
+    each(first)
+
+    def second(number):
+        for s in streams:
+            s.v_add(number)
+            if s.kind == "A":
+                s.u_copy(number).start()
+            elif number > 0:
+                up = number >= CHAIN
+                s.chain_step(up, number - (CHAIN - 1) if up else number)
+
+    each(second)
+
+    def third(number):
+        for s in streams:
+            if s.kind == "A":
+                s.u_add(number)
+                if number > 0:
+                    up = number >= CHAIN
+                    s.chain_step(up, number - (CHAIN - 1) if up else number)
+
+    each(third)
+    for s in streams:
+        if s.kind == "B":
+            s.chain_end()
+            s.u_copy(0).start()
+    for s in streams:
+        if s.kind == "A":
+            s.chain_end()
+    for s, plan in zip(streams, plans):
+        if s.kind == "B":
+            s.u_add(0)
+    for a in range(count):
+        for item in range(outs[a].shape[0]):
+            outs[a][item] = accs[a][item, place.z, place.x, place.y].astype(jnp.float32)
+
+    def last(number):
+        for a in range(count):
+            core_copy(a, number).wait_send()
+        for s in streams:
+            s.v_copy(number).wait_send()
+            if s.kind == "A" or number == 0:
+                s.u_copy(number).wait_send()
+            if number > 0:
+                up = number >= CHAIN
+                s.chain_copy(up, number - (CHAIN - 1) if up else number).wait_send()
+
+    each(last)
+
+
+def reduce_gradients(grads, collective_id):
+    parts = 8 * CHAIN
+    arrays = [g.reshape(g.shape[0], CHAIN, 2, 2, 2, g.shape[1] // parts, g.shape[2]) for g in grads]
+    plans = plans_for(arrays)
+    count = len(arrays)
+    sems = pltpu.SemaphoreType.DMA
+    scratch = []
+    for lead in ((CHAIN, 2, 2), (CHAIN, 2, 2), (CHAIN, 2), (CHAIN,), (2, CHAIN - 1, 2)):
+        for a in arrays:
+            scratch.append(pltpu.VMEM((a.shape[0],) + lead + a.shape[-2:], a.dtype))
+    return pl.pallas_call(
+        functools.partial(reduce_kernel, plans, count),
+        out_shape=[jax.ShapeDtypeStruct((a.shape[0],) + a.shape[-2:], jnp.float32) for a in arrays],
+        in_specs=[pl.BlockSpec(memory_space=pltpu.HBM)] * count,
+        out_specs=[pl.BlockSpec(memory_space=pltpu.VMEM)] * count,
+        scratch_shapes=scratch
+        + [
+            sems((len(plans), SLOTS)),
+            sems((len(plans), SLOTS)),
+            sems((count * 7,)),
+            sems((count * 7,)),
+            sems((count * 7,)),
+        ],
+        compiler_params=pltpu.CompilerParams(
+            collective_id=collective_id, has_side_effects=True, vmem_limit_bytes=60 * 2**20
+        ),
+    )(*arrays)
 
 
 def hop(value, bit):
     size = 4 * CHAIN * 2
     return lax.ppermute(value, BOTH, [(i, i ^ bit) for i in range(size)])
-
-
-def place_of():
-    row = lax.axis_index("rows")
-    return {"z": row // 4, "x": (row // 2) % 2, "c": row % 2, "y": lax.axis_index("seq")}
-
-
-def assemble_kernel(count, shifts, *refs):
-    pieces = refs[:8]
-    outs = refs[8 : 8 + count]
-    sem = refs[8 + count]
-    row = lax.axis_index("rows")
-    here = {"x": (row // 2) % 2, "c": row % 2, "y": lax.axis_index("seq")}
-    copies = []
-    for number, piece in enumerate(pieces):
-        moved = shifts[number]
-        slot = {a: here[a] + (1 - 2 * here[a]) * (1 if a in moved else 0) for a in "xcy"}
-        index = slot["x"] * 4 + slot["c"] * 2 + slot["y"]
-        for item in range(count):
-            copy = pltpu.make_async_copy(
-                piece.at[item], outs[item].at[:, index], sem.at[number, item]
-            )
-            copy.start()
-            copies.append(copy)
-    for copy in copies:
-        copy.wait()
-
-
-def assemble(pieces, shifts):
-    count, chain, height, width = pieces[0].shape
-    outs = pl.pallas_call(
-        functools.partial(assemble_kernel, count, shifts),
-        out_shape=[jax.ShapeDtypeStruct((chain, 8, height, width), pieces[0].dtype)] * count,
-        in_specs=[pl.BlockSpec(memory_space=pl.ANY)] * 8,
-        out_specs=[pl.BlockSpec(memory_space=pl.ANY)] * count,
-        scratch_shapes=[pltpu.SemaphoreType.DMA((8, count))],
-        cost_estimate=pl.CostEstimate(
-            flops=0, bytes_accessed=2 * 8 * pieces[0].size * 2, transcendentals=0
-        ),
-    )(*pieces)
-    return [out.reshape(chain * 8 * height, width) for out in outs]
-
-
-def gather_group(shards, order):
-    own = jnp.stack(shards)
-    place = place_of()
-    up, down = own, own
-    ups, downs = {}, {}
-    for step in range(1, CHAIN):
-        up = shift(up, 1, 1 - step)
-        down = shift(down, -1, step - 1)
-        ups[step], downs[step] = up, down
-    blocks = []
-    for k in range(CHAIN):
-        block = own
-        for step in range(1, CHAIN):
-            if k + step < CHAIN:
-                block = jnp.where(place["z"] == k + step, ups[step], block)
-            if k - step >= 0:
-                block = jnp.where(place["z"] == k - step, downs[step], block)
-        blocks.append(block)
-    pieces = {"": jnp.stack(blocks, axis=1)}
-    for axis in order:
-        for name in list(pieces):
-            pieces[name + axis] = swap(pieces[name], axis)
-    names = list(pieces)
-    return assemble([pieces[name] for name in names], names)
-
-
-def reduce_group(grads, order):
-    place = place_of()
-    axes = ["z", "x", "c", "y"]
-    parts = [
-        grad.reshape(CHAIN, 2, 2, 2, grad.shape[0] // (8 * CHAIN), grad.shape[1]) for grad in grads
-    ]
-    held = None
-    for axis in reversed(order):
-        at = axes.index(axis)
-        axes.remove(axis)
-        mine = place[axis]
-        if held is None:
-            pick = lambda where: jnp.stack(
-                [lax.dynamic_index_in_dim(part, where, at, keepdims=False) for part in parts]
-            )
-        else:
-            pick = lambda where: lax.dynamic_index_in_dim(held, where, at + 1, keepdims=False)
-        sent = swap(pick(1 - mine), axis)
-        held = (pick(mine).astype(jnp.float32) + sent.astype(jnp.float32)).astype(jnp.bfloat16)
-    pick = lambda where: lax.dynamic_index_in_dim(
-        held, jnp.clip(where, 0, CHAIN - 1), 1, keepdims=False
-    ).astype(jnp.float32)
-    total = pick(place["z"])
-    for sign in (1, -1):
-        moving = None
-        for step in range(CHAIN - 1, 0, -1):
-            term = pick(place["z"] + sign * step)
-            if moving is not None:
-                term = term + moving.astype(jnp.float32)
-            moving = shift(term.astype(jnp.bfloat16), sign, sign * step)
-        total = total + moving.astype(jnp.float32)
-    return [total[i] for i in range(len(grads))]
 
 
 def sum_everywhere(value):
@@ -459,14 +862,12 @@
 
 
 GROUPS = (
-    (("eq", "ek"), "xyc"),
-    (("ev", "eo"), "yxc"),
-    (("ew",), "xyc"),
-    (("en",), "yxc"),
-    (("dq", "dk", "dv", "do"), "xyc"),
-    (("cq", "ck", "cv", "co"), "yxc"),
-    (("dw",), "xyc"),
-    (("dn",), "yxc"),
+    ("eq", "ek", "ev", "eo"),
+    ("ew",),
+    ("en",),
+    ("dq", "dk", "dv", "do", "cq", "ck", "cv", "co"),
+    ("dw",),
+    ("dn",),
 )
 WEIGHT_ARGS = {
     "eq": 6, "ek": 7, "ev": 8, "eo": 9, "ew": 12, "en": 13, "dq": 16, "dk": 17, "dv": 18, "do": 19,
@@ -488,11 +889,13 @@
     own_gains = jnp.stack([args[i] for i in GAIN_ARGS])
     weights = {}
     if near:
-        spread = jnp.zeros((6, row_count * own_gains.shape[1]), jnp.bfloat16)
-        spread = lax.dynamic_update_slice_in_dim(spread, own_gains, me * own_gains.shape[1], 1)
-        gains = sum_everywhere(spread)
-        for names, order in GROUPS:
-            weights.update(zip(names, gather_group([shards[n] for n in names], order)))
+        tile = jnp.pad(own_gains, ((0, 2), (0, 128 - own_gains.shape[1])))[None]
+        stacks = [jnp.stack([shards[n] for n in names]) for names in GROUPS]
+        gathered = gather_weights(stacks + [tile], 0)
+        for names, stack in zip(GROUPS, gathered):
+            weights.update((n, stack[i]) for i, n in enumerate(names))
+        tiles = gathered[-1].reshape(row_count, 8, 128)[:, :6, : own_gains.shape[1]]
+        gains = jnp.transpose(tiles, (1, 0, 2)).reshape(6, -1)
     else:
         gains = lax.all_gather(own_gains, BOTH, axis=1, tiled=True)
         for name, shard in shards.items():
@@ -519,8 +922,10 @@
         outs[i] = own_slots(value)
     reduced = {}
     if near:
-        for names, order in reversed(GROUPS):
-            reduced.update(zip(names, reduce_group([grads[n] for n in names], order)))
+        for number, groups in ((1, GROUPS[3:]), (2, GROUPS[:3])):
+            stacks = [jnp.stack([grads[n] for n in names]) for names in groups]
+            for names, total in zip(groups, reduce_gradients(stacks, number)):
+                reduced.update((n, total[i]) for i, n in enumerate(names))
         small = sum_everywhere(small)
     else:
         for name, grad in grads.items():

time: 1920 us -> 583 us (0.30)
  Pallas kernels: 1090 us -> 380 us
  starting transfers between devices: 325 us -> 18.3 us
  waiting for transfers between devices: 232 us -> 2.1 us
  local copies, waits for them, and re-layouts: 85.1 us -> 52.2 us
  other arithmetic: 55.2 us -> 23.4 us
    pallas_call x8 -> x3, Pallas kernels: 1010 us -> 302 us  [the longest x2 158 us: reduce_gradients(): pl.pallas_call(functools.partial(reduce_kernel, plans, count), out_shape=...]
    ppermute x176 -> x0, starting transfers between devices: 304 us -> none  [the longest x96 250 us: shift(): return lax.ppermute(value, BOTH, pairs)]
    ppermute x176 -> x0, waiting for transfers between devices: 212 us -> none  [the longest x80 142 us: swap(): return lax.ppermute(value, BOTH, pairs)]
    dynamic_slice x44 -> x0, local copies, waits for them, and re-layouts: 27.9 us -> none  [reduce_group(): lax.dynamic_index_in_dim(part, where, at, keepdims=False)]
  transfers between devices with their start and end apart: 194 -> 13, of which waited for: 57 -> 3; matrix products, arithmetic and copies ran while one was open for 8% -> 15% of each run, Pallas kernels for 47% -> 60%
where the time goes in v2:
time: 583 us; the launch traced here: 575 us
  Pallas kernels  380 us (65%)
  matrix products  96.9 us (17%)
  local copies, waits for them, and re-layouts  52.2 us (9%)
  other arithmetic  23.4 us (4%)
  starting transfers between devices  18.3 us (3%)
    pallas_call x2, Pallas kernels, reduce_gradients(): pl.pallas_call(functools.partial(reduce_kernel, plans, count), out_shape=...  158 us
    pallas_call x1, Pallas kernels, gather_weights(): pl.pallas_call(functools.partial(gather_kernel, plans, count), out_shape=...  144 us
    pallas_call x6, Pallas kernels, attn(): pl.pallas_call(functools.partial(kernel, mode, half), grid=(width // 128,...  77.8 us
    dot_general x32, matrix products, dotf(): return lax.dot_general(a, b, dims, preferred_element_type=jnp.float32)  72.6 us
    unnamed x240, local copies, waits for them, and re-layouts  22.8 us
    dot_general x16, matrix products, matmul(): return jnp.dot(left, right, preferred_element_type=jnp.float32)  22.2 us
  transfers between devices with their start and end apart: 13, of which 3 were waited for; matrix products, arithmetic and copies ran while one was open for 15% of the time, Pallas kernels for 60%

profile of v2, /device:TPU:0, one launch (start us, length us, event | category | flops | bytes accessed | tf_op | source)
XLA Modules:
  0.0 575.2 jit_solution(15699315286357516029)
XLA Ops:
  0.9 1.9 dynamic-slice_bitcast_fusion.1
  2.8 3.0 collective-permute-start
  7.6 2.0 collective-permute-start.5
  9.6 1.8 dynamic-slice_bitcast_fusion
  15.3 1.2 convert_reduce_fusion.1
  16.5 1.2 convert_reduce_fusion.2
  19.3 144.0 %shard_map.518 = (bf16[4,4,2,2,2,24,768]{6,5,4,3,2,1,0:T(8,128)(2,1)}, bf16[1,4,2,2,2,24,3072]{6,5,4,3,2,1,0:T(8,128)(2,1)}, bf16[1,4,2,2,2,96,768]{6,5,4,3,2,1,...) custom-call(bf16[4,24,768]{2,1,0:T(8,128)(2,1)} %pad_maximum_fusion., ...), custom_call_target="tpu_custom_call" | custom-call | tf_op jit(solution)/shard_map/pallas_call | solution.py:349
  164.3 4.5 fusion.92
  169.9 6.7 %fusion.91 = (bf16[1,4,2,2,2,24,768]{6,5,4,3,2,1,0:T(8,128)(2,1)}, bf16[1,4,2,2,2,24,768]{6,5,4,3,2,1,0:T(8,128)(2,1)}, bf16[1,4,2,2,2,24,768]{6,5,4,3,2,1,0:T(8...) fusion(bf16[8,4,2,2,2,24,768]{6,5,4,3,2,1,0:T(8,128)(2,1)} %get, ...), kind=kLoop, calls=%fused_computation.242 | loop fusion | bytes 18874368 | tf_op jit(solution)/shard_map/slice | solution.py:896
  179.3 1.7 convolution_convert_fusion.25.refs_2_
  181.8 5.6 shard_map.520
  189.7 1.2 copy-done.34
  194.2 21.3 %shard_map.519 = bf16[512,768]{1,0:T(8,128)(2,1)S(1)} custom-call(bf16[512,768]{1,0:T(8,128)(2,1)S(1)} %convolution_convert_fusion.21.refs_0_, bf16[512,768]{1,0:T(8,128)(2,1)S(1)} %convolution_convert_fusion.20.refs_1_, bf16[512,768]{1,0:T(8,128)(2,1)S(1)} %convolution_convert_fusion.19.refs_2_, s32[512,1]{1,0:T(8,128)S(1)} %copy.68.refs_3_.refs_4_, ...), custom_call_target="tpu_custom_call" | custom-call | tf_op jit(solution)/shard_map/pallas_call | solution.py:84
  216.5 5.7 fusion.76
  222.3 4.6 multiply_reduce_fusion.5
  227.1 1.9 copy-done.53
  230.6 6.2 %shard_map.521 = bf16[128,768]{1,0:T(8,128)(2,1)S(1)} custom-call(bf16[128,768]{1,0:T(8,128)(2,1)S(1)} %convolution_convert_fusion.24.refs_0_, bf16[512,768]{1,0:T(8,128)(2,1)S(1)} %convolution_convert_fusion.18.refs_1_, bf16[512,768]{1,0:T(8,128)(2,1)S(1)} %convolution_convert_fusion.17.refs_2_, s32[128,1]{1,0:T(8,128)S(1)} %fusion.62.refs_3_.refs_4_, ...), custom_call_target="tpu_custom_call" | custom-call | tf_op jit(solution)/shard_map/pallas_call | solution.py:84
  238.2 5.4 fusion.17
  243.6 1.8 multiply_reduce_fusion.6
  245.4 2.5 select_reduce_fusion.2
  248.5 9.2 %shard_map.522 = (bf16[128,768]{1,0:T(8,128)(2,1)S(1)}, bf16[512,768]{1,0:T(8,128)(2,1)S(1)}, bf16[512,768]{1,0:T(8,128)(2,1)S(1)}) custom-call(bf16[128,768]{1,0:T(8,128)(2,1)S(1)} %convolution_convert_fusion.24.refs_0_, bf16[512,768]{1,0:T(8,128)(2,1)S(1)} %convolution_convert_fusion.18.refs_1_, bf16[512,768]{1,0:T(8,128)(2,1)S(1)} %convolution_convert_fusion.17.refs_2_, ...), custom_call_target="tpu_custom_call" | custom-call | tf_op jit(solution)/shard_map/pallas_call | solution.py:84
  258.5 1.7 multiply_reduce_fusion
  261.8 8.4 %fusion.6 = bf16[512,3072]{1,0:T(8,128)(2,1)S(1)} fusion(f32[512,3072]{1,0:T(8,128)S(1)} %bitcast.229, bf16[3072,768]{1,0:T(8,128)(2,1)} %bitcast.287, f32[512,768]{1,0:T(8,128)S(1)} %fusion.18), kind=kOutput, calls=%fused_computation.8 | convolution fusion | flops 2447769600 | bytes 15728640 | tf_op jit(solution)/shard_map/dot_general | solution.py:23
  270.3 2.8 multiply_reduce_fusion.1
  273.1 4.6 convolution_convert_fusion.3
  279.8 1.9 convolution_convert_fusion.12
  281.7 25.5 %shard_map.523 = (bf16[512,768]{1,0:T(8,128)(2,1)S(1)}, bf16[512,768]{1,0:T(8,128)(2,1)S(1)}, bf16[512,768]{1,0:T(8,128)(2,1)S(1)}, f32[6,2,1024]{2,1,0:T(2,128)S(1)}) custom-call(bf16[512,768]{1,0:T(8,128)(2,1)S(1)} %convolution_convert_fusion.21.refs_0_, bf16[512,768]{1,0:T(8,128)(2,1)S(1)} %convolution_convert_fusion.20.refs_1_, ...), custom_call_target="tpu_custom_call" | custom-call | tf_op jit(solution)/shard_map/pallas_call | solution.py:84
  307.2 2.0 fusion.98
  309.2 1.9 convolution_convert_fusion.15
  311.1 2.0 fusion.99
  313.1 2.0 convolution_convert_fusion.14
  315.1 5.1 convolution_convert_fusion.2
  320.1 3.6 convolution_convert_fusion.1
  324.4 1.6 convolution_convert_fusion.7
  326.9 1.6 convolution_convert_fusion.8
  328.5 10.0 %shard_map.524 = (bf16[128,768]{1,0:T(8,128)(2,1)S(1)}, bf16[128,768]{1,0:T(8,128)(2,1)S(1)}, bf16[128,768]{1,0:T(8,128)(2,1)S(1)}, f32[6,2,1024]{2,1,0:T(2,128)S(1)}) custom-call(bf16[128,768]{1,0:T(8,128)(2,1)S(1)} %convolution_convert_fusion.27.refs_0_, bf16[128,768]{1,0:T(8,128)(2,1)S(1)} %convolution_convert_fusion.26.refs_1_, ...), custom_call_target="tpu_custom_call" | custom-call | tf_op jit(solution)/shard_map/pallas_call | solution.py:84
  339.1 1.6 convolution_convert_fusion.11
  340.7 1.8 convolution_convert_fusion.6
  342.5 1.9 convolution_convert_fusion.5
  344.4 1.6 convolution_convert_fusion.4
  345.9 3.8 convolution_convert_fusion
  349.7 1.6 convolution_convert_fusion.10
  351.9 1.6 convolution_convert_fusion.9
  353.5 1.3 fusion.31
  356.3 3.2 convolution_convert_fusion.13
  359.5 3.7 fusion.10
  363.2 4.0 concatenate.21
  367.2 1.5 collective-permute-start.8
  368.7 2.5 constant_dynamic-update-slice_fusion.7
  371.2 2.0 dynamic-slice_convert_fusion.1
  377.1 1.1 constant_dynamic-update-slice_fusion.3
  378.8 1.1 constant_dynamic-update-slice_fusion.2
  380.0 1.2 constant_dynamic-update-slice_fusion.1
  381.7 1.1 constant_dynamic-update-slice_fusion.refs_0_
  383.6 1.6 fusion.20
  386.5 2.4 pad_maximum_fusion.refs_0_
  388.9 68.0 %shard_map.525 = (f32[4,24,768]{2,1,0:T(8,128)}, f32[1,24,3072]{2,1,0:T(8,128)}, f32[1,96,768]{2,1,0:T(8,128)}) custom-call(bf16[4,4,2,2,2,24,768]{6,5,4,3,2,1,0:T(8,128)(2,1)} %pad_maximum_fusion.refs_0_, bf16[1,4,2,2,2,24,3072]{6,5,4,3,2,1,0:T(8,128)(2,1)} %bitcast.239, bf16[1,4,2,2,2,96,768]{6,5,4,3,2,1,0:T(8,128)(2,1)} %bitcast.240), custom_call_target="tpu_custom_call" | custom-call | tf_op jit(solution)/shard_map/pallas_call | solution.py:604
  457.0 89.8 %shard_map.526 = (f32[8,24,768]{2,1,0:T(8,128)}, f32[1,24,3072]{2,1,0:T(8,128)}, f32[1,96,768]{2,1,0:T(8,128)}) custom-call(bf16[8,4,2,2,2,24,768]{6,5,4,3,2,1,0:T(8,128)(2,1)} %constant_dynamic-update-slice_fusion.refs_0_, bf16[1,4,2,2,2,24,3072]{6,5,4,3,2,1,0:T(8,128)(2,1)} %bitcast.217, bf16[1,4,2,2,2,96,768]{6,5,4,3,2,1,0:T(8,128)(2,1)} %bitcast.216), custom_call_target="tpu_custom_call" | custom-call | tf_op jit(solution)/shard_map/pallas_call | solution.py:604
  547.0 2.1 collective-permute-start.6
  553.2 4.2 collective-permute-start.11
  559.2 2.3 collective-permute-start.12
  566.7 1.9 fusion.67
  568.8 1.2 pad_maximum_fusion.2
  570.9 1.2 pad_maximum_fusion.1
  (359 shorter events, 53.4 us)
Async XLA Ops:
  0.7 168.5 %copy-start = (f32[32,12]{0,1:T(8,128)S(1)}, f32[32,12]{0,1:T(8,128)}, u32[]{:S(2)}) copy-start(f32[32,12]{0,1:T(8,128)} %param.41) | copy-start | bytes 4612
  0.7 10.7 %copy-start.97 = (s32[2]{0:T(128)S(1)}, s32[2]{0:T(128)}, u32[]{:S(2)}) copy-start(s32[2]{0:T(128)} %param.34) | copy-start | bytes 28
  0.7 12.6 %copy-start.94 = (s32[2,8]{1,0:T(2,128)S(1)}, s32[2,8]{1,0:T(2,128)}, u32[]{:S(2)}) copy-start(s32[2,8]{1,0:T(2,128)} %param.33) | copy-start | bytes 196
  0.7 17.0 %copy-start.80 = (bf16[24,768]{1,0:T(8,128)(2,1)S(1)}, bf16[24,768]{1,0:T(8,128)(2,1)}, u32[]{:S(2)}) copy-start(bf16[24,768]{1,0:T(8,128)(2,1)} %param.47) | copy-start | bytes 110596
  0.7 17.0 %copy-start.88 = (bf16[24]{0:T(256)(128)(2,1)S(1)}, bf16[24]{0:T(256)(128)(2,1)}, u32[]{:S(2)}) copy-start(bf16[24]{0:T(256)(128)(2,1)} %param.36) | copy-start | bytes 148
  0.7 17.0 %copy-start.89 = (bf16[24]{0:T(256)(128)(2,1)S(1)}, bf16[24]{0:T(256)(128)(2,1)}, u32[]{:S(2)}) copy-start(bf16[24]{0:T(256)(128)(2,1)} %param.42) | copy-start | bytes 148
  0.7 17.0 %copy-start.90 = (bf16[24]{0:T(256)(128)(2,1)S(1)}, bf16[24]{0:T(256)(128)(2,1)}, u32[]{:S(2)}) copy-start(bf16[24]{0:T(256)(128)(2,1)} %param.45) | copy-start | bytes 148
  0.8 17.0 %copy-start.91 = (bf16[24]{0:T(256)(128)(2,1)S(1)}, bf16[24]{0:T(256)(128)(2,1)}, u32[]{:S(2)}) copy-start(bf16[24]{0:T(256)(128)(2,1)} %param.46) | copy-start | bytes 148
  0.8 17.0 %copy-start.92 = (bf16[24]{0:T(256)(128)(2,1)S(1)}, bf16[24]{0:T(256)(128)(2,1)}, u32[]{:S(2)}) copy-start(bf16[24]{0:T(256)(128)(2,1)} %param.52) | copy-start | bytes 148
  0.8 17.0 %copy-start.93 = (bf16[24]{0:T(256)(128)(2,1)S(1)}, bf16[24]{0:T(256)(128)(2,1)}, u32[]{:S(2)}) copy-start(bf16[24]{0:T(256)(128)(2,1)} %param.57) | copy-start | bytes 148
  0.8 17.6 %copy-start.81 = (bf16[24,768]{1,0:T(8,128)(2,1)S(1)}, bf16[24,768]{1,0:T(8,128)(2,1)}, u32[]{:S(2)}) copy-start(bf16[24,768]{1,0:T(8,128)(2,1)} %param.48) | copy-start | bytes 110596
  0.8 17.6 %copy-start.82 = (bf16[24,768]{1,0:T(8,128)(2,1)S(1)}, bf16[24,768]{1,0:T(8,128)(2,1)}, u32[]{:S(2)}) copy-start(bf16[24,768]{1,0:T(8,128)(2,1)} %param.49) | copy-start | bytes 110596
  0.8 17.7 %copy-start.83 = (bf16[24,768]{1,0:T(8,128)(2,1)S(1)}, bf16[24,768]{1,0:T(8,128)(2,1)}, u32[]{:S(2)}) copy-start(bf16[24,768]{1,0:T(8,128)(2,1)} %param.50) | copy-start | bytes 110596
  0.8 17.7 %copy-start.84 = (bf16[24,768]{1,0:T(8,128)(2,1)S(1)}, bf16[24,768]{1,0:T(8,128)(2,1)}, u32[]{:S(2)}) copy-start(bf16[24,768]{1,0:T(8,128)(2,1)} %param.53) | copy-start | bytes 110596
  0.8 17.7 %copy-start.85 = (bf16[24,768]{1,0:T(8,128)(2,1)S(1)}, bf16[24,768]{1,0:T(8,128)(2,1)}, u32[]{:S(2)}) copy-start(bf16[24,768]{1,0:T(8,128)(2,1)} %param.54) | copy-start | bytes 110596
  0.8 17.7 %copy-start.86 = (bf16[24,768]{1,0:T(8,128)(2,1)S(1)}, bf16[24,768]{1,0:T(8,128)(2,1)}, u32[]{:S(2)}) copy-start(bf16[24,768]{1,0:T(8,128)(2,1)} %param.55) | copy-start | bytes 110596
  0.8 17.7 %copy-start.87 = (bf16[24,768]{1,0:T(8,128)(2,1)S(1)}, bf16[24,768]{1,0:T(8,128)(2,1)}, u32[]{:S(2)}) copy-start(bf16[24,768]{1,0:T(8,128)(2,1)} %param.56) | copy-start | bytes 110596
  0.9 17.7 %copy-start.79 = (bf16[24,768]{1,0:T(8,128)(2,1)S(1)}, bf16[24,768]{1,0:T(8,128)(2,1)}, u32[]{:S(2)}) copy-start(bf16[24,768]{1,0:T(8,128)(2,1)} %param.37) | copy-start | bytes 110596
  0.9 17.7 %copy-start.78 = (bf16[24,768]{1,0:T(8,128)(2,1)S(1)}, bf16[24,768]{1,0:T(8,128)(2,1)}, u32[]{:S(2)}) copy-start(bf16[24,768]{1,0:T(8,128)(2,1)} %param.38) | copy-start | bytes 110596
  0.9 17.7 %copy-start.77 = (bf16[24,768]{1,0:T(8,128)(2,1)S(1)}, bf16[24,768]{1,0:T(8,128)(2,1)}, u32[]{:S(2)}) copy-start(bf16[24,768]{1,0:T(8,128)(2,1)} %param.39) | copy-start | bytes 110596
  0.9 17.7 %copy-start.76 = (bf16[24,768]{1,0:T(8,128)(2,1)S(1)}, bf16[24,768]{1,0:T(8,128)(2,1)}, u32[]{:S(2)}) copy-start(bf16[24,768]{1,0:T(8,128)(2,1)} %param.40) | copy-start | bytes 110596
  2.8 186.5 %collective-permute-start = (bf16[256,768]{1,0:T(8,128)(2,1)}, bf16[256,768]{1,0:T(8,128)(2,1)S(1)}, u32[]{:S(2)}, u32[]{:S(2)}) collective-permute-start(bf16[256,768]{1,0:T(8,128)(2,1)} %dynamic-slice_bitcast_fusion.1), channel_id=1, source_target_pairs={{0,1},{1,0},{2,3},{3,2},{4,5},{5,4},{6,7},{7,6},{8,9},{9,8},{10,11... | collective-permute-start | bytes 1179656 | tf_op jit(solution)/shard_map/ppermute | solution.py:637
  6.7 171.5 %collective-permute-start.2 = (bf16[64,768]{1,0:T(8,128)(2,1)S(1)}, bf16[64,768]{1,0:T(8,128)(2,1)}, u32[]{:S(2)}, u32[]{:S(2)}) collective-permute-start(bf16[64,768]{1,0:T(8,128)(2,1)S(1)} %dynamic-slice_bitcast_fusion.3), channel_id=1, source_target_pairs={{0,1},{1,0},{2,3},{3,2},{4,5},{5,4},{6,7},{7,6},{8,9},{9,8},{10,11... | collective-permute-start | bytes 294920 | tf_op jit(solution)/shard_map/ppermute | solution.py:637
  7.6 180.3 %collective-permute-start.5 = (bf16[64,768]{1,0:T(8,128)(2,1)S(1)}, bf16[64,768]{1,0:T(8,128)(2,1)}, u32[]{:S(2)}, u32[]{:S(2)}) collective-permute-start(bf16[64,768]{1,0:T(8,128)(2,1)S(1)} %dynamic-slice_bitcast_fusion.2), channel_id=1, source_target_pairs={{0,1},{1,0},{2,3},{3,2},{4,5},{5,4},{6,7},{7,6},{8,9},{9,8},{10,11... | collective-permute-start | bytes 294920 | tf_op jit(solution)/shard_map/ppermute | solution.py:637
  11.4 248.9 %collective-permute-start.4 = (bf16[256,768]{1,0:T(8,128)(2,1)}, bf16[256,768]{1,0:T(8,128)(2,1)}, u32[]{:S(2)}, u32[]{:S(2)}) collective-permute-start(bf16[256,768]{1,0:T(8,128)(2,1)} %dynamic-slice_bitcast_fusion), channel_id=1, source_target_pairs={{0,1},{1,0},{2,3},{3,2},{4,5},{5,4},{6,7},{7,6},{8,9},{9,8},{10,11... | collective-permute-start | bytes 1179656 | tf_op jit(solution)/shard_map/ppermute | solution.py:637
  169.9 6.8 %copy-start.95 = (f32[32,12]{0,1:T(8,128)S(1)}, f32[32,12]{0,1:T(8,128)}, u32[]{:S(2)}) copy-start(f32[32,12]{0,1:T(8,128)} %param.51) | copy-start | bytes 4612
  176.6 10.8 %copy-start.6 = (bf16[1,4,2,2,2,24,768]{6,5,4,3,2,1,0:T(8,128)(2,1)}, bf16[1,4,2,2,2,24,768]{6,5,4,3,2,1,0:T(8,128)(2,1)S(1)}, u32[]{:S(2)}) copy-start(bf16[1,4,2,2,2,24,768]{6,5,4,3,2,1,0:T(8,128)(2,1)S(1)} %get-tuple-element.157) | copy-start | bytes 3538948
  176.6 12.3 %copy-start.8 = (bf16[1,4,2,2,2,24,768]{6,5,4,3,2,1,0:T(8,128)(2,1)}, bf16[1,4,2,2,2,24,768]{6,5,4,3,2,1,0:T(8,128)(2,1)S(1)}, u32[]{:S(2)}) copy-start(bf16[1,4,2,2,2,24,768]{6,5,4,3,2,1,0:T(8,128)(2,1)S(1)} %get-tuple-element.156) | copy-start | bytes 3538948
  181.8 6.1 %copy-start.75 = (bf16[2,64,768]{2,1,0:T(8,128)(2,1)S(1)}, bf16[2,64,768]{2,1,0:T(8,128)(2,1)}, u32[]{:S(2)}) copy-start(bf16[2,64,768]{2,1,0:T(8,128)(2,1)} %param.61) | copy-start | bytes 589828
  189.4 26.2 %copy-start.14 = (bf16[256,768]{1,0:T(8,128)(2,1)}, bf16[256,768]{1,0:T(8,128)(2,1)S(1)}, u32[]{:S(2)}) copy-start(bf16[256,768]{1,0:T(8,128)(2,1)S(1)} %get-tuple-element.172) | copy-start | bytes 1179652
  189.4 26.2 %copy-start.17 = (bf16[256,768]{1,0:T(8,128)(2,1)}, bf16[256,768]{1,0:T(8,128)(2,1)S(1)}, u32[]{:S(2)}) copy-start(bf16[256,768]{1,0:T(8,128)(2,1)S(1)} %get-tuple-element.173) | copy-start | bytes 1179652
  194.2 21.3 %copy-start.51 = (bf16[1,4,2,2,2,24,768]{6,5,4,3,2,1,0:T(8,128)(2,1)S(1)}, bf16[1,4,2,2,2,24,768]{6,5,4,3,2,1,0:T(8,128)(2,1)}, u32[]{:S(2)}) copy-start(bf16[1,4,2,2,2,24,768]{6,5,4,3,2,1,0:T(8,128)(2,1)} %get-tuple-element.161) | copy-start | bytes 3538948
  215.6 6.7 %slice-start.8 = ((s8[4718592]{0:T(1024)(128)(4,1)}), s8[4194304]{0:T(1024)(128)(4,1)S(1)}, s32[]{:S(2)}) async-start(s8[4718592]{0:T(1024)(128)(4,1)} %bitcast.288), calls=%async_computation.8 | async-start | bytes 8388608
  226.9 34.4 %copy-start.4 = (f32[512,768]{1,0:T(8,128)}, f32[512,768]{1,0:T(8,128)S(1)}, u32[]{:S(2)}) copy-start(f32[512,768]{1,0:T(8,128)S(1)} %get-tuple-element.152) | copy-start | bytes 4718596
  229.0 8.3 %slice-start = ((s8[4718592]{0:T(1024)(128)(4,1)}), s8[4194304]{0:T(1024)(128)(4,1)S(1)}, s32[]{:S(2)}) async-start(s8[4718592]{0:T(1024)(128)(4,1)} %bitcast.218), calls=%async_computation | async-start | bytes 8388608
  229.8 7.5 %slice-start.1 = ((s8[4718592]{0:T(1024)(128)(4,1)}), s8[524288]{0:T(1024)(128)(4,1)S(1)}, s32[]{:S(2)}) async-start(s8[4718592]{0:T(1024)(128)(4,1)} %bitcast.218), calls=%async_computation.1 | async-start | bytes 1048576
  230.6 6.2 %copy-start.10 = (bf16[1,4,2,2,2,24,768]{6,5,4,3,2,1,0:T(8,128)(2,1)S(1)}, bf16[1,4,2,2,2,24,768]{6,5,4,3,2,1,0:T(8,128)(2,1)}, u32[]{:S(2)}) copy-start(bf16[1,4,2,2,2,24,768]{6,5,4,3,2,1,0:T(8,128)(2,1)} %get-tuple-element.153) | copy-start | bytes 3538948
  237.2 8.1 %copy-start.11 = (f32[128,768]{1,0:T(8,128)}, f32[128,768]{1,0:T(8,128)S(1)}, u32[]{:S(2)}) copy-start(f32[128,768]{1,0:T(8,128)S(1)} %get-tuple-element.218) | copy-start | bytes 1179652
  237.3 8.1 %slice-start.10 = ((s8[4718592]{0:T(1024)(128)(4,1)}), s8[4194304]{0:T(1024)(128)(4,1)S(1)}, s32[]{:S(2)}) async-start(s8[4718592]{0:T(1024)(128)(4,1)} %bitcast.292), calls=%async_computation.10 | async-start | bytes 8388608
  238.1 7.3 %copy-start.2 = (f32[128,3072]{1,0:T(8,128)}, f32[128,3072]{1,0:T(8,128)S(1)}, u32[]{:S(2)}) copy-start(f32[128,3072]{1,0:T(8,128)S(1)} %fusion.75) | copy-start | bytes 4718596
  238.2 7.3 %slice-start.11 = ((s8[4718592]{0:T(1024)(128)(4,1)}), s8[524288]{0:T(1024)(128)(4,1)S(1)}, s32[]{:S(2)}) async-start(s8[4718592]{0:T(1024)(128)(4,1)} %bitcast.292), calls=%async_computation.11 | async-start | bytes 1048576
  247.9 9.8 %copy-start.41 = (f32[128,768]{1,0:T(8,128)}, f32[128,768]{1,0:T(8,128)S(1)}, u32[]{:S(2)}) copy-start(f32[128,768]{1,0:T(8,128)S(1)} %get-tuple-element.186) | copy-start | bytes 1179652
  247.9 9.8 %copy-start.56 = (bf16[1,4,2,2,2,24,768]{6,5,4,3,2,1,0:T(8,128)(2,1)S(1)}, bf16[1,4,2,2,2,24,768]{6,5,4,3,2,1,0:T(8,128)(2,1)}, u32[]{:S(2)}) copy-start(bf16[1,4,2,2,2,24,768]{6,5,4,3,2,1,0:T(8,128)(2,1)} %get-tuple-element.155) | copy-start | bytes 3538948
  248.5 10.1 %copy-start.54 = (bf16[1,4,2,2,2,24,768]{6,5,4,3,2,1,0:T(8,128)(2,1)S(1)}, bf16[1,4,2,2,2,24,768]{6,5,4,3,2,1,0:T(8,128)(2,1)}, u32[]{:S(2)}) copy-start(bf16[1,4,2,2,2,24,768]{6,5,4,3,2,1,0:T(8,128)(2,1)} %get-tuple-element.154) | copy-start | bytes 3538948
  261.3 8.9 %slice-start.6 = ((s8[4718592]{0:T(1024)(128)(4,1)}), s8[4194304]{0:T(1024)(128)(4,1)S(1)}, s32[]{:S(2)}) async-start(s8[4718592]{0:T(1024)(128)(4,1)} %bitcast.250), calls=%async_computation.6 | async-start | bytes 8388608
  261.8 15.9 %copy-start.22 = (f32[512,768]{1,0:T(8,128)}, f32[512,768]{1,0:T(8,128)S(1)}, u32[]{:S(2)}) copy-start(f32[512,768]{1,0:T(8,128)S(1)} %fusion.18) | copy-start | bytes 4718596
  261.8 8.5 %copy-start.25 = (f32[512,768]{1,0:T(8,128)S(1)}, f32[512,768]{1,0:T(8,128)}, u32[]{:S(2)}) copy-start(f32[512,768]{1,0:T(8,128)} %copy-done.24) | copy-start | bytes 4718596
  261.8 8.5 %slice-start.7 = ((s8[4718592]{0:T(1024)(128)(4,1)}), s8[524288]{0:T(1024)(128)(4,1)S(1)}, s32[]{:S(2)}) async-start(s8[4718592]{0:T(1024)(128)(4,1)} %bitcast.250), calls=%async_computation.7 | async-start | bytes 1048576
  281.7 25.5 %copy-start.50 = (bf16[1,4,2,2,2,24,768]{6,5,4,3,2,1,0:T(8,128)(2,1)S(1)}, bf16[1,4,2,2,2,24,768]{6,5,4,3,2,1,0:T(8,128)(2,1)}, u32[]{:S(2)}) copy-start(bf16[1,4,2,2,2,24,768]{6,5,4,3,2,1,0:T(8,128)(2,1)} %get-tuple-element.164) | copy-start | bytes 3538948
  309.2 5.9 %slice-start.4 = ((s8[6291456]{0:T(1024)(128)(4,1)}), s8[2097152]{0:T(1024)(128)(4,1)S(1)}, s32[]{:S(2)}) async-start(s8[6291456]{0:T(1024)(128)(4,1)} %bitcast.230), calls=%async_computation.4 | async-start | bytes 4194304
  326.9 11.6 %copy-start.33 = (bf16[1,4,2,2,2,24,768]{6,5,4,3,2,1,0:T(8,128)(2,1)S(1)}, bf16[1,4,2,2,2,24,768]{6,5,4,3,2,1,0:T(8,128)(2,1)}, u32[]{:S(2)}) copy-start(bf16[1,4,2,2,2,24,768]{6,5,4,3,2,1,0:T(8,128)(2,1)} %get-tuple-element.160) | copy-start | bytes 3538948
  367.2 179.7 %collective-permute-start.8 = (f32[5382]{0:T(1024)S(1)}, f32[5382]{0:T(1024)S(1)}, u32[]{:S(2)}, u32[]{:S(2)}) collective-permute-start(f32[5382]{0:T(1024)S(1)} %concatenate.21), channel_id=1, source_target_pairs={{0,1},{1,0},{2,3},{3,2},{4,5},{5,4},{6,7},{7,6},{8,9},{9,8},{10,11... | collective-permute-start | bytes 64592 | tf_op jit(solution)/shard_map/ppermute | solution.py:625
  456.9 90.0 %copy-start.27 = (f32[512,768]{1,0:T(8,128)S(1)}, f32[512,768]{1,0:T(8,128)}, u32[]{:S(2)}) copy-start(f32[512,768]{1,0:T(8,128)} %fusion.20) | copy-start | bytes 4718596
  456.9 95.3 %copy-start.67 = (bf16[256,768]{1,0:T(8,128)(2,1)S(1)}, bf16[256,768]{1,0:T(8,128)(2,1)}, u32[]{:S(2)}) copy-start(bf16[256,768]{1,0:T(8,128)(2,1)} %dynamic-slice_convert_fusion.1) | copy-start | bytes 1179652
  457.0 100.4 %copy-start.69 = (f32[4,24,768]{2,1,0:T(8,128)S(1)}, f32[4,24,768]{2,1,0:T(8,128)}, u32[]{:S(2)}) copy-start(f32[4,24,768]{2,1,0:T(8,128)} %get-tuple-element.71) | copy-start | bytes 884740
  546.8 10.6 %copy-start.66 = (f32[8,24,768]{2,1,0:T(8,128)S(1)}, f32[8,24,768]{2,1,0:T(8,128)}, u32[]{:S(2)}) copy-start(f32[8,24,768]{2,1,0:T(8,128)} %get-tuple-element.74) | copy-start | bytes 1769476
  546.8 14.7 %collective-permute-start.7 = (bf16[64,768]{1,0:T(8,128)(2,1)S(1)}, bf16[64,768]{1,0:T(8,128)(2,1)S(1)}, u32[]{:S(2)}, u32[]{:S(2)}) collective-permute-start(bf16[64,768]{1,0:T(8,128)(2,1)S(1)} %dynamic-slice_convert_fusion.2), channel_id=1, source_target_pairs={{0,1},{1,0},{2,3},{3,2},{4,5},{5,4},{6,7},{7,6},{8,9},{9,8},{10,11... | collective-permute-start | bytes 294920 | tf_op jit(solution)/shard_map/ppermute | solution.py:650
  546.9 2.2 collective-permute-start.9
  547.0 21.6 %collective-permute-start.6 = (bf16[256,768]{1,0:T(8,128)(2,1)S(1)}, bf16[256,768]{1,0:T(8,128)(2,1)S(1)}, u32[]{:S(2)}, u32[]{:S(2)}) collective-permute-start(bf16[256,768]{1,0:T(8,128)(2,1)S(1)} %dynamic-slice_convert_fusion), channel_id=1, source_target_pairs={{0,1},{1,0},{2,3},{3,2},{4,5},{5,4},{6,7},{7,6},{8,9},{9,8},{10,11... | collective-permute-start | bytes 1179656 | tf_op jit(solution)/shard_map/ppermute | solution.py:650
  549.1 4.1 collective-permute-start.10
  551.1 12.0 %collective-permute-start.3 = (bf16[64,768]{1,0:T(8,128)(2,1)S(1)}, bf16[64,768]{1,0:T(8,128)(2,1)S(1)}, u32[]{:S(2)}, u32[]{:S(2)}) collective-permute-start(bf16[64,768]{1,0:T(8,128)(2,1)S(1)} %dynamic-slice_convert_fusion.3), channel_id=1, source_target_pairs={{0,1},{1,0},{2,3},{3,2},{4,5},{5,4},{6,7},{7,6},{8,9},{9,8},{10,11... | collective-permute-start | bytes 294920 | tf_op jit(solution)/shard_map/ppermute | solution.py:650
  552.2 18.2 %collective-permute-start.1 = (bf16[256,768]{1,0:T(8,128)(2,1)S(1)}, bf16[256,768]{1,0:T(8,128)(2,1)S(1)}, u32[]{:S(2)}, u32[]{:S(2)}) collective-permute-start(bf16[256,768]{1,0:T(8,128)(2,1)S(1)} %copy-done.67), channel_id=1, source_target_pairs={{0,1},{1,0},{2,3},{3,2},{4,5},{5,4},{6,7},{7,6},{8,9},{9,8},{10,11... | collective-permute-start | bytes 1179656 | tf_op jit(solution)/shard_map/ppermute | solution.py:650
  553.2 6.0 %collective-permute-start.11 = (f32[5382]{0:T(1024)S(1)}, f32[5382]{0:T(1024)S(1)}, u32[]{:S(2)}, u32[]{:S(2)}) collective-permute-start(f32[5382]{0:T(1024)S(1)} %add.253), channel_id=1, source_target_pairs={{0,8},{1,9},{2,10},{3,11},{4,12},{5,13},{6,14},{7,15},{8,0},{9,1},... | collective-permute-start | bytes 64592 | tf_op jit(solution)/shard_map/ppermute | solution.py:625
  559.2 4.7 collective-permute-start.12
  (59 other events, 154.3 us)
